TPU v7x, 32 devices: a whole 2x2x4 slice. The times are simulated.
32 devices in a mesh: grp: 16 (over z, y, core), mdl: 2 (over x).
Axes of the slice: x: 2, y: 2, z: 4, core: 2. Of those that a mesh axis runs over, the one named last changes fastest.
Arguments:
- model: float32 [4096, 2, 128], P(None, 'mdl'), may hold values from -1 to 1.5
- source: float32 [64, 3, 8, 4096], P(('grp', 'mdl')), may hold values from -6 to 6
- observed: float32 [64, 3, 8, 4096], P(('grp', 'mdl')), may hold values from -6 to 6
- owner_ids: int32 [64, 8, 1], P(('grp', 'mdl')), may hold values from 0 to 1; in each aligned block of 16 rows (0 to 15, 16 to 31, ..., all dimensions but the last counted through in order) at most 16 rows name the same one
- offsets: int32 [64, 8], P(('grp', 'mdl')), may hold values from 0 to 4064
- lengths: int32 [64, 8], P(('grp', 'mdl')), may hold values from 1 to 32, 192 in all within a row
Outputs:
- gradient: float32 [4096, 2, 128], P('grp', 'mdl')
Inputs may be any that keep to these rules, and one draw needn't show every extreme that they name: `owner_ids`: among the layers of the soundings of one device (aligned blocks of 16 layers), no owner is named by more than 16 layers; in some blocks one owner is named by exactly 16. A layer covers rows offsets to offsets + lengths - 1 of its owner's block. The first lengths rows of a layer lie in the earth, the others in the air; a sounding's 8 lengths sum to 192.
All inputs are finite; a program needn't handle non-finite values.
Results may differ from a plain program's by a relative error of at most 0.0003.
Values sent between devices are 32-bit elements; how exact they have to be, the bound alone decides.
No kernel may reach another device: no remote copies, remote signals or barrier semaphores. Data moves between devices by JAX's collectives and lax.ppermute only.
A program may use at most 64 MiB of HBM per device.

v0:
```python
import jax
import jax.numpy as jnp
from jax import lax
from jax.sharding import PartitionSpec as P

LY = 64
LZ = 8
STEPS_FWD = 4
STEPS_ADJ = 4
LAYER = 4096
TILE = 32


AIR = 0.05
OMEGA = 0.5
BETA = 0.5


def shift_next(field, count):
    filler = jnp.zeros(field.shape[:-1] + (count,), field.dtype)
    return jnp.concatenate([field[..., count:], filler], axis=-1)


def shift_prev(field, count):
    filler = jnp.zeros(field.shape[:-1] + (count,), field.dtype)
    return jnp.concatenate([filler, field[..., :-count]], axis=-1)


def layer_masks(width):
    column = jnp.arange(LAYER, dtype=jnp.int32) % width
    return ((column != width - 1).astype(jnp.float32), (column != 0).astype(jnp.float32))


def forward_diff(field, which, masks):
    if which == 0:
        return shift_next(field, LY) - field
    if which == 1:
        return shift_next(field, 1) * masks[0] - field
    deeper = jnp.concatenate([field[:, 1:], jnp.zeros_like(field[:, :1])], axis=1)
    return deeper - field


def adjoint_diff(field, which, masks):
    if which == 0:
        return shift_prev(field, LY) - field
    if which == 1:
        return shift_prev(field, 1) * masks[1] - field
    upper = jnp.concatenate([jnp.zeros_like(field[:, :1]), field[:, :-1]], axis=1)
    return upper - field


def apply_operator(field, conduct, masks):
    east, north, vertical = (field[:, 0], field[:, 1], field[:, 2])
    curl_x = forward_diff(vertical, 1, masks) - forward_diff(north, 2, masks)
    curl_y = forward_diff(east, 2, masks) - forward_diff(vertical, 0, masks)
    curl_z = forward_diff(north, 0, masks) - forward_diff(east, 1, masks)
    back_x = adjoint_diff(curl_y, 2, masks) - adjoint_diff(curl_z, 1, masks)
    back_y = adjoint_diff(curl_z, 0, masks) - adjoint_diff(curl_x, 2, masks)
    back_z = adjoint_diff(curl_x, 1, masks) - adjoint_diff(curl_y, 0, masks)
    return jnp.stack([back_x, back_y, back_z], axis=1) + conduct[:, None] * field


def relax(right_side, conduct, count, masks):
    state = jnp.zeros_like(right_side)
    scale = OMEGA / (4.0 + conduct[:, None])
    for sweep in range(count):
        state = state + scale * (right_side - apply_operator(state, conduct, masks))
    return state


def sounding_partial(source, observed, conduct, earth, masks):
    efield = relax(source, conduct, STEPS_FWD, masks)
    adjoint_field = relax(efield - observed, conduct, STEPS_ADJ, masks)
    return -conduct * jnp.sum(efield * adjoint_field, axis=1) * earth


def smoothing(values):
    left = jnp.concatenate([values[..., :1], values[..., :-1]], axis=-1)
    right = jnp.concatenate([values[..., 1:], values[..., -1:]], axis=-1)
    return BETA * (2.0 * values - left - right)


def place_slots(owner_flat, owners_count, capacity):
    chosen = (owner_flat[:, None] == jnp.arange(owners_count, dtype=jnp.int32)[None, :]).astype(
        jnp.int32
    )
    before = jnp.cumsum(chosen, axis=0) - chosen
    return owner_flat * capacity + jnp.sum(before * chosen, axis=1)


def settle(block, source, observed, owner_ids, offsets, lengths, owners_count, capacity, masks):
    count = source.shape[0]
    tiles = count * LZ
    within = jnp.arange(TILE, dtype=jnp.int32)
    places = place_slots(owner_ids.reshape(tiles), owners_count, capacity)
    request = (
        jnp.zeros((owners_count * capacity,), jnp.int32).at[places].set(offsets.reshape(tiles))
    )
    request = request.reshape(owners_count, capacity)
    values = jnp.exp(
        block[
            lax.all_to_all(request, "mdl", split_axis=0, concat_axis=0, tiled=True)[..., None]
            + within
        ]
    )
    answer = lax.all_to_all(values, "mdl", split_axis=0, concat_axis=0, tiled=True)
    fetched = answer.reshape(owners_count * capacity, TILE, 128)[places].reshape(count, LZ, LAYER)
    earth = (within[None, :] < lengths.reshape(tiles)[:, None]).astype(jnp.float32)
    earth = jnp.broadcast_to(earth[..., None], (tiles, TILE, 128)).reshape(count, LZ, LAYER)
    conduct = jnp.where(earth > 0.5, fetched, AIR)
    partial_value = sounding_partial(source, observed, conduct, earth, masks)
    outgoing = jnp.zeros((owners_count * capacity, TILE, 128), jnp.float32)
    outgoing = outgoing.at[places].set(partial_value.reshape(tiles, TILE, 128))
    outgoing = outgoing.reshape(owners_count, capacity, TILE, 128)
    arrived, arrived_starts = (
        lax.all_to_all(outgoing, "mdl", split_axis=0, concat_axis=0, tiled=True),
        lax.all_to_all(request, "mdl", split_axis=0, concat_axis=0, tiled=True),
    )
    target_rows = (arrived_starts[..., None] + within).reshape(-1)
    return (
        jnp.zeros((block.shape[0], 128), jnp.float32).at[target_rows].add(arrived.reshape(-1, 128))
    )


def per_device(model, source, observed, owner_ids, offsets, lengths):
    block = model[:, 0, :]
    masks = layer_masks(LY)
    owners_count = lax.axis_size("mdl")
    capacity = max(4, 2 * source.shape[0] * LZ // owners_count)
    block_partial = settle(
        block, source, observed, owner_ids, offsets, lengths, owners_count, capacity, masks
    )
    share = block.shape[0] // lax.axis_size("grp")
    mine = lax.psum_scatter(block_partial, "grp", scatter_dimension=0, tiled=True)
    local_model = lax.dynamic_slice_in_dim(block, lax.axis_index("grp") * share, share, 0)
    return (mine + smoothing(local_model))[:, None, :]


def solution(mesh):
    placed = (
        P(None, "mdl", None),
        P(("grp", "mdl"), None, None, None),
        P(("grp", "mdl"), None, None, None),
        P(("grp", "mdl"), None, None),
        P(("grp", "mdl"), None),
        P(("grp", "mdl"), None),
    )
    return jax.shard_map(
        per_device, mesh=mesh, in_specs=placed, out_specs=P("grp", "mdl", None), check_vma=False
    )
```

profile of v0, /device:TPU:0, one launch (start us, length us, event | category | flops | bytes accessed | tf_op | source)
XLA Modules:
  0.0 141.4 jit_solution(14784463816364143224)
XLA Ops:
  6.5 0.5 broadcast.389
  7.0 1.5 %fusion.35 = (s32[2,8]{1,0:T(2,128)S(1)}, s32[2,8]{1,0:T(2,128)S(1)}) fusion(s32[2,8,1]{1,2,0:T(1,128)} %param.9, s32[]{:T(128)} %broadcast.389), kind=kLoop, calls=%fused_computation.130 | loop fusion | flops 16 | bytes 196 | tf_op args[3]
  8.7 0.2 select_reduce_fusion
  9.0 0.8 reshape.187
  9.7 0.6 scatter_custom_fusion
  10.4 0.6 all_to_all.13
  11.0 4.2 %all-to-all-start = ((s32[2,1,16]{2,1,0:T(1,128)}), s32[2,1,16]{2,1,0:T(1,128)S(1)}, u32[]{:S(2)}, u32[]{:S(2)}) async-start(s32[2,1,16]{2,1,0:T(1,128)} %bitcast.2), calls=%async_computation | async-start | bytes 2048 | tf_op jit(solution)/shard_map/all_to_all | solution.py:117
  15.6 3.3 %all-to-all-done = s32[2,1,16]{2,1,0:T(1,128)S(1)} async-done(((s32[2,1,16]{2,1,0:T(1,128)}), s32[2,1,16]{2,1,0:T(1,128)S(1)}, u32[]{:S(2)}, u32[]{:S(2)}) %all-to-all-start) | async-done | bytes 160 | tf_op jit(solution)/shard_map/all_to_all | solution.py:117
  19.1 2.8 %gather_fusion = f32[1024,128]{1,0:T(8,128)S(1)} fusion(f32[4096,128]{1,0:T(8,128)S(1)} %bitcast.211, s32[1024]{0:T(1024)S(1)} %broadcast_clamp_fusion), kind=kCustom, calls=%fused_computation | custom fusion | bytes 1052672 | tf_op jit(solution)/shard_map/gather | solution.py:101
  21.9 0.9 exp.4
  22.8 4.3 %all-to-all-start.1 = ((f32[2,16,32,128]{3,2,1,0:T(8,128)}), f32[2,16,32,128]{3,2,1,0:T(8,128)}, u32[]{:S(2)}, u32[]{:S(2)}) async-start(f32[2,16,32,128]{3,2,1,0:T(8,128)} %bitcast.251), calls=%async_computation.1 | async-start | bytes 1048576 | tf_op jit(solution)/shard_map/all_to_all | solution.py:106
  27.3 7.2 %all-to-all-done.1 = f32[2,16,32,128]{3,2,1,0:T(8,128)} async-done(((f32[2,16,32,128]{3,2,1,0:T(8,128)}), f32[2,16,32,128]{3,2,1,0:T(8,128)}, u32[]{:S(2)}, u32[]{:S(2)}) %all-to-all-start.1) | async-done | bytes 524320 | tf_op jit(solution)/shard_map/all_to_all | solution.py:106
  34.5 1.6 %gather_fusion.1 = f32[16,32,128]{2,1,0:T(8,128)S(1)} fusion(f32[32,32,128]{2,1,0:T(8,128)} %bitcast.7, s32[1024]{0:T(1024)S(1)} %pad_clamp_fusion), kind=kCustom, calls=%fused_computation.1 | custom fusion | bytes 524352 | tf_op jit(solution)/shard_map/gather | solution.py:107
  36.1 0.7 copy-done.2
  36.8 0.8 broadcast_select_fusion
  37.7 1.0 select_n.116
  39.3 0.1 slice.410
  39.6 0.1 subtract_subtract_fusion.16
  39.7 0.3 subtract_bitcast_fusion.17
  40.1 0.2 fusion.4
  40.5 0.1 slice.418
  40.7 0.1 slice.425
  41.0 0.1 subtract_subtract_fusion.13
  41.1 0.3 subtract_bitcast_fusion.14
  41.5 0.3 copy_add_fusion.2
  42.5 0.2 subtract_subtract_fusion.10
  42.7 0.3 subtract_bitcast_fusion.11
  43.0 0.8 copy-done.4
  43.8 0.3 fusion.36
  44.1 0.1 subtract_multiply_fusion
  44.9 0.1 subtract_subtract_fusion.7
  45.0 0.3 subtract_bitcast_fusion.8
  45.4 0.2 fusion.9
  46.3 0.1 subtract_subtract_fusion.4
  46.4 0.3 subtract_bitcast_fusion.5
  46.8 0.4 fusion.12
  47.8 0.2 subtract_subtract_fusion.1
  48.0 0.3 subtract_bitcast_fusion.2
  48.4 0.3 fusion.14
  48.7 0.6 copy-done.3
  49.3 0.2 fusion.19
  49.5 0.9 broadcast_in_dim.18
  50.4 2.4 %scatter_fusion = f32[32,32,128]{2,1,0:T(8,128)} fusion(f32[32,32,128]{2,1,0:T(8,128)} %broadcast_in_dim.18, s32[16]{0:T(128)S(1)} %fusion.32, f32[16,32,128]{2,1,0:T(8,128)S(1)} %fusion.19), kind=kCustom, calls=%fused_computation.3 | custom fusion | bytes 786496 | tf_op jit(solution)/shard_map/scatter | solution.py:113
  52.8 3.5 %all-to-all-start.2 = ((f32[2,16,32,128]{3,2,1,0:T(8,128)}), f32[2,16,32,128]{3,2,1,0:T(8,128)S(1)}, u32[]{:S(2)}, u32[]{:S(2)}) async-start(f32[2,16,32,128]{3,2,1,0:T(8,128)} %bitcast.44), calls=%async_computation.2 | async-start | bytes 1048576 | tf_op jit(solution)/shard_map/all_to_all | solution.py:116
  56.5 6.3 %all-to-all-done.2 = f32[2,16,32,128]{3,2,1,0:T(8,128)S(1)} async-done(((f32[2,16,32,128]{3,2,1,0:T(8,128)}), f32[2,16,32,128]{3,2,1,0:T(8,128)S(1)}, u32[]{:S(2)}, u32[]{:S(2)}) %all-to-all-start.2) | async-done | bytes 524320 | tf_op jit(solution)/shard_map/all_to_all | solution.py:116
  62.9 7.4 %scatter_custom_fusion.2 = f32[4096,128]{1,0:T(8,128)} fusion(s32[1024]{0:T(1024)S(1)} %bitcast.256, f32[1024,128]{1,0:T(8,128)S(1)} %bitcast.253, f32[]{:T(128)} %constant.18.clone.1), kind=kCustom, calls=%fused_computation.5 | custom fusion | flops 131072 | bytes 2097156 | tf_op jit(solution)/shard_map/scatter-add | solution.py:121
  70.6 62.3 %reduce-scatter.2.cloned.1.call-done = f32[256,128]{1,0:T(8,128)} async-done(((f32[4096,128]{1,0:T(8,128)}), f32[256,128]{1,0:T(8,128)}) %reduce-scatter.2.cloned.1.call-update) | async-done | bytes 131088 | tf_op jit(solution)/shard_map/reduce_scatter | solution.py:134
  132.9 1.7 %fusion.22 = f32[256,128]{1,0:T(8,128)} fusion(f32[256,128]{1,0:T(8,128)} %reduce-scatter.2.cloned.1.call-done, f32[256,127]{1,0:T(8,128)S(1)} %get-tuple-element.66, f32[256,1]{1,0:T(8,128)S(1)} %get-tuple-element.68, f32[256,1]{1,0:T(8,128)S(1)} %get-tuple-element.67, f32[256,127]{1,0:T(8,128)S(1)} %get-tuple-element.65, f32[256,128]{1,0:T(8,128)S(1)} %bitcast.214), kind=kLoop, calls=%fused_computation.97 | loop fusion | flops 229376 | bytes 655360 | tf_op jit(solution)/shard_map/add | solution.py:136
  (81 shorter events, 4.9 us)
Async XLA Ops:
  6.5 12.6 %copy-start = (f32[4096,1,128]{2,1,0:T(1,128)S(1)}, f32[4096,1,128]{2,1,0:T(1,128)}, u32[]{:S(2)}) copy-start(f32[4096,1,128]{2,1,0:T(1,128)} %param.6) | copy-start | bytes 6291460
  11.0 7.9 %all-to-all-start = ((s32[2,1,16]{2,1,0:T(1,128)}), s32[2,1,16]{2,1,0:T(1,128)S(1)}, u32[]{:S(2)}, u32[]{:S(2)}) async-start(s32[2,1,16]{2,1,0:T(1,128)} %bitcast.2), calls=%async_computation | async-start | bytes 2048 | tf_op jit(solution)/shard_map/all_to_all | solution.py:117
  21.9 5.2 %copy-start.5 = (s32[2,8]{1,0:T(2,128)S(1)}, s32[2,8]{1,0:T(2,128)}, u32[]{:S(2)}) copy-start(s32[2,8]{1,0:T(2,128)} %param.11) | copy-start | bytes 196
  22.8 16.0 %copy-start.1 = (f32[2,3,8,4096]{3,2,1,0:T(8,128)S(1)}, f32[2,3,8,4096]{3,2,1,0:T(8,128)}, u32[]{:S(2)}) copy-start(f32[2,3,8,4096]{3,2,1,0:T(8,128)} %param.7) | copy-start | bytes 2359300
  22.8 11.7 %all-to-all-start.1 = ((f32[2,16,32,128]{3,2,1,0:T(8,128)}), f32[2,16,32,128]{3,2,1,0:T(8,128)}, u32[]{:S(2)}, u32[]{:S(2)}) async-start(f32[2,16,32,128]{3,2,1,0:T(8,128)} %bitcast.251), calls=%async_computation.1 | async-start | bytes 1048576 | tf_op jit(solution)/shard_map/all_to_all | solution.py:106
  36.1 0.7 copy-start.2
  42.7 1.1 copy-start.4
  48.4 1.0 copy-start.3
  52.8 10.1 %all-to-all-start.2 = ((f32[2,16,32,128]{3,2,1,0:T(8,128)}), f32[2,16,32,128]{3,2,1,0:T(8,128)S(1)}, u32[]{:S(2)}, u32[]{:S(2)}) async-start(f32[2,16,32,128]{3,2,1,0:T(8,128)} %bitcast.44), calls=%async_computation.2 | async-start | bytes 1048576 | tf_op jit(solution)/shard_map/all_to_all | solution.py:116
  56.3 76.6 %reduce-scatter.2.cloned.1.call-start = ((), (), s32[]{:S(2)}) async-start(), calls=%async_computation.4 | async-start | bytes 2228224 | tf_op jit(solution)/shard_map/reduce_scatter | solution.py:134
Sparse Core Ops, SparseCore 0:
  70.5 62.3 reduce-scatter.1
where the time goes:
time: 142 us; the launch traced here: 141 us
  waiting for transfers between devices  79.2 us (56%)
  local copies, waits for them, and re-layouts  18.8 us (13%)
  other arithmetic  17.3 us (12%)
  between operations  14 us (10%)
  starting transfers between devices  12.1 us (9%)
    reduce_scatter x1, waiting for transfers between devices, per_device(): lax.psum_scatter(block_partial, 'grp', scatter_dimension=0, tiled=True)  62.3 us
    scatter-add x1, other arithmetic, settle(): jnp.zeros((block.shape[0], 128), jnp.float32).at[target_rows]  7.43 us
    all_to_all x1, waiting for transfers between devices, settle(): lax.all_to_all(values, 'mdl', split_axis=0, concat_axis=0, tiled=True)  7.19 us
    all_to_all x1, waiting for transfers between devices, settle(): lax.all_to_all(outgoing, 'mdl', split_axis=0, concat_axis=0, tiled=True)  6.35 us
    all_to_all x1, starting transfers between devices, settle(): lax.all_to_all(values, 'mdl', split_axis=0, concat_axis=0, tiled=True)  4.34 us
    all_to_all x1, starting transfers between devices, settle(): lax.all_to_all(request, 'mdl', split_axis=0, concat_axis=0, tiled=True)  4.23 us
    all_to_all x1, starting transfers between devices, settle(): lax.all_to_all(outgoing, 'mdl', split_axis=0, concat_axis=0, tiled=True)  3.49 us
    all_to_all x1, waiting for transfers between devices, settle(): lax.all_to_all(request, 'mdl', split_axis=0, concat_axis=0, tiled=True)  3.35 us
  transfers between devices with their start and end apart: 4, of which 4 were waited for; matrix products, arithmetic and copies ran while one was open for 1% of the time, Pallas kernels for 0%

commit v1 on v0

--- a/solution.py
+++ b/solution.py
@@ -122,6 +122,33 @@
     )
 
 
+def halve(blocks, bit):
+    held, data = blocks
+    where = held.index(bit)
+    mine = (lax.axis_index("grp") >> bit) & 1
+    keep = lax.dynamic_index_in_dim(data, mine, where, keepdims=False)
+    give = lax.dynamic_index_in_dim(data, 1 - mine, where, keepdims=False)
+    ring = [(i, i ^ (1 << bit)) for i in range(lax.axis_size("grp"))]
+    got = lax.ppermute(give, "grp", ring)
+    return held[:where] + held[where + 1 :], keep + got
+
+
+def scatter_sums(total):
+    groups = lax.axis_size("grp")
+    bits = groups.bit_length() - 1
+    share = total.shape[0] // groups
+    held = tuple(range(bits - 1, -1, -1))
+    blocks = halve((held, total.reshape((2,) * bits + (share, 128))), 0)
+    rest = tuple(range(1, bits))
+    swapped = rest[1:2] + rest[0:1] + rest[2:]
+    half = share // 2
+    low = (blocks[0], blocks[1][..., :half, :])
+    high = (blocks[0], blocks[1][..., half:, :])
+    for first, second in zip(rest, swapped):
+        low, high = halve(low, first), halve(high, second)
+    return jnp.concatenate([low[1], high[1]], axis=0)
+
+
 def per_device(model, source, observed, owner_ids, offsets, lengths):
     block = model[:, 0, :]
     masks = layer_masks(LY)
@@ -131,7 +158,7 @@
         block, source, observed, owner_ids, offsets, lengths, owners_count, capacity, masks
     )
     share = block.shape[0] // lax.axis_size("grp")
-    mine = lax.psum_scatter(block_partial, "grp", scatter_dimension=0, tiled=True)
+    mine = scatter_sums(block_partial)
     local_model = lax.dynamic_slice_in_dim(block, lax.axis_index("grp") * share, share, 0)
     return (mine + smoothing(local_model))[:, None, :]
 

time: 142 us -> 87.8 us (0.62)
  waiting for transfers between devices: 79.2 us -> 28.6 us
  between operations: 14 us -> 0.74 us
  starting transfers between devices: 12.1 us -> 22.1 us
    reduce_scatter x1 -> x0, waiting for transfers between devices: 62.3 us -> none  [per_device(): lax.psum_scatter(block_partial, 'grp', scatter_dimension=0, tiled=True)]
    ppermute x0 -> x7, waiting for transfers between devices: none -> 11.8 us  [halve(): got = lax.ppermute(give, 'grp', ring)]
    ppermute x0 -> x7, starting transfers between devices: none -> 10.8 us  [halve(): got = lax.ppermute(give, 'grp', ring)]
    gather x1, local copies, waits for them, and re-layouts: 2.8 us -> 4.4 us  [settle(): block[lax.all_to_all(request, 'mdl', split_axis=0, concat_axis=0, tiled=T...]
    add x0 -> x7, other arithmetic: none -> 1.46 us  [halve(): return (held[:where] + held[where + 1:], keep + got)]
  transfers between devices with their start and end apart: 4 -> 10, of which waited for: 4 -> 10; matrix products, arithmetic and copies ran while one was open for 1% -> 3% of each run, Pallas kernels for 0% -> 0%
where the time goes in v1:
time: 87.8 us; the launch traced here: 87.3 us
  waiting for transfers between devices  28.6 us (33%)
  starting transfers between devices  22.1 us (25%)
  local copies, waits for them, and re-layouts  18.2 us (21%)
  other arithmetic  17.6 us (20%)
    ppermute x7, waiting for transfers between devices, halve(): got = lax.ppermute(give, 'grp', ring)  11.8 us
    ppermute x7, starting transfers between devices, halve(): got = lax.ppermute(give, 'grp', ring)  10.8 us
    all_to_all x1, waiting for transfers between devices, settle(): lax.all_to_all(values, 'mdl', split_axis=0, concat_axis=0, tiled=True)  7.08 us
    scatter-add x1, other arithmetic, settle(): jnp.zeros((block.shape[0], 128), jnp.float32).at[target_rows]  6.52 us
    all_to_all x1, waiting for transfers between devices, settle(): lax.all_to_all(outgoing, 'mdl', split_axis=0, concat_axis=0, tiled=True)  6.4 us
    gather x1, local copies, waits for them, and re-layouts, settle(): block[lax.all_to_all(request, 'mdl', split_axis=0, concat_axis=0, tiled=T...  4.4 us
    all_to_all x1, starting transfers between devices, settle(): lax.all_to_all(request, 'mdl', split_axis=0, concat_axis=0, tiled=True)  4.23 us
    all_to_all x1, starting transfers between devices, settle(): lax.all_to_all(values, 'mdl', split_axis=0, concat_axis=0, tiled=True)  3.62 us
  transfers between devices with their start and end apart: 10, of which 10 were waited for; matrix products, arithmetic and copies ran while one was open for 3% of the time, Pallas kernels for 0%

profile of v1, /device:TPU:0, one launch (start us, length us, event | category | flops | bytes accessed | tf_op | source)
XLA Modules:
  0.0 87.3 jit_solution(17877187944302963854)
XLA Ops:
  0.0 0.5 broadcast.391
  0.5 1.3 %fusion.33 = (s32[2,8]{1,0:T(2,128)S(1)}, s32[2,8]{1,0:T(2,128)S(1)}) fusion(s32[2,8,1]{1,2,0:T(1,128)} %param.9, s32[]{:T(128)} %broadcast.391), kind=kLoop, calls=%fused_computation.146 | loop fusion | flops 16 | bytes 196 | tf_op args[3]
  2.3 0.8 reshape.197
  3.1 0.6 scatter_custom_fusion
  3.7 0.6 all_to_all.13
  4.4 4.2 %all-to-all-start = ((s32[2,1,16]{2,1,0:T(1,128)}), s32[2,1,16]{2,1,0:T(1,128)S(1)}, u32[]{:S(2)}, u32[]{:S(2)}) async-start(s32[2,1,16]{2,1,0:T(1,128)} %bitcast.2), calls=%async_computation | async-start | bytes 2048 | tf_op jit(solution)/shard_map/all_to_all | solution.py:117
  8.9 3.3 %all-to-all-done = s32[2,1,16]{2,1,0:T(1,128)S(1)} async-done(((s32[2,1,16]{2,1,0:T(1,128)}), s32[2,1,16]{2,1,0:T(1,128)S(1)}, u32[]{:S(2)}, u32[]{:S(2)}) %all-to-all-start) | async-done | bytes 160 | tf_op jit(solution)/shard_map/all_to_all | solution.py:117
  12.4 4.4 %gather_fusion = f32[1024,128]{1,0:T(8,128)S(1)} fusion(f32[4096,128]{1,0:T(8,128)} %bitcast.250, s32[1024]{0:T(1024)S(1)} %broadcast_clamp_fusion), kind=kCustom, calls=%fused_computation | custom fusion | bytes 1052672 | tf_op jit(solution)/shard_map/gather | solution.py:101
  16.9 0.9 exp.4
  17.7 3.6 %all-to-all-start.1 = ((f32[2,16,32,128]{3,2,1,0:T(8,128)}), f32[2,16,32,128]{3,2,1,0:T(8,128)S(1)}, u32[]{:S(2)}, u32[]{:S(2)}) async-start(f32[2,16,32,128]{3,2,1,0:T(8,128)} %bitcast.6), calls=%async_computation.1 | async-start | bytes 1048576 | tf_op jit(solution)/shard_map/all_to_all | solution.py:106
  21.5 7.1 %all-to-all-done.1 = f32[2,16,32,128]{3,2,1,0:T(8,128)S(1)} async-done(((f32[2,16,32,128]{3,2,1,0:T(8,128)}), f32[2,16,32,128]{3,2,1,0:T(8,128)S(1)}, u32[]{:S(2)}, u32[]{:S(2)}) %all-to-all-start.1) | async-done | bytes 524320 | tf_op jit(solution)/shard_map/all_to_all | solution.py:106
  28.6 0.6 gather_fusion.1
  30.4 0.3 subtract_bitcast_fusion.17
  30.8 0.2 fusion.4
  31.9 0.3 subtract_bitcast_fusion.14
  32.2 0.3 copy_add_fusion.2
  33.4 0.3 subtract_bitcast_fusion.11
  33.8 0.8 copy-done.1
  34.6 0.3 fusion.34
  35.8 0.3 subtract_bitcast_fusion.8
  36.2 0.2 fusion.9
  37.3 0.3 subtract_bitcast_fusion.5
  37.6 0.3 fusion.12
  38.9 0.3 subtract_bitcast_fusion.2
  39.2 0.3 fusion.14
  39.6 0.2 fusion.19
  39.8 0.9 broadcast_in_dim.16
  40.6 2.5 %scatter_fusion = f32[32,32,128]{2,1,0:T(8,128)} fusion(f32[32,32,128]{2,1,0:T(8,128)} %broadcast_in_dim.16, s32[16]{0:T(128)S(1)} %fusion.30, f32[16,32,128]{2,1,0:T(8,128)S(1)} %fusion.19), kind=kCustom, calls=%fused_computation.3 | custom fusion | bytes 786496 | tf_op jit(solution)/shard_map/scatter | solution.py:113
  43.1 3.5 %all-to-all-start.2 = ((f32[2,16,32,128]{3,2,1,0:T(8,128)}), f32[2,16,32,128]{3,2,1,0:T(8,128)S(1)}, u32[]{:S(2)}, u32[]{:S(2)}) async-start(f32[2,16,32,128]{3,2,1,0:T(8,128)} %bitcast.44), calls=%async_computation.2 | async-start | bytes 1048576 | tf_op jit(solution)/shard_map/all_to_all | solution.py:116
  46.7 6.4 %all-to-all-done.2 = f32[2,16,32,128]{3,2,1,0:T(8,128)S(1)} async-done(((f32[2,16,32,128]{3,2,1,0:T(8,128)}), f32[2,16,32,128]{3,2,1,0:T(8,128)S(1)}, u32[]{:S(2)}, u32[]{:S(2)}) %all-to-all-start.2) | async-done | bytes 524320 | tf_op jit(solution)/shard_map/all_to_all | solution.py:116
  53.1 6.5 %scatter_custom_fusion.2 = f32[4096,128]{1,0:T(8,128)S(1)} fusion(s32[1024]{0:T(1024)S(1)} %bitcast.301, f32[1024,128]{1,0:T(8,128)S(1)} %bitcast.294, f32[]{:T(128)} %constant.97.clone.1), kind=kCustom, calls=%fused_computation.7 | custom fusion | flops 131072 | bytes 2097156 | tf_op jit(solution)/shard_map/scatter-add | solution.py:121
  59.8 0.9 %dynamic-slice_bitcast_fusion.5 = f32[256,128]{1,0:T(8,128)S(1)} fusion(f32[4096,1,128]{2,0,1:T(8,128)} %bitcast.251, s32[]{:T(128)S(6)} %select_n.161), kind=kLoop, calls=%fused_computation.113 | loop fusion | bytes 262148 | tf_op jit(solution)/shard_map/dynamic_slice | solution.py:162
  60.9 1.8 %collective-permute-done = f32[2,2,2,256,128]{4,3,2,1,0:T(8,128)} collective-permute-done((f32[2,2,2,256,128]{4,3,2,1,0:T(8,128)S(1)}, f32[2,2,2,256,128]{4,3,2,1,0:T(8,128)}, u32[]{:S(2)}, u32[]{:S(2)}) %collective-permute-start) | collective-permute-done | bytes 1048608 | tf_op jit(solution)/shard_map/ppermute | solution.py:132
  62.6 1.3 %bitcast_add_fusion = f32[2,2,2,256,128]{4,3,2,1,0:T(8,128)S(1)} fusion(f32[2,2,2,256,128]{4,3,2,1,0:T(8,128)} %collective-permute-done, f32[2,2,2,2,256,128]{5,4,3,2,1,0:T(8,128)S(1)} %bitcast.254, s32[]{:T(128)S(6)} %select_n.153), kind=kLoop, calls=%fused_computation.5 | loop fusion | flops 262144 | bytes 3145732 | tf_op jit(solution)/shard_map/add | solution.py:133
  64.1 1.8 %collective-permute-start.1 = (f32[2,2,128,128]{3,2,1,0:T(8,128)S(1)}, f32[2,2,128,128]{3,2,1,0:T(8,128)S(1)}, u32[]{:S(2)}, u32[]{:S(2)}) collective-permute-start(f32[2,2,128,128]{3,2,1,0:T(8,128)S(1)} %dynamic-slice_bitcast_fusion.2), channel_id=1, source_target_pairs={{0,4},{2,6},{4,0},{6,2},{8,12},{10,14},{12,8},{14,10},{16,20},{18,... | collective-permute-start | bytes 786440 | tf_op jit(solution)/shard_map/ppermute | solution.py:132
  66.0 1.0 %maximum_subtract_fusion = f32[256,1,128]{2,0,1:T(8,128)S(1)} fusion(f32[256,1,127]{2,0,1:T(8,128)S(1)} %get-tuple-element.68, f32[256,1,1]{2,0,1:T(8,128)S(1)} %get-tuple-element.70, f32[4096,1,128]{2,0,1:T(8,128)} %bitcast.252, s32[]{:T(128)S(6)} %select_n.161), kind=kLoop, calls=%fused_computation.103 | loop fusion | flops 98304 | bytes 393220 | tf_op jit(solution)/shard_map/sub | solution.py:80
  67.1 1.6 %collective-permute-start.4 = (f32[2,2,128,128]{3,2,1,0:T(8,128)S(1)}, f32[2,2,128,128]{3,2,1,0:T(8,128)S(1)}, u32[]{:S(2)}, u32[]{:S(2)}) collective-permute-start(f32[2,2,128,128]{3,2,1,0:T(8,128)S(1)} %dynamic-slice_bitcast_fusion.1), channel_id=1, source_target_pairs={{0,8},{2,10},{4,12},{6,14},{8,0},{10,2},{12,4},{14,6},{16,24},{18,... | collective-permute-start | bytes 786440 | tf_op jit(solution)/shard_map/ppermute | solution.py:132
  68.7 3.8 %collective-permute-done.1 = f32[2,2,128,128]{3,2,1,0:T(8,128)S(1)} collective-permute-done((f32[2,2,128,128]{3,2,1,0:T(8,128)S(1)}, f32[2,2,128,128]{3,2,1,0:T(8,128)S(1)}, u32[]{:S(2)}, u32[]{:S(2)}) %collective-permute-start.1) | collective-permute-done | bytes 262176 | tf_op jit(solution)/shard_map/ppermute | solution.py:132
  72.6 1.9 %collective-permute-start.2 = (f32[2,128,128]{2,1,0:T(8,128)S(1)}, f32[2,128,128]{2,1,0:T(8,128)S(1)}, u32[]{:S(2)}, u32[]{:S(2)}) collective-permute-start(f32[2,128,128]{2,1,0:T(8,128)S(1)} %dynamic-slice_bitcast_fusion.4), channel_id=1, source_target_pairs={{0,8},{2,10},{4,12},{6,14},{8,0},{10,2},{12,4},{14,6},{16,24},{18,... | collective-permute-start | bytes 393224 | tf_op jit(solution)/shard_map/ppermute | solution.py:132
  74.4 1.4 %collective-permute-done.4 = f32[2,2,128,128]{3,2,1,0:T(8,128)S(1)} collective-permute-done((f32[2,2,128,128]{3,2,1,0:T(8,128)S(1)}, f32[2,2,128,128]{3,2,1,0:T(8,128)S(1)}, u32[]{:S(2)}, u32[]{:S(2)}) %collective-permute-start.4) | collective-permute-done | bytes 262176 | tf_op jit(solution)/shard_map/ppermute | solution.py:132
  75.9 0.2 collective-permute-start.5
  76.1 1.9 %collective-permute-done.2 = f32[2,128,128]{2,1,0:T(8,128)S(1)} collective-permute-done((f32[2,128,128]{2,1,0:T(8,128)S(1)}, f32[2,128,128]{2,1,0:T(8,128)S(1)}, u32[]{:S(2)}, u32[]{:S(2)}) %collective-permute-start.2) | collective-permute-done | bytes 131104 | tf_op jit(solution)/shard_map/ppermute | solution.py:132
  78.1 2.7 %collective-permute-start.3 = (f32[128,128]{1,0:T(8,128)S(1)}, f32[128,128]{1,0:T(8,128)S(1)}, u32[]{:S(2)}, u32[]{:S(2)}) collective-permute-start(f32[128,128]{1,0:T(8,128)S(1)} %dynamic-slice_bitcast_fusion.7), channel_id=1, source_target_pairs={{0,16},{2,18},{4,20},{6,22},{8,24},{10,26},{12,28},{14,30},{16,0},... | collective-permute-start | bytes 196616 | tf_op jit(solution)/shard_map/ppermute | solution.py:132
  80.7 0.2 collective-permute-done.5
  81.0 2.5 %collective-permute-start.6 = (f32[128,128]{1,0:T(8,128)S(1)}, f32[128,128]{1,0:T(8,128)S(1)}, u32[]{:S(2)}, u32[]{:S(2)}) collective-permute-start(f32[128,128]{1,0:T(8,128)S(1)} %dynamic-slice_bitcast_fusion.6), channel_id=1, source_target_pairs={{0,16},{2,18},{4,20},{6,22},{8,24},{10,26},{12,28},{14,30},{16,0},... | collective-permute-start | bytes 196616 | tf_op jit(solution)/shard_map/ppermute | solution.py:132
  83.5 0.2 collective-permute-done.3
  83.7 2.5 %collective-permute-done.6 = f32[128,128]{1,0:T(8,128)S(1)} collective-permute-done((f32[128,128]{1,0:T(8,128)S(1)}, f32[128,128]{1,0:T(8,128)S(1)}, u32[]{:S(2)}, u32[]{:S(2)}) %collective-permute-start.6) | collective-permute-done | bytes 65568 | tf_op jit(solution)/shard_map/ppermute | solution.py:132
  86.2 1.1 %maximum_add_fusion.6 = f32[256,1,128]{2,1,0:T(1,128)} fusion(f32[128,1,128]{2,1,0:T(1,128)S(1)} %bitcast.298, f32[128,1,128]{2,1,0:T(1,128)S(1)} %bitcast.297, f32[256,1,128]{2,1,0:T(1,128)S(1)} %bitcast.293, f32[256,1,1]{2,1,0:T(1,128)S(1)} %bitcast.296, f32[256,1,127]{2,1,0:T(1,128)S(1)} %bitcast.295), kind=kLoop, calls=%fused_computation.102 | loop fusion | flops 163840 | bytes 524288 | tf_op jit(solution)/shard_map/add | solution.py:163
  (102 shorter events, 7.3 us)
Async XLA Ops:
  4.4 7.9 %all-to-all-start = ((s32[2,1,16]{2,1,0:T(1,128)}), s32[2,1,16]{2,1,0:T(1,128)S(1)}, u32[]{:S(2)}, u32[]{:S(2)}) async-start(s32[2,1,16]{2,1,0:T(1,128)} %bitcast.2), calls=%async_computation | async-start | bytes 2048 | tf_op jit(solution)/shard_map/all_to_all | solution.py:117
  16.9 4.5 %copy-start.2 = (s32[2,8]{1,0:T(2,128)S(1)}, s32[2,8]{1,0:T(2,128)}, u32[]{:S(2)}) copy-start(s32[2,8]{1,0:T(2,128)} %param.11) | copy-start | bytes 196
  17.7 11.8 %copy-start = (f32[2,3,8,4096]{3,2,1,0:T(8,128)S(1)}, f32[2,3,8,4096]{3,2,1,0:T(8,128)}, u32[]{:S(2)}) copy-start(f32[2,3,8,4096]{3,2,1,0:T(8,128)} %param.7) | copy-start | bytes 2359300
  17.7 10.9 %all-to-all-start.1 = ((f32[2,16,32,128]{3,2,1,0:T(8,128)}), f32[2,16,32,128]{3,2,1,0:T(8,128)S(1)}, u32[]{:S(2)}, u32[]{:S(2)}) async-start(f32[2,16,32,128]{3,2,1,0:T(8,128)} %bitcast.6), calls=%async_computation.1 | async-start | bytes 1048576 | tf_op jit(solution)/shard_map/all_to_all | solution.py:106
  33.4 1.1 %copy-start.1 = (f32[2,3,8,4096]{3,2,1,0:T(8,128)S(1)}, f32[2,3,8,4096]{3,2,1,0:T(8,128)}, u32[]{:S(2)}) copy-start(f32[2,3,8,4096]{3,2,1,0:T(8,128)} %param.8) | copy-start | bytes 2359300
  43.1 10.1 %all-to-all-start.2 = ((f32[2,16,32,128]{3,2,1,0:T(8,128)}), f32[2,16,32,128]{3,2,1,0:T(8,128)S(1)}, u32[]{:S(2)}, u32[]{:S(2)}) async-start(f32[2,16,32,128]{3,2,1,0:T(8,128)} %bitcast.44), calls=%async_computation.2 | async-start | bytes 1048576 | tf_op jit(solution)/shard_map/all_to_all | solution.py:116
  59.8 2.9 %collective-permute-start = (f32[2,2,2,256,128]{4,3,2,1,0:T(8,128)S(1)}, f32[2,2,2,256,128]{4,3,2,1,0:T(8,128)}, u32[]{:S(2)}, u32[]{:S(2)}) collective-permute-start(f32[2,2,2,256,128]{4,3,2,1,0:T(8,128)S(1)} %dynamic-slice_bitcast_fusion), channel_id=1, source_target_pairs={{0,2},{2,0},{4,6},{6,4},{8,10},{10,8},{12,14},{14,12},{16,18},{18,... | collective-permute-start | bytes 3145736 | tf_op jit(solution)/shard_map/ppermute | solution.py:132
  64.1 8.4 %collective-permute-start.1 = (f32[2,2,128,128]{3,2,1,0:T(8,128)S(1)}, f32[2,2,128,128]{3,2,1,0:T(8,128)S(1)}, u32[]{:S(2)}, u32[]{:S(2)}) collective-permute-start(f32[2,2,128,128]{3,2,1,0:T(8,128)S(1)} %dynamic-slice_bitcast_fusion.2), channel_id=1, source_target_pairs={{0,4},{2,6},{4,0},{6,2},{8,12},{10,14},{12,8},{14,10},{16,20},{18,... | collective-permute-start | bytes 786440 | tf_op jit(solution)/shard_map/ppermute | solution.py:132
  67.1 8.8 %collective-permute-start.4 = (f32[2,2,128,128]{3,2,1,0:T(8,128)S(1)}, f32[2,2,128,128]{3,2,1,0:T(8,128)S(1)}, u32[]{:S(2)}, u32[]{:S(2)}) collective-permute-start(f32[2,2,128,128]{3,2,1,0:T(8,128)S(1)} %dynamic-slice_bitcast_fusion.1), channel_id=1, source_target_pairs={{0,8},{2,10},{4,12},{6,14},{8,0},{10,2},{12,4},{14,6},{16,24},{18,... | collective-permute-start | bytes 786440 | tf_op jit(solution)/shard_map/ppermute | solution.py:132
  72.6 5.4 %collective-permute-start.2 = (f32[2,128,128]{2,1,0:T(8,128)S(1)}, f32[2,128,128]{2,1,0:T(8,128)S(1)}, u32[]{:S(2)}, u32[]{:S(2)}) collective-permute-start(f32[2,128,128]{2,1,0:T(8,128)S(1)} %dynamic-slice_bitcast_fusion.4), channel_id=1, source_target_pairs={{0,8},{2,10},{4,12},{6,14},{8,0},{10,2},{12,4},{14,6},{16,24},{18,... | collective-permute-start | bytes 393224 | tf_op jit(solution)/shard_map/ppermute | solution.py:132
  75.9 5.0 %collective-permute-start.5 = (f32[2,128,128]{2,1,0:T(8,128)S(1)}, f32[2,128,128]{2,1,0:T(8,128)S(1)}, u32[]{:S(2)}, u32[]{:S(2)}) collective-permute-start(f32[2,128,128]{2,1,0:T(8,128)S(1)} %dynamic-slice_bitcast_fusion.3), channel_id=1, source_target_pairs={{0,4},{2,6},{4,0},{6,2},{8,12},{10,14},{12,8},{14,10},{16,20},{18,... | collective-permute-start | bytes 393224 | tf_op jit(solution)/shard_map/ppermute | solution.py:132
  78.1 5.6 %collective-permute-start.3 = (f32[128,128]{1,0:T(8,128)S(1)}, f32[128,128]{1,0:T(8,128)S(1)}, u32[]{:S(2)}, u32[]{:S(2)}) collective-permute-start(f32[128,128]{1,0:T(8,128)S(1)} %dynamic-slice_bitcast_fusion.7), channel_id=1, source_target_pairs={{0,16},{2,18},{4,20},{6,22},{8,24},{10,26},{12,28},{14,30},{16,0},... | collective-permute-start | bytes 196616 | tf_op jit(solution)/shard_map/ppermute | solution.py:132
  81.0 5.2 %collective-permute-start.6 = (f32[128,128]{1,0:T(8,128)S(1)}, f32[128,128]{1,0:T(8,128)S(1)}, u32[]{:S(2)}, u32[]{:S(2)}) collective-permute-start(f32[128,128]{1,0:T(8,128)S(1)} %dynamic-slice_bitcast_fusion.6), channel_id=1, source_target_pairs={{0,16},{2,18},{4,20},{6,22},{8,24},{10,26},{12,28},{14,30},{16,0},... | collective-permute-start | bytes 196616 | tf_op jit(solution)/shard_map/ppermute | solution.py:132

commit v2 on v0

v2 whole, which is shorter than its diff:
```python
import functools

import jax
import jax.numpy as jnp
from jax import lax
from jax.experimental import pallas as pl
from jax.experimental.pallas import tpu as pltpu
from jax.sharding import PartitionSpec as P

LY = 64
LZ = 8
STEPS_FWD = 4
STEPS_ADJ = 4
TILE = 32
LANES = 128
SUB = 8
PARTS = TILE // SUB

AIR = 0.05
OMEGA = 0.5
BETA = 0.5

VMEM = pl.BlockSpec(memory_space=pltpu.VMEM)
SMEM = pl.BlockSpec(memory_space=pltpu.SMEM)


def place_slots(owner_flat, owners_count, capacity):
    chosen = (owner_flat[:, None] == jnp.arange(owners_count, dtype=jnp.int32)[None, :]).astype(
        jnp.int32
    )
    before = jnp.cumsum(chosen, axis=0) - chosen
    return owner_flat * capacity + jnp.sum(before * chosen, axis=1)


def swap_over(axis, mask):
    ring = [(i, i ^ mask) for i in range(lax.axis_size(axis))]
    return lambda value: lax.ppermute(value, axis, ring)


def gather_body(index_ref, block_ref, out_ref):
    for tile in range(out_ref.shape[0]):
        start = index_ref[0, tile]
        out_ref[tile] = block_ref[pl.ds(start, TILE), :]


def gather_rows(index, block):
    tiles = index.shape[1]
    return pl.pallas_call(
        gather_body,
        out_shape=jax.ShapeDtypeStruct((tiles, TILE, LANES), jnp.float32),
        in_specs=[SMEM, VMEM],
        out_specs=VMEM,
        cost_estimate=pl.CostEstimate(
            flops=0, bytes_accessed=2 * tiles * TILE * LANES * 4, transcendentals=0
        ),
        name="gather_rows",
    )(index, block)


def stencil_body(
    index_ref, lengths_ref, table_ref, answer_ref, source_ref, observed_ref, out_ref,
    field, adjoint, right, scale, decay,
):
    me = lax.axis_index("mdl")
    lane = lax.broadcasted_iota(jnp.int32, (PARTS, SUB, LANES), 2)
    sub = lax.broadcasted_iota(jnp.int32, (1, SUB, LANES), 1)
    row = (
        PARTS * lax.broadcasted_iota(jnp.int32, (PARTS, SUB, LANES), 1)
        + lax.broadcasted_iota(jnp.int32, (PARTS, SUB, LANES), 0)
    )
    low = lane < LY
    not_last = lane % LY != LY - 1
    not_first = lane % LY != 0

    def turn(value, count):
        return pltpu.roll(value, count % LANES, 2)

    def y_next(value):
        return jnp.where(not_last, turn(value, -1), 0.0)

    def y_prev(value):
        return jnp.where(not_first, turn(value, 1), 0.0)

    def x_next(value):
        wrapped = jnp.where(sub != SUB - 1, pltpu.roll(value[:1], SUB - 1, 1), 0.0)
        below = jnp.concatenate([value[1:], wrapped], axis=0)
        return turn(jnp.where(low, below, value), LY)

    def x_prev(value):
        wrapped = jnp.where(sub != 0, pltpu.roll(value[PARTS - 1 :], 1, 1), 0.0)
        above = jnp.concatenate([wrapped, value[: PARTS - 1]], axis=0)
        return turn(jnp.where(low, value, above), LY)

    def rows_of(ref, base, step):
        return jnp.stack(
            [ref[pl.ds(base + step * j, SUB, stride=step * PARTS), :] for j in range(PARTS)]
        )

    def sweep(state):
        east, north, vert = state[0, 0], state[1, 0], state[2, 0]
        zero = jnp.zeros_like(east)
        up_x, up_y = zero, zero
        for z in range(LZ):
            if z + 1 < LZ:
                east_d, north_d, vert_d = state[0, z + 1], state[1, z + 1], state[2, z + 1]
            else:
                east_d, north_d, vert_d = zero, zero, zero
            curl_x = (y_next(vert) - vert) - (north_d - north)
            curl_y = (east_d - east) - (x_next(vert) - vert)
            curl_z = (x_next(north) - north) - (y_next(east) - east)
            back_x = (up_y - curl_y) - (y_prev(curl_z) - curl_z)
            back_y = (x_prev(curl_z) - curl_z) - (up_x - curl_x)
            back_z = (y_prev(curl_x) - curl_x) - (x_prev(curl_y) - curl_y)
            s, d = scale[z], decay[z]
            state[0, z] = d * east + (right[0, z] - s * back_x)
            state[1, z] = d * north + (right[1, z] - s * back_y)
            state[2, z] = d * vert + (right[2, z] - s * back_z)
            up_x, up_y = curl_x, curl_y
            east, north, vert = east_d, north_d, vert_d

    for sounding in range(source_ref.shape[0] // (3 * LZ * TILE)):
        first = sounding * LZ

        def conduct_of(z):
            tile = first + z
            length = lengths_ref[tile]
            raw = rows_of(table_ref, index_ref[0, tile], 1)
            sent = rows_of(answer_ref, tile * TILE, 1)
            mine = jnp.full((PARTS, SUB, LANES), index_ref[1, tile] == me)
            value = jnp.exp(jnp.where(mine, raw, sent))
            earth = row < length
            return jnp.where(earth, value, AIR), earth

        def cells(ref, part, z):
            return rows_of(ref, (sounding * 3 + part) * LZ * TILE + z, LZ)

        for z in range(LZ):
            conduct, _ = conduct_of(z)
            s = OMEGA / (4.0 + conduct)
            scale[z] = s
            decay[z] = 1.0 - s * conduct
            for part in range(3):
                value = s * cells(source_ref, part, z)
                right[part, z] = value
                field[part, z] = value

        @pl.loop(0, STEPS_FWD - 1)
        def _(step):
            sweep(field)

        for z in range(LZ):
            for part in range(3):
                value = scale[z] * (field[part, z] - cells(observed_ref, part, z))
                right[part, z] = value
                adjoint[part, z] = value

        @pl.loop(0, STEPS_ADJ - 1)
        def _(step):
            sweep(adjoint)

        for z in range(LZ):
            conduct, earth = conduct_of(z)
            total = field[0, z] * adjoint[0, z]
            total += field[1, z] * adjoint[1, z]
            total += field[2, z] * adjoint[2, z]
            partial = jnp.where(earth, -conduct * total, 0.0)
            for j in range(PARTS):
                out_ref[pl.ds((first + z) * TILE + j, SUB, stride=PARTS), :] = partial[j]


def by_rows(values):
    count = values.shape[0]
    parts = values.reshape(count, 3, LZ, TILE, LANES)
    return parts.transpose(0, 1, 3, 2, 4).reshape(count * 3 * TILE * LZ, LANES)


def soundings_partial(index, lengths, table, answer, source, observed):
    tiles = index.shape[1]
    count = tiles // LZ
    planes = pltpu.VMEM((3, LZ, PARTS, SUB, LANES), jnp.float32)
    single = pltpu.VMEM((LZ, PARTS, SUB, LANES), jnp.float32)
    out = pl.pallas_call(
        stencil_body,
        out_shape=jax.ShapeDtypeStruct((tiles * TILE, LANES), jnp.float32),
        in_specs=[SMEM, SMEM, VMEM, VMEM, VMEM, VMEM],
        out_specs=VMEM,
        scratch_shapes=[planes, planes, planes, single, single],
        cost_estimate=pl.CostEstimate(
            flops=count * 8 * 60 * LZ * TILE * LANES,
            bytes_accessed=4 * (2 * source.size + 3 * tiles * TILE * LANES),
            transcendentals=2 * tiles * TILE * LANES,
        ),
        name="soundings_partial",
    )(
        index, lengths, table, answer.reshape(tiles * TILE, LANES), by_rows(source),
        by_rows(observed),
    )
    return out.reshape(tiles, TILE, LANES)


def arranged(order):
    if not order:
        return [0]
    rest = arranged(order[1:])
    return [slot | (1 << order[0]) for slot in rest] + rest


def accumulate_body(orders, groups, terms_count, *refs):
    indexes, terms = refs[:terms_count], refs[terms_count : 2 * terms_count]
    model_ref = refs[2 * terms_count]
    outs, total = refs[2 * terms_count + 1 : -1], refs[-1]
    owner, me = lax.axis_index("mdl"), lax.axis_index("grp")
    share = model_ref.shape[0] // groups
    span = share + 2 * TILE
    slots = groups // 2
    half = share // 2
    total[...] = jnp.zeros_like(total)
    local = model_ref[pl.ds(pl.multiple_of(me * share, share), share), :]
    lane = lax.broadcasted_iota(jnp.int32, local.shape, 1)
    left = jnp.where(lane == 0, local, pltpu.roll(local, 1, 1))
    right = jnp.where(lane == LANES - 1, local, pltpu.roll(local, LANES - 1, 1))
    total[TILE : TILE + share, :] = BETA * (2.0 * local - left - right)

    for index_ref, terms_ref in zip(indexes, terms):

        @pl.loop(0, terms_ref.shape[0])
        def _(tile):
            start = index_ref[0, tile]
            first = lax.div(start, share)
            target = first + ((first ^ me) & 1)
            where = start - target * share

            @pl.when((index_ref[1, tile] == owner) & (where > -TILE))
            def _():
                base = ((target >> 1) ^ (me >> 1)) * span + TILE + where
                total[pl.ds(base, TILE), :] += terms_ref[tile]

    for which, order in enumerate(orders):
        for place, slot in enumerate(arranged(order)):
            out = outs[2 * which + (place * 2 >= slots)]
            begin = slot * span + TILE + which * half
            out[place % (slots // 2)] = total[begin : begin + half, :]


def accumulate(indexes, terms, block, orders):
    groups = lax.axis_size("grp")
    share, slots = block.shape[0] // groups, groups // 2
    out = jax.ShapeDtypeStruct((slots // 2, share // 2, LANES), jnp.float32)
    count = len(terms)
    return pl.pallas_call(
        functools.partial(accumulate_body, orders, groups, count),
        out_shape=(out,) * 4,
        in_specs=[SMEM] * count + [VMEM] * (count + 1),
        out_specs=(VMEM,) * 4,
        scratch_shapes=[pltpu.VMEM((slots * (share + 2 * TILE), LANES), jnp.float32)],
        cost_estimate=pl.CostEstimate(
            flops=sum(t.size for t in terms),
            bytes_accessed=4 * sum(t.size for t in terms),
            transcendentals=0,
        ),
        name="accumulate",
    )(*indexes, *terms, block)


def per_device(model, source, observed, owner_ids, offsets, lengths):
    rows, owners, groups = model.shape[0], lax.axis_size("mdl"), lax.axis_size("grp")
    block = model.reshape(rows, LANES)
    tiles = source.shape[0] * LZ
    across, beside = swap_over("mdl", 1), swap_over("grp", 1)
    flat_owner, flat_start = owner_ids.reshape(tiles), offsets.reshape(tiles)
    flat_length = lengths.reshape(tiles)
    index = jnp.stack([flat_start, flat_owner])
    if owners == 2:
        asked = across(index)
        answer = across(gather_rows(asked, block))
        terms = soundings_partial(index, flat_length, block, answer, source, observed)
        others = across(terms)
        index_pair = beside(jnp.stack([index, asked]))
        indexes = [index, asked, index_pair[0], index_pair[1]]
        terms_list = [terms, others, beside(terms), beside(others)]
    else:
        capacity = max(4, 2 * tiles // owners)
        places = place_slots(flat_owner, owners, capacity)
        swap = functools.partial(
            lax.all_to_all, axis_name="mdl", split_axis=0, concat_axis=0, tiled=True
        )
        request = jnp.zeros((owners * capacity,), jnp.int32).at[places].set(flat_start)
        asked = swap(request.reshape(owners, capacity)).reshape(1, owners * capacity)
        mine = jnp.full_like(asked, lax.axis_index("mdl"))
        asked = jnp.concatenate([asked, mine])
        given = gather_rows(asked, block).reshape(owners, capacity, TILE, LANES)
        fetched = swap(given).reshape(owners * capacity * TILE, LANES)
        local = jnp.stack([places * TILE, jnp.full_like(places, lax.axis_index("mdl"))])
        dummy = jnp.zeros((tiles, TILE, LANES), jnp.float32)
        terms = soundings_partial(local, flat_length, fetched, dummy, source, observed)
        outgoing = jnp.zeros((owners * capacity, TILE, LANES), jnp.float32)
        outgoing = outgoing.at[places].set(terms).reshape(owners, capacity, TILE, LANES)
        arrived = swap(outgoing).reshape(owners * capacity, TILE, LANES)
        indexes = [asked, beside(asked)]
        terms_list = [arrived, beside(arrived)]

    bits = tuple(range(groups.bit_length() - 2))
    orders = (bits, bits[1:2] + bits[0:1] + bits[2:])
    low_give, low, high_give, high = accumulate(indexes, terms_list, block, orders)
    for step, (low_bit, high_bit) in enumerate(zip(*orders)):
        got_low = swap_over("grp", 2 << low_bit)(low_give)
        got_high = swap_over("grp", 2 << high_bit)(high_give)
        cut = low.shape[0] // 2
        if cut:
            low_give, low = got_low[:cut] + low[:cut], got_low[cut:] + low[cut:]
            high_give, high = got_high[:cut] + high[:cut], got_high[cut:] + high[cut:]
        else:
            low, high = got_low + low, got_high + high
    return jnp.concatenate([low[0], high[0]], axis=0)[:, None, :]


def solution(mesh):
    placed = (
        P(None, "mdl", None),
        P(("grp", "mdl"), None, None, None),
        P(("grp", "mdl"), None, None, None),
        P(("grp", "mdl"), None, None),
        P(("grp", "mdl"), None),
        P(("grp", "mdl"), None),
    )
    return jax.shard_map(
        per_device, mesh=mesh, in_specs=placed, out_specs=P("grp", "mdl", None), check_vma=False
    )
```

time: 142 us -> 68.4 us (0.48)
  waiting for transfers between devices: 79.2 us -> 20.5 us
  Pallas kernels: 0 us -> 19.2 us
  local copies, waits for them, and re-layouts: 18.8 us -> 4.66 us
  between operations: 14 us -> 0.07 us
  other arithmetic: 17.3 us -> 4.07 us
  starting transfers between devices: 12.1 us -> 19.6 us
    reduce_scatter x1 -> x0, waiting for transfers between devices: 62.3 us -> none  [per_device(): lax.psum_scatter(block_partial, 'grp', scatter_dimension=0, tiled=True)]
    ppermute x0 -> x12, waiting for transfers between devices: none -> 20.5 us  [swap_over(): return lambda value: lax.ppermute(value, axis, ring)]
    ppermute x0 -> x12, starting transfers between devices: none -> 19.6 us  [swap_over(): return lambda value: lax.ppermute(value, axis, ring)]
    pallas_call x0 -> x3, Pallas kernels: none -> 19.2 us  [the longest x1 12.5 us: soundings_partial(): pl.pallas_call(stencil_body, out_shape=jax.ShapeDtypeStruct((tiles * TILE...]
    all_to_all x3 -> x0, waiting for transfers between devices: 16.9 us -> none  [the longest x1 7.19 us: settle(): lax.all_to_all(values, 'mdl', split_axis=0, concat_axis=0, tiled=True)]
    all_to_all x3 -> x0, starting transfers between devices: 12.1 us -> none  [the longest x1 4.34 us: settle(): lax.all_to_all(values, 'mdl', split_axis=0, concat_axis=0, tiled=True)]
    scatter-add x1 -> x0, other arithmetic: 7.43 us -> none  [settle(): jnp.zeros((block.shape[0], 128), jnp.float32).at[target_rows]]
    gather x2 -> x0, local copies, waits for them, and re-layouts: 4.41 us -> none  [the longest x1 2.8 us: settle(): block[lax.all_to_all(request, 'mdl', split_axis=0, concat_axis=0, tiled=T...]
  transfers between devices with their start and end apart: 4 -> 12, of which waited for: 4 -> 8; matrix products, arithmetic and copies ran while one was open for 1% -> 5% of each run, Pallas kernels for 0% -> 0%
where the time goes in v2:
time: 68.4 us; the launch traced here: 68.1 us
  waiting for transfers between devices  20.5 us (30%)
  starting transfers between devices  19.6 us (29%)
  Pallas kernels  19.2 us (28%)
  local copies, waits for them, and re-layouts  4.66 us (7%)
  other arithmetic  4.07 us (6%)
    ppermute x12, waiting for transfers between devices, swap_over(): return lambda value: lax.ppermute(value, axis, ring)  20.5 us
    ppermute x12, starting transfers between devices, swap_over(): return lambda value: lax.ppermute(value, axis, ring)  19.6 us
    pallas_call x1, Pallas kernels, soundings_partial(): pl.pallas_call(stencil_body, out_shape=jax.ShapeDtypeStruct((tiles * TILE...  12.5 us
    pallas_call x1, Pallas kernels, accumulate(): pl.pallas_call(functools.partial(accumulate_body, orders, groups, count),...  4.39 us
    unnamed x17, local copies, waits for them, and re-layouts  2.56 us
    pallas_call x1, Pallas kernels, gather_rows(): pl.pallas_call(gather_body, out_shape=jax.ShapeDtypeStruct((tiles, TILE,...  2.32 us
  transfers between devices with their start and end apart: 12, of which 8 were waited for; matrix products, arithmetic and copies ran while one was open for 5% of the time, Pallas kernels for 0%

profile of v2, /device:TPU:0, one launch (start us, length us, event | category | flops | bytes accessed | tf_op | source)
XLA Modules:
  0.0 68.1 jit_solution(4695301019073431635)
XLA Ops:
  0.0 0.0 copy-start.7
  0.0 0.5 broadcast.3
  0.5 1.3 %reduce.3 = s32[2,8]{1,0:T(2,128)S(1)} reduce(s32[2,8,1]{1,2,0:T(1,128)} %param.9, s32[]{:T(128)} %broadcast.3), dimensions={2}, to_apply=%param.9.reduce_sub_computation.3 | reduce | bytes 132 | tf_op args[3]
  1.9 0.1 stack_reshape.7
  1.9 0.8 %stack_reshape.6 = s32[1,16]{1,0:T(1,128)S(1)} reshape(s32[2,8]{1,0:T(2,128)} %param.10) | data formatting | bytes 128 | tf_op jit(solution)/shard_map/stack;reshape | solution.py:272
  2.7 0.0 copy-start.4
  2.7 3.0 %collective-permute-start = (s32[2,16]{1,0:T(2,128)S(1)}, s32[2,16]{1,0:T(2,128)S(1)}, u32[]{:S(2)}, u32[]{:S(2)}) collective-permute-start(s32[2,16]{1,0:T(2,128)S(1)} %get-tuple-element.20.index_ref.refs_0_), channel_id=1, source_target_pairs={{0,1},{1,0},{2,3},{3,2},{4,5},{5,4},{6,7},{7,6},{8,9},{9,8},{10,11... | collective-permute-start | bytes 392 | tf_op jit(solution)/shard_map/ppermute | solution.py:37
  5.7 1.6 %collective-permute-done.index_ref.refs_1_ = s32[2,16]{1,0:T(2,128)S(1)} collective-permute-done((s32[2,16]{1,0:T(2,128)S(1)}, s32[2,16]{1,0:T(2,128)S(1)}, u32[]{:S(2)}, u32[]{:S(2)}) %collective-permute-start) | collective-permute-done | bytes 160 | tf_op jit(solution)/shard_map/ppermute | solution.py:37
  7.3 0.0 copy-start.5
  7.3 0.6 copy-done.5
  7.9 2.3 %gather_rows.1 = f32[16,32,128]{2,1,0:T(8,128)} custom-call(s32[2,16]{1,0:T(2,128)} %copy-done.5, f32[4096,128]{1,0:T(8,128)} %bitcast.28), custom_call_target="tpu_custom_call" | custom-call | bytes 524288 | tf_op jit(solution)/shard_map/gather_rows/pallas_call | solution.py:48
  10.2 2.0 %collective-permute-start.2 = (f32[16,32,128]{2,1,0:T(8,128)}, f32[16,32,128]{2,1,0:T(8,128)S(1)}, u32[]{:S(2)}, u32[]{:S(2)}) collective-permute-start(f32[16,32,128]{2,1,0:T(8,128)} %gather_rows.1), channel_id=1, source_target_pairs={{0,1},{1,0},{2,3},{3,2},{4,5},{5,4},{6,7},{7,6},{8,9},{9,8},{10,11... | collective-permute-start | bytes 786440 | tf_op jit(solution)/shard_map/ppermute | solution.py:37
  12.2 0.0 copy-done.7
  12.2 0.7 reshape.24.lengths_ref
  12.9 4.7 %collective-permute-done.2 = f32[16,32,128]{2,1,0:T(8,128)S(1)} collective-permute-done((f32[16,32,128]{2,1,0:T(8,128)}, f32[16,32,128]{2,1,0:T(8,128)S(1)}, u32[]{:S(2)}, u32[]{:S(2)}) %collective-permute-start.2) | collective-permute-done | bytes 262176 | tf_op jit(solution)/shard_map/ppermute | solution.py:37
  17.6 0.0 copy-done.4
  17.6 0.7 %copy-done.3 = f32[16,32,128]{2,1,0:T(8,128)} copy-done((f32[16,32,128]{2,1,0:T(8,128)}, f32[16,32,128]{2,1,0:T(8,128)S(1)}, u32[]{:S(2)}) %copy-start.3) | copy-done | bytes 262168
  18.3 12.5 %soundings_partial.1 = f32[512,128]{1,0:T(8,128)} custom-call(s32[2,16]{1,0:T(2,128)} %copy-done.4, s32[16]{0:T(128)} %reshape.24.lengths_ref, f32[4096,128]{1,0:T(8,128)} %bitcast.29, f32[512,128]{1,0:T(8,128)} %bitcast.36, f32[1536,128]{1,0:T(8,128)} %bitcast.34, f32[1536,128]{1,0:T(8,128)} %bitcast.35), custom_call_target="tpu_custom_call" | custom-call | flops 31457280 | bytes 2359296 | tf_op jit(solution)/shard_map/soundings_partial/pallas_call | solution.py:182
  30.8 1.7 %collective-permute-start.3 = (f32[16,32,128]{2,1,0:T(8,128)}, f32[16,32,128]{2,1,0:T(8,128)S(1)}, u32[]{:S(2)}, u32[]{:S(2)}) collective-permute-start(f32[16,32,128]{2,1,0:T(8,128)} %bitcast.31), channel_id=1, source_target_pairs={{0,1},{1,0},{2,3},{3,2},{4,5},{5,4},{6,7},{7,6},{8,9},{9,8},{10,11... | collective-permute-start | bytes 786440 | tf_op jit(solution)/shard_map/ppermute | solution.py:37
  32.5 0.0 collective-permute-start.4
  32.5 4.8 %collective-permute-done.3.refs_5_ = f32[16,32,128]{2,1,0:T(8,128)S(1)} collective-permute-done((f32[16,32,128]{2,1,0:T(8,128)}, f32[16,32,128]{2,1,0:T(8,128)S(1)}, u32[]{:S(2)}, u32[]{:S(2)}) %collective-permute-start.3) | collective-permute-done | bytes 262176 | tf_op jit(solution)/shard_map/ppermute | solution.py:37
  37.4 0.0 collective-permute-start.5
  37.4 0.0 copy-done.6
  37.4 0.5 collective-permute-start.1
  37.9 1.0 %collective-permute-done.1 = s32[2,2,16]{2,1,0:T(2,128)S(1)} collective-permute-done((s32[2,2,16]{2,1,0:T(2,128)S(1)}, s32[2,2,16]{2,1,0:T(2,128)S(1)}, u32[]{:S(2)}, u32[]{:S(2)}) %collective-permute-start.1) | collective-permute-done | bytes 288 | tf_op jit(solution)/shard_map/ppermute | solution.py:37
  38.9 0.6 slice_bitcast_fusion
  39.5 0.0 collective-permute-done.4.refs_6_
  39.5 0.0 collective-permute-done.5.refs_7_
  39.5 0.0 copy-start.2
  39.5 0.0 copy-done
  39.5 0.7 copy-done.1
  40.2 0.1 copy-done.2
  40.3 4.4 %accumulate.1 = (f32[4,128,128]{2,1,0:T(8,128)}, f32[4,128,128]{2,1,0:T(8,128)}, f32[4,128,128]{2,1,0:T(8,128)}, f32[4,128,128]{2,1,0:T(8,128)}) custom-call(s32[2,16]{1,0:T(2,128)} %copy-done.4, s32[2,16]{1,0:T(2,128)} %copy-done.5, s32[2,16]{1,0:T(2,128)} %get-tuple-element.18.refs_2_, s32[2,16]{1,0:T(2,128)} %get-tuple-element.17.refs_3_, ...), custom_call_target="tpu_custom_call" | custom-call | flops 262144 | bytes 1048576 | tf_op jit(solution)/shard_map/accumulate/pallas_call | solution.py:250
  44.7 1.8 %collective-permute-start.6 = (f32[4,128,128]{2,1,0:T(8,128)}, f32[4,128,128]{2,1,0:T(8,128)S(1)}, u32[]{:S(2)}, u32[]{:S(2)}) collective-permute-start(f32[4,128,128]{2,1,0:T(8,128)} %get-tuple-element.9), channel_id=1, source_target_pairs={{0,4},{2,6},{4,0},{6,2},{8,12},{10,14},{12,8},{14,10},{16,20},{18,... | collective-permute-start | bytes 786440 | tf_op jit(solution)/shard_map/ppermute | solution.py:37
  46.5 1.6 %collective-permute-start.9 = (f32[4,128,128]{2,1,0:T(8,128)}, f32[4,128,128]{2,1,0:T(8,128)S(1)}, u32[]{:S(2)}, u32[]{:S(2)}) collective-permute-start(f32[4,128,128]{2,1,0:T(8,128)} %get-tuple-element.11), channel_id=1, source_target_pairs={{0,8},{2,10},{4,12},{6,14},{8,0},{10,2},{12,4},{14,6},{16,24},{18,... | collective-permute-start | bytes 786440 | tf_op jit(solution)/shard_map/ppermute | solution.py:37
  48.0 5.3 %collective-permute-done.6 = f32[4,128,128]{2,1,0:T(8,128)S(1)} collective-permute-done((f32[4,128,128]{2,1,0:T(8,128)}, f32[4,128,128]{2,1,0:T(8,128)S(1)}, u32[]{:S(2)}, u32[]{:S(2)}) %collective-permute-start.6) | collective-permute-done | bytes 262176 | tf_op jit(solution)/shard_map/ppermute | solution.py:37
  53.3 1.0 %slice_add_fusion.3 = (f32[2,128,128]{2,1,0:T(8,128)S(1)}, f32[2,128,128]{2,1,0:T(8,128)S(1)}) fusion(f32[4,128,128]{2,1,0:T(8,128)S(1)} %collective-permute-done.6, f32[4,128,128]{2,1,0:T(8,128)} %get-tuple-element.10), kind=kLoop, calls=%fused_computation.3 | loop fusion | flops 65536 | bytes 786432 | tf_op jit(solution)/shard_map/add | solution.py:310
  54.3 1.8 %collective-permute-start.7 = (f32[2,128,128]{2,1,0:T(8,128)S(1)}, f32[2,128,128]{2,1,0:T(8,128)S(1)}, u32[]{:S(2)}, u32[]{:S(2)}) collective-permute-start(f32[2,128,128]{2,1,0:T(8,128)S(1)} %get-tuple-element.13), channel_id=1, source_target_pairs={{0,8},{2,10},{4,12},{6,14},{8,0},{10,2},{12,4},{14,6},{16,24},{18,... | collective-permute-start | bytes 393224 | tf_op jit(solution)/shard_map/ppermute | solution.py:37
  56.2 0.0 collective-permute-done.9
  56.2 1.0 %slice_add_fusion.1 = (f32[2,128,128]{2,1,0:T(8,128)S(1)}, f32[2,128,128]{2,1,0:T(8,128)S(1)}) fusion(f32[4,128,128]{2,1,0:T(8,128)S(1)} %collective-permute-done.9, f32[4,128,128]{2,1,0:T(8,128)} %get-tuple-element.12), kind=kLoop, calls=%fused_computation.1 | loop fusion | flops 65536 | bytes 786432 | tf_op jit(solution)/shard_map/add | solution.py:311
  57.2 1.6 %collective-permute-start.10 = (f32[2,128,128]{2,1,0:T(8,128)S(1)}, f32[2,128,128]{2,1,0:T(8,128)S(1)}, u32[]{:S(2)}, u32[]{:S(2)}) collective-permute-start(f32[2,128,128]{2,1,0:T(8,128)S(1)} %get-tuple-element.15), channel_id=1, source_target_pairs={{0,4},{2,6},{4,0},{6,2},{8,12},{10,14},{12,8},{14,10},{16,20},{18,... | collective-permute-start | bytes 393224 | tf_op jit(solution)/shard_map/ppermute | solution.py:37
  58.8 0.6 collective-permute-done.7
  59.4 2.9 %collective-permute-start.8 = (f32[1,128,128]{2,1,0:T(8,128)S(1)}, f32[1,128,128]{2,1,0:T(8,128)S(1)}, u32[]{:S(2)}, u32[]{:S(2)}) collective-permute-start(f32[1,128,128]{2,1,0:T(8,128)S(1)} %slice_add_fusion.7), channel_id=1, source_target_pairs={{0,16},{2,18},{4,20},{6,22},{8,24},{10,26},{12,28},{14,30},{16,0},... | collective-permute-start | bytes 196616 | tf_op jit(solution)/shard_map/ppermute | solution.py:37
  62.2 0.0 collective-permute-done.10
  62.2 2.6 %collective-permute-start.11 = (f32[1,128,128]{2,1,0:T(8,128)S(1)}, f32[1,128,128]{2,1,0:T(8,128)S(1)}, u32[]{:S(2)}, u32[]{:S(2)}) collective-permute-start(f32[1,128,128]{2,1,0:T(8,128)S(1)} %slice_add_fusion.5), channel_id=1, source_target_pairs={{0,16},{2,18},{4,20},{6,22},{8,24},{10,26},{12,28},{14,30},{16,0},... | collective-permute-start | bytes 196616 | tf_op jit(solution)/shard_map/ppermute | solution.py:37
  64.9 1.6 %collective-permute-done.8 = f32[1,128,128]{2,1,0:T(8,128)S(1)} collective-permute-done((f32[1,128,128]{2,1,0:T(8,128)S(1)}, f32[1,128,128]{2,1,0:T(8,128)S(1)}, u32[]{:S(2)}, u32[]{:S(2)}) %collective-permute-start.8) | collective-permute-done | bytes 65568 | tf_op jit(solution)/shard_map/ppermute | solution.py:37
  66.5 1.0 %collective-permute-done.11 = f32[1,128,128]{2,1,0:T(8,128)S(1)} collective-permute-done((f32[1,128,128]{2,1,0:T(8,128)S(1)}, f32[1,128,128]{2,1,0:T(8,128)S(1)}, u32[]{:S(2)}, u32[]{:S(2)}) %collective-permute-start.11) | collective-permute-done | bytes 65568 | tf_op jit(solution)/shard_map/ppermute | solution.py:37
  67.5 0.7 pad_maximum_fusion
  (10 shorter events, 0.1 us)
Async XLA Ops:
  0.0 12.2 %copy-start.7 = (s32[2,8]{1,0:T(2,128)S(1)}, s32[2,8]{1,0:T(2,128)}, u32[]{:S(2)}) copy-start(s32[2,8]{1,0:T(2,128)} %param.11) | copy-start | bytes 196
  2.7 14.9 %copy-start.4 = (s32[2,16]{1,0:T(2,128)}, s32[2,16]{1,0:T(2,128)S(1)}, u32[]{:S(2)}) copy-start(s32[2,16]{1,0:T(2,128)S(1)} %get-tuple-element.20.index_ref.refs_0_) | copy-start | bytes 388
  2.7 4.6 %collective-permute-start = (s32[2,16]{1,0:T(2,128)S(1)}, s32[2,16]{1,0:T(2,128)S(1)}, u32[]{:S(2)}, u32[]{:S(2)}) collective-permute-start(s32[2,16]{1,0:T(2,128)S(1)} %get-tuple-element.20.index_ref.refs_0_), channel_id=1, source_target_pairs={{0,1},{1,0},{2,3},{3,2},{4,5},{5,4},{6,7},{7,6},{8,9},{9,8},{10,11... | collective-permute-start | bytes 392 | tf_op jit(solution)/shard_map/ppermute | solution.py:37
  7.3 0.6 copy-start.5
  10.2 7.4 %collective-permute-start.2 = (f32[16,32,128]{2,1,0:T(8,128)}, f32[16,32,128]{2,1,0:T(8,128)S(1)}, u32[]{:S(2)}, u32[]{:S(2)}) collective-permute-start(f32[16,32,128]{2,1,0:T(8,128)} %gather_rows.1), channel_id=1, source_target_pairs={{0,1},{1,0},{2,3},{3,2},{4,5},{5,4},{6,7},{7,6},{8,9},{9,8},{10,11... | collective-permute-start | bytes 786440 | tf_op jit(solution)/shard_map/ppermute | solution.py:37
  17.6 0.7 %copy-start.3 = (f32[16,32,128]{2,1,0:T(8,128)}, f32[16,32,128]{2,1,0:T(8,128)S(1)}, u32[]{:S(2)}) copy-start(f32[16,32,128]{2,1,0:T(8,128)S(1)} %collective-permute-done.2) | copy-start | bytes 786436
  18.3 19.1 %copy-start.6 = (s32[2,16]{1,0:T(2,128)S(1)}, s32[2,16]{1,0:T(2,128)}, u32[]{:S(2)}) copy-start(s32[2,16]{1,0:T(2,128)} %copy-done.5) | copy-start | bytes 388
  30.8 6.6 %collective-permute-start.3 = (f32[16,32,128]{2,1,0:T(8,128)}, f32[16,32,128]{2,1,0:T(8,128)S(1)}, u32[]{:S(2)}, u32[]{:S(2)}) collective-permute-start(f32[16,32,128]{2,1,0:T(8,128)} %bitcast.31), channel_id=1, source_target_pairs={{0,1},{1,0},{2,3},{3,2},{4,5},{5,4},{6,7},{7,6},{8,9},{9,8},{10,11... | collective-permute-start | bytes 786440 | tf_op jit(solution)/shard_map/ppermute | solution.py:37
  32.5 7.0 %collective-permute-start.4 = (f32[16,32,128]{2,1,0:T(8,128)}, f32[16,32,128]{2,1,0:T(8,128)S(1)}, u32[]{:S(2)}, u32[]{:S(2)}) collective-permute-start(f32[16,32,128]{2,1,0:T(8,128)} %bitcast.32), channel_id=1, source_target_pairs={{0,2},{2,0},{4,6},{6,4},{8,10},{10,8},{12,14},{14,12},{16,18},{18,... | collective-permute-start | bytes 786440 | tf_op jit(solution)/shard_map/ppermute | solution.py:37
  37.4 2.2 %copy-start = (f32[16,32,128]{2,1,0:T(8,128)}, f32[16,32,128]{2,1,0:T(8,128)S(1)}, u32[]{:S(2)}) copy-start(f32[16,32,128]{2,1,0:T(8,128)S(1)} %collective-permute-done.3.refs_5_) | copy-start | bytes 786436
  37.4 2.1 %collective-permute-start.5 = (f32[16,32,128]{2,1,0:T(8,128)S(1)}, f32[16,32,128]{2,1,0:T(8,128)S(1)}, u32[]{:S(2)}, u32[]{:S(2)}) collective-permute-start(f32[16,32,128]{2,1,0:T(8,128)S(1)} %collective-permute-done.3.refs_5_), channel_id=1, source_target_pairs={{0,2},{2,0},{4,6},{6,4},{8,10},{10,8},{12,14},{14,12},{16,18},{18,... | collective-permute-start | bytes 786440 | tf_op jit(solution)/shard_map/ppermute | solution.py:37
  37.4 1.5 %collective-permute-start.1 = (s32[2,2,16]{2,1,0:T(2,128)S(1)}, s32[2,2,16]{2,1,0:T(2,128)S(1)}, u32[]{:S(2)}, u32[]{:S(2)}) collective-permute-start(s32[2,2,16]{2,1,0:T(2,128)S(1)} %pad_add_fusion), channel_id=1, source_target_pairs={{0,2},{2,0},{4,6},{6,4},{8,10},{10,8},{12,14},{14,12},{16,18},{18,... | collective-permute-start | bytes 776 | tf_op jit(solution)/shard_map/ppermute | solution.py:37
  39.5 0.7 %copy-start.1 = (f32[16,32,128]{2,1,0:T(8,128)}, f32[16,32,128]{2,1,0:T(8,128)S(1)}, u32[]{:S(2)}) copy-start(f32[16,32,128]{2,1,0:T(8,128)S(1)} %collective-permute-done.4.refs_6_) | copy-start | bytes 786436
  39.5 0.8 %copy-start.2 = (f32[16,32,128]{2,1,0:T(8,128)}, f32[16,32,128]{2,1,0:T(8,128)S(1)}, u32[]{:S(2)}) copy-start(f32[16,32,128]{2,1,0:T(8,128)S(1)} %collective-permute-done.5.refs_7_) | copy-start | bytes 786436
  44.7 8.6 %collective-permute-start.6 = (f32[4,128,128]{2,1,0:T(8,128)}, f32[4,128,128]{2,1,0:T(8,128)S(1)}, u32[]{:S(2)}, u32[]{:S(2)}) collective-permute-start(f32[4,128,128]{2,1,0:T(8,128)} %get-tuple-element.9), channel_id=1, source_target_pairs={{0,4},{2,6},{4,0},{6,2},{8,12},{10,14},{12,8},{14,10},{16,20},{18,... | collective-permute-start | bytes 786440 | tf_op jit(solution)/shard_map/ppermute | solution.py:37
  46.5 9.7 %collective-permute-start.9 = (f32[4,128,128]{2,1,0:T(8,128)}, f32[4,128,128]{2,1,0:T(8,128)S(1)}, u32[]{:S(2)}, u32[]{:S(2)}) collective-permute-start(f32[4,128,128]{2,1,0:T(8,128)} %get-tuple-element.11), channel_id=1, source_target_pairs={{0,8},{2,10},{4,12},{6,14},{8,0},{10,2},{12,4},{14,6},{16,24},{18,... | collective-permute-start | bytes 786440 | tf_op jit(solution)/shard_map/ppermute | solution.py:37
  54.3 5.0 %collective-permute-start.7 = (f32[2,128,128]{2,1,0:T(8,128)S(1)}, f32[2,128,128]{2,1,0:T(8,128)S(1)}, u32[]{:S(2)}, u32[]{:S(2)}) collective-permute-start(f32[2,128,128]{2,1,0:T(8,128)S(1)} %get-tuple-element.13), channel_id=1, source_target_pairs={{0,8},{2,10},{4,12},{6,14},{8,0},{10,2},{12,4},{14,6},{16,24},{18,... | collective-permute-start | bytes 393224 | tf_op jit(solution)/shard_map/ppermute | solution.py:37
  57.2 5.1 %collective-permute-start.10 = (f32[2,128,128]{2,1,0:T(8,128)S(1)}, f32[2,128,128]{2,1,0:T(8,128)S(1)}, u32[]{:S(2)}, u32[]{:S(2)}) collective-permute-start(f32[2,128,128]{2,1,0:T(8,128)S(1)} %get-tuple-element.15), channel_id=1, source_target_pairs={{0,4},{2,6},{4,0},{6,2},{8,12},{10,14},{12,8},{14,10},{16,20},{18,... | collective-permute-start | bytes 393224 | tf_op jit(solution)/shard_map/ppermute | solution.py:37
  59.4 7.1 %collective-permute-start.8 = (f32[1,128,128]{2,1,0:T(8,128)S(1)}, f32[1,128,128]{2,1,0:T(8,128)S(1)}, u32[]{:S(2)}, u32[]{:S(2)}) collective-permute-start(f32[1,128,128]{2,1,0:T(8,128)S(1)} %slice_add_fusion.7), channel_id=1, source_target_pairs={{0,16},{2,18},{4,20},{6,22},{8,24},{10,26},{12,28},{14,30},{16,0},... | collective-permute-start | bytes 196616 | tf_op jit(solution)/shard_map/ppermute | solution.py:37
  62.2 5.2 %collective-permute-start.11 = (f32[1,128,128]{2,1,0:T(8,128)S(1)}, f32[1,128,128]{2,1,0:T(8,128)S(1)}, u32[]{:S(2)}, u32[]{:S(2)}) collective-permute-start(f32[1,128,128]{2,1,0:T(8,128)S(1)} %slice_add_fusion.5), channel_id=1, source_target_pairs={{0,16},{2,18},{4,20},{6,22},{8,24},{10,26},{12,28},{14,30},{16,0},... | collective-permute-start | bytes 196616 | tf_op jit(solution)/shard_map/ppermute | solution.py:37

commit v3 on v0

v3 whole, which is shorter than its diff:
```python
import functools

import jax
import jax.numpy as jnp
from jax import lax
from jax.experimental import pallas as pl
from jax.experimental.pallas import tpu as pltpu
from jax.sharding import PartitionSpec as P

LY = 64
LZ = 8
STEPS_FWD = 4
STEPS_ADJ = 4
TILE = 32
LANES = 128
SUB = 8
PARTS = TILE // SUB

AIR = 0.05
OMEGA = 0.5
BETA = 0.5

HALVES = LANES // LY
PACKED = TILE // SUB * HALVES

VMEM = pl.BlockSpec(memory_space=pltpu.VMEM)
SMEM = pl.BlockSpec(memory_space=pltpu.SMEM)
LIMIT = 16 << 20


def call(body, name, out, in_specs, work, moved, **kwargs):
    return pl.pallas_call(
        body,
        out_shape=out,
        in_specs=in_specs,
        out_specs=jax.tree.map(lambda _: VMEM, out),
        compiler_params=pltpu.CompilerParams(vmem_limit_bytes=LIMIT),
        cost_estimate=pl.CostEstimate(flops=work, bytes_accessed=moved, transcendentals=0),
        name=name,
        **kwargs,
    )


def floats(*shape):
    return jax.ShapeDtypeStruct(shape, jnp.float32)


def place_slots(owner_flat, owners_count, capacity):
    chosen = (owner_flat[:, None] == jnp.arange(owners_count, dtype=jnp.int32)[None, :]).astype(
        jnp.int32
    )
    before = jnp.cumsum(chosen, axis=0) - chosen
    return owner_flat * capacity + jnp.sum(before * chosen, axis=1)


def swap_over(axis, mask):
    ring = [(i, i ^ mask) for i in range(lax.axis_size(axis))]
    return lambda value: lax.ppermute(value, axis, ring)


def gather_body(starts_ref, block_ref, out_ref):
    wide = starts_ref.shape[1]
    for tile in range(out_ref.shape[0]):
        start = starts_ref[tile // wide, tile % wide]
        out_ref[tile] = block_ref[pl.ds(start, TILE), :]


def gather_rows(starts, block):
    out = floats(starts.size, TILE, LANES)
    return call(gather_body, "gather_rows", out, [SMEM, VMEM], 0, 8 * out.size)(starts, block)


def low_half():
    return lax.broadcasted_iota(jnp.int32, (SUB, LANES), 1) < LY


def pack(first, second, low):
    even = jnp.where(low, first, pltpu.roll(second, LY, 1))
    odd = jnp.where(low, pltpu.roll(first, LY, 1), second)
    return even, odd


def rows_of(ref, base, step):
    return ref[pl.ds(base, SUB, stride=step * PARTS), :]


def prepare_body(source_ref, observed_ref, source_out, observed_out):
    low = low_half()
    for ref, out in ((source_ref, source_out), (observed_ref, observed_out)):
        for part in range(3):
            for z in range(LZ):
                for j in range(PARTS):
                    base = part * LZ * TILE + z + LZ * j
                    first = rows_of(ref, base, LZ)
                    second = rows_of(ref, base + 3 * LZ * TILE, LZ)
                    out[part, z, 2 * j], out[part, z, 2 * j + 1] = pack(first, second, low)


def by_rows(values):
    count = values.shape[0]
    parts = values.reshape(count, 3, LZ, TILE, LANES)
    return parts.transpose(0, 1, 3, 2, 4).reshape(count * 3 * TILE * LZ, LANES)


def prepare(source, observed):
    out = floats(3, LZ, PACKED, SUB, LANES)
    return call(
        prepare_body, "prepare", (out, out), [VMEM, VMEM], 8 * source.size, 16 * source.size
    )(by_rows(source), by_rows(observed))


def fields_body(
    starts_ref, owners_ref, lengths_ref, table_ref, answer_ref, source_ref, observed_ref, out_ref,
    field, adjoint, right, curl, scale, decay, weight,
):
    me = lax.axis_index("mdl")
    lane = lax.broadcasted_iota(jnp.int32, (SUB, LANES), 1)
    sub = lax.broadcasted_iota(jnp.int32, (SUB, LANES), 0)
    low = low_half()
    not_last = lane % LY != LY - 1
    not_first = lane % LY != 0
    top, bottom = sub != 0, sub != SUB - 1
    zero = jnp.zeros((SUB, LANES), jnp.float32)

    def y_next(value):
        return jnp.where(not_last, pltpu.roll(value, LANES - 1, 1), 0.0)

    def y_prev(value):
        return jnp.where(not_first, pltpu.roll(value, 1, 1), 0.0)

    def x_next(ref, part, z, k):
        if k + 1 < PACKED:
            return ref[part, z, k + 1]
        return jnp.where(bottom, pltpu.roll(ref[part, z, 0], SUB - 1, 0), 0.0)

    def x_prev(ref, part, z, k):
        if k > 0:
            return ref[part, z, k - 1]
        return jnp.where(top, pltpu.roll(ref[part, z, PACKED - 1], 1, 0), 0.0)

    def sweep(state):
        for z in range(LZ):
            for k in range(PACKED):
                east, north, vert = state[0, z, k], state[1, z, k], state[2, z, k]
                east_d = state[0, z + 1, k] if z + 1 < LZ else zero
                north_d = state[1, z + 1, k] if z + 1 < LZ else zero
                curl[0, z, k] = (y_next(vert) - vert) - (north_d - north)
                curl[1, z, k] = (east_d - east) - (x_next(state, 2, z, k) - vert)
                curl[2, z, k] = (x_next(state, 1, z, k) - north) - (y_next(east) - east)
            for k in range(PACKED):
                curl_x, curl_y, curl_z = curl[0, z, k], curl[1, z, k], curl[2, z, k]
                up_x = curl[0, z - 1, k] if z else zero
                up_y = curl[1, z - 1, k] if z else zero
                back_x = (up_y - curl_y) - (y_prev(curl_z) - curl_z)
                back_y = (x_prev(curl, 2, z, k) - curl_z) - (up_x - curl_x)
                back_z = (y_prev(curl_x) - curl_x) - (x_prev(curl, 1, z, k) - curl_y)
                s, d = scale[z, k], decay[z, k]
                state[0, z, k] = d * state[0, z, k] + (right[0, z, k] - s * back_x)
                state[1, z, k] = d * state[1, z, k] + (right[1, z, k] - s * back_y)
                state[2, z, k] = d * state[2, z, k] + (right[2, z, k] - s * back_z)

    for z in range(LZ):

        def layer(sounding, j):
            raw = rows_of(table_ref, starts_ref[sounding, z] + j, 1)
            sent = rows_of(answer_ref, (sounding * LZ + z) * TILE + j, 1)
            mine = jnp.full((SUB, LANES), owners_ref[sounding, z] == me)
            return jnp.where(mine, raw, sent)

        length = jnp.where(low, lengths_ref[0, z], lengths_ref[1, z])
        for j in range(PARTS):
            earth = PARTS * sub + j < length
            for odd, logs in enumerate(pack(layer(0, j), layer(1, j), low)):
                k = 2 * j + odd
                conduct = jnp.where(earth, jnp.exp(logs), AIR)
                s = OMEGA / (4.0 + conduct)
                scale[z, k] = s
                decay[z, k] = 1.0 - s * conduct
                weight[z, k] = jnp.where(earth, -conduct, 0.0)
                for part in range(3):
                    value = s * source_ref[part, z, k]
                    right[part, z, k] = value
                    field[part, z, k] = value

    @pl.loop(0, STEPS_FWD - 1)
    def _(step):
        sweep(field)

    for z in range(LZ):
        for k in range(PACKED):
            for part in range(3):
                value = scale[z, k] * (field[part, z, k] - observed_ref[part, z, k])
                right[part, z, k] = value
                adjoint[part, z, k] = value

    @pl.loop(0, STEPS_ADJ - 1)
    def _(step):
        sweep(adjoint)

    for z in range(LZ):

        def partial(k):
            total = field[0, z, k] * adjoint[0, z, k]
            total += field[1, z, k] * adjoint[1, z, k]
            total += field[2, z, k] * adjoint[2, z, k]
            return weight[z, k] * total

        for j in range(PARTS):
            first, second = pack(partial(2 * j), partial(2 * j + 1), low)
            out_ref[pl.ds(z * TILE + j, SUB, stride=PARTS), :] = first
            out_ref[pl.ds((LZ + z) * TILE + j, SUB, stride=PARTS), :] = second


def soundings_partial(starts, owners, lengths, table, answer, source, observed):
    tiles = starts.size
    planes = pltpu.VMEM((3, LZ, PACKED, SUB, LANES), jnp.float32)
    single = pltpu.VMEM((LZ, PACKED, SUB, LANES), jnp.float32)
    cells = tiles * TILE * LANES
    out = call(
        fields_body, "soundings_partial", floats(tiles * TILE, LANES),
        [SMEM] * 3 + [VMEM] * 4, 500 * cells, 40 * cells,
        scratch_shapes=[planes] * 4 + [single] * 3,
    )(starts, owners, lengths, table, answer.reshape(tiles * TILE, LANES), source, observed)
    return out.reshape(tiles, TILE, LANES)


def arranged(order):
    if not order:
        return [0]
    rest = arranged(order[1:])
    return [slot | (1 << order[0]) for slot in rest] + rest


def add_terms(starts_ref, owners_ref, terms_ref, total, share, slots):
    owner, me = lax.axis_index("mdl"), lax.axis_index("grp")
    span, wide = share + 2 * TILE, starts_ref.shape[1]
    for tile in range(terms_ref.shape[0]):
        start = starts_ref[tile // wide, tile % wide]
        first = lax.div(start, share)
        target = first + ((first ^ me) & 1)
        where = start - target * share
        wanted = (owners_ref[tile // wide, tile % wide] == owner) & (where > -TILE)
        base = ((target >> 1) ^ (me >> 1)) * span + TILE + where
        base = jnp.where(wanted, base, slots * span)
        total[pl.ds(base, TILE), :] += terms_ref[tile]


def first_body(groups, count, *refs):
    model_ref, total = refs[3 * count], refs[-1]
    me = lax.axis_index("grp")
    share = model_ref.shape[0] // groups
    total[...] = jnp.zeros_like(total)
    local = model_ref[pl.ds(pl.multiple_of(me * share, share), share), :]
    lane = lax.broadcasted_iota(jnp.int32, local.shape, 1)
    left = jnp.where(lane == 0, local, pltpu.roll(local, 1, 1))
    right = jnp.where(lane == LANES - 1, local, pltpu.roll(local, LANES - 1, 1))
    total[TILE : TILE + share, :] = BETA * (2.0 * local - left - right)
    for i in range(count):
        add_terms(*refs[3 * i : 3 * i + 3], total, share, groups // 2)


def first_sums(groups_of, block):
    groups = lax.axis_size("grp")
    share = block.shape[0] // groups
    out = floats(groups // 2 * (share + 2 * TILE) + TILE, LANES)
    flat = [a for triple in groups_of for a in triple]
    return call(
        functools.partial(first_body, groups, len(groups_of)), "first_sums", out,
        [SMEM, SMEM, VMEM] * len(groups_of) + [VMEM], out.size, 8 * out.size,
    )(*flat, block)


def last_body(orders, groups, share, count, *refs):
    total, outs = refs[3 * count + 1], refs[3 * count + 2 :]
    span, slots, half = share + 2 * TILE, groups // 2, share // 2
    for i in range(count):
        add_terms(*refs[3 * i : 3 * i + 3], total, share, slots)
    for which, order in enumerate(orders):
        for place, slot in enumerate(arranged(order)):
            out = outs[2 * which + (place * 2 >= slots)]
            begin = slot * span + TILE + which * half
            out[place % (slots // 2)] = total[begin : begin + half, :]


def last_sums(groups_of, total, rows, orders):
    groups = lax.axis_size("grp")
    share, slots = rows // groups, groups // 2
    out = floats(slots // 2, share // 2, LANES)
    flat = [a for triple in groups_of for a in triple]
    count = len(groups_of)
    return call(
        functools.partial(last_body, orders, groups, share, count), "last_sums",
        (floats(*total.shape),) + (out,) * 4, [SMEM, SMEM, VMEM] * count + [VMEM],
        total.size, 8 * total.size, input_output_aliases={3 * count: 0},
    )(*flat, total)[1:]


def finish_body(got_low, low, got_high, high, out_ref):
    half = out_ref.shape[0] // 2
    out_ref[:half] = got_low[0] + low[0]
    out_ref[half:] = got_high[0] + high[0]


def per_device(model, source, observed, owner_ids, offsets, lengths):
    rows, owners_count, groups = model.shape[0], lax.axis_size("mdl"), lax.axis_size("grp")
    block = model.reshape(rows, LANES)
    tiles = source.shape[0] * LZ
    across, beside = swap_over("mdl", 1), swap_over("grp", 1)
    if owners_count == 2:
        asked, asked_ids = lax.optimization_barrier((across(offsets), across(owner_ids)))
        owners, asked_owners = (ids.reshape(offsets.shape) for ids in (owner_ids, asked_ids))
        source, observed = prepare(source, observed)
        answer = across(gather_rows(asked, block))
        told = beside(jnp.concatenate([offsets, owners, asked, asked_owners]))
        answer, told = lax.optimization_barrier((answer, told))
        told = told.reshape(4, *offsets.shape)
        terms = soundings_partial(offsets, owners, lengths, block, answer, source, observed)
        others = across(terms)
        total = first_sums([(offsets, owners, terms), (told[0], told[1], beside(terms))], block)
        final = [(asked, asked_owners, others), (told[2], told[3], beside(others))]
    else:
        capacity = max(4, 2 * tiles // owners_count)
        places = place_slots(owner_ids.reshape(tiles), owners_count, capacity)
        swap = functools.partial(
            lax.all_to_all, axis_name="mdl", split_axis=0, concat_axis=0, tiled=True
        )
        request = jnp.zeros((owners_count * capacity,), jnp.int32).at[places].set(
            offsets.reshape(tiles)
        )
        asked = swap(request.reshape(owners_count, capacity))
        source, observed = prepare(source, observed)
        given = gather_rows(asked, block).reshape(owners_count, capacity, TILE, LANES)
        fetched = swap(given).reshape(owners_count * capacity * TILE, LANES)
        mine = jnp.full_like(asked, lax.axis_index("mdl"))
        terms = soundings_partial(
            (places * TILE).reshape(offsets.shape), jnp.full_like(offsets, lax.axis_index("mdl")),
            lengths, fetched, jnp.zeros((tiles, TILE, LANES), jnp.float32), source, observed,
        )
        outgoing = jnp.zeros((owners_count * capacity, TILE, LANES), jnp.float32)
        outgoing = outgoing.at[places].set(terms).reshape(owners_count, capacity, TILE, LANES)
        arrived = swap(outgoing).reshape(owners_count * capacity, TILE, LANES)
        total = first_sums([(asked, mine, arrived)], block)
        final = [(beside(asked), mine, beside(arrived))]

    bits = tuple(range(groups.bit_length() - 2))
    orders = (bits, bits[1:2] + bits[0:1] + bits[2:])
    low_give, low, high_give, high = last_sums(final, total, rows, orders)
    for low_bit, high_bit in zip(*orders):
        got_low = swap_over("grp", 2 << low_bit)(low_give)
        got_high = swap_over("grp", 2 << high_bit)(high_give)
        cut = low.shape[0] // 2
        if cut:
            low_give, low = got_low[:cut] + low[:cut], got_low[cut:] + low[cut:]
            high_give, high = got_high[:cut] + high[:cut], got_high[cut:] + high[cut:]
    out = call(
        finish_body, "finish", floats(rows // groups, LANES), [VMEM] * 4, low.size, 24 * low.size
    )(got_low, low, got_high, high)
    return out[:, None, :]


def solution(mesh):
    placed = (
        P(None, "mdl", None),
        P(("grp", "mdl"), None, None, None),
        P(("grp", "mdl"), None, None, None),
        P(("grp", "mdl"), None, None),
        P(("grp", "mdl"), None),
        P(("grp", "mdl"), None),
    )
    return jax.shard_map(
        per_device, mesh=mesh, in_specs=placed, out_specs=P("grp", "mdl", None), check_vma=False
    )
```

time: 142 us -> 51.8 us (0.36)
  waiting for transfers between devices: 79.2 us -> 23.7 us
  other arithmetic: 17.3 us -> 0.11 us
  local copies, waits for them, and re-layouts: 18.8 us -> 3.87 us
  between operations: 14 us -> 0.08 us
  Pallas kernels: 0 us -> 8.79 us
  starting transfers between devices: 12.1 us -> 15 us
    reduce_scatter x1 -> x0, waiting for transfers between devices: 62.3 us -> none  [per_device(): lax.psum_scatter(block_partial, 'grp', scatter_dimension=0, tiled=True)]
    ppermute x0 -> x13, waiting for transfers between devices: none -> 23.7 us  [swap_over(): return lambda value: lax.ppermute(value, axis, ring)]
    all_to_all x3 -> x0, waiting for transfers between devices: 16.9 us -> none  [the longest x1 7.19 us: settle(): lax.all_to_all(values, 'mdl', split_axis=0, concat_axis=0, tiled=True)]
    ppermute x0 -> x13, starting transfers between devices: none -> 15 us  [swap_over(): return lambda value: lax.ppermute(value, axis, ring)]
    all_to_all x3 -> x0, starting transfers between devices: 12.1 us -> none  [the longest x1 4.34 us: settle(): lax.all_to_all(values, 'mdl', split_axis=0, concat_axis=0, tiled=True)]
    pallas_call x0 -> x6, Pallas kernels: none -> 8.79 us  [the longest x1 4.75 us: soundings_partial(): call(fields_body, 'soundings_partial', floats(tiles * TILE, LANES), [SMEM...]
    scatter-add x1 -> x0, other arithmetic: 7.43 us -> none  [settle(): jnp.zeros((block.shape[0], 128), jnp.float32).at[target_rows]]
    gather x2 -> x0, local copies, waits for them, and re-layouts: 4.41 us -> none  [the longest x1 2.8 us: settle(): block[lax.all_to_all(request, 'mdl', split_axis=0, concat_axis=0, tiled=T...]
  transfers between devices with their start and end apart: 4 -> 13, of which waited for: 4 -> 9; matrix products, arithmetic and copies ran while one was open for 1% -> 0% of each run, Pallas kernels for 0% -> 4%
where the time goes in v3:
time: 51.8 us; the launch traced here: 51.5 us
  waiting for transfers between devices  23.7 us (46%)
  starting transfers between devices  15 us (29%)
  Pallas kernels  8.79 us (17%)
  local copies, waits for them, and re-layouts  3.87 us (7%)
    ppermute x13, waiting for transfers between devices, swap_over(): return lambda value: lax.ppermute(value, axis, ring)  23.7 us
    ppermute x13, starting transfers between devices, swap_over(): return lambda value: lax.ppermute(value, axis, ring)  15 us
    pallas_call x1, Pallas kernels, soundings_partial(): call(fields_body, 'soundings_partial', floats(tiles * TILE, LANES), [SMEM...  4.75 us
    unnamed x14, local copies, waits for them, and re-layouts  3.87 us
  transfers between devices with their start and end apart: 13, of which 9 were waited for; matrix products, arithmetic and copies ran while one was open for 0% of the time, Pallas kernels for 4%

profile of v3, /device:TPU:0, one launch (start us, length us, event | category | flops | bytes accessed | tf_op | source)
XLA Modules:
  0.0 51.5 jit_solution(10385003634285785993)
XLA Ops:
  0.0 0.0 copy-start.4
  0.0 3.0 %collective-permute-start.1 = (s32[2,8,1]{1,2,0:T(1,128)}, s32[2,8,1]{1,2,0:T(1,128)S(1)}, u32[]{:S(2)}, u32[]{:S(2)}) collective-permute-start(s32[2,8,1]{1,2,0:T(1,128)} %param.9), channel_id=1, source_target_pairs={{0,1},{1,0},{2,3},{3,2},{4,5},{5,4},{6,7},{7,6},{8,9},{9,8},{10,11... | collective-permute-start | bytes 200 | tf_op jit(solution)/shard_map/ppermute | solution.py:58
  3.0 0.1 collective-permute-start
  3.0 1.7 %collective-permute-done.1 = s32[2,8,1]{1,2,0:T(1,128)S(1)} collective-permute-done((s32[2,8,1]{1,2,0:T(1,128)}, s32[2,8,1]{1,2,0:T(1,128)S(1)}, u32[]{:S(2)}, u32[]{:S(2)}) %collective-permute-start.1) | collective-permute-done | bytes 96 | tf_op jit(solution)/shard_map/ppermute | solution.py:58
  4.7 2.0 %collective-permute-done.starts_ref.refs_0_ = s32[2,8]{1,0:T(2,128)S(1)} collective-permute-done((s32[2,8]{1,0:T(2,128)}, s32[2,8]{1,0:T(2,128)S(1)}, u32[]{:S(2)}, u32[]{:S(2)}) %collective-permute-start) | collective-permute-done | bytes 96 | tf_op jit(solution)/shard_map/ppermute | solution.py:58
  6.8 0.0 copy-start
  6.8 1.6 %copy-done = f32[4096,1,128]{2,1,0:T(1,128)S(1)} copy-done((f32[4096,1,128]{2,1,0:T(1,128)S(1)}, f32[4096,1,128]{2,1,0:T(1,128)}, u32[]{:S(2)}) %copy-start) | copy-done | bytes 2097176
  8.3 0.0 copy-start.5
  8.3 0.0 copy-start.1
  8.4 0.6 %gather_rows.1 = f32[16,32,128]{2,1,0:T(8,128)S(1)} custom-call(s32[2,8]{1,0:T(2,128)S(1)} %collective-permute-done.starts_ref.refs_0_, f32[4096,128]{1,0:T(8,128)S(1)} %bitcast.18), custom_call_target="tpu_custom_call" | custom-call | bytes 524288 | tf_op jit(solution)/shard_map/gather_rows/pallas_call | solution.py:70
  8.9 0.0 copy-start.6
  8.9 0.1 collective-permute-start.2
  9.1 0.0 copy-done.4
  9.1 0.0 copy-done.5
  9.1 0.1 collective-permute-start.3
  9.2 0.0 copy-start.2
  9.2 1.1 %copy-done.2 = f32[2,3,8,4096]{3,2,1,0:T(8,128)S(1)} copy-done((f32[2,3,8,4096]{3,2,1,0:T(8,128)S(1)}, f32[2,3,8,4096]{3,2,1,0:T(8,128)}, u32[]{:S(2)}) %copy-start.2) | copy-done | bytes 786456
  10.3 0.0 copy-start.3
  10.3 1.1 %copy-done.3 = f32[2,3,8,4096]{3,2,1,0:T(8,128)S(1)} copy-done((f32[2,3,8,4096]{3,2,1,0:T(8,128)S(1)}, f32[2,3,8,4096]{3,2,1,0:T(8,128)}, u32[]{:S(2)}) %copy-start.3) | copy-done | bytes 786456
  11.4 0.9 %prepare.1 = (f32[3,8,8,8,128]{4,3,2,1,0:T(8,128)S(1)}, f32[3,8,8,8,128]{4,3,2,1,0:T(8,128)S(1)}) custom-call(f32[1536,128]{1,0:T(8,128)S(1)} %bitcast.24, f32[1536,128]{1,0:T(8,128)S(1)} %bitcast.25), custom_call_target="tpu_custom_call" | custom-call | flops 1572864 | bytes 3145728 | tf_op jit(solution)/shard_map/prepare/pallas_call | solution.py:107
  12.4 0.0 collective-permute-done.3
  12.4 3.2 %collective-permute-done.2 = f32[16,32,128]{2,1,0:T(8,128)S(1)} collective-permute-done((f32[16,32,128]{2,1,0:T(8,128)S(1)}, f32[16,32,128]{2,1,0:T(8,128)S(1)}, u32[]{:S(2)}, u32[]{:S(2)}) %collective-permute-start.2) | collective-permute-done | bytes 262176 | tf_op jit(solution)/shard_map/ppermute | solution.py:58
  15.6 0.0 copy-done.1
  15.6 0.0 copy-done.6
  15.6 4.8 %soundings_partial.1 = f32[512,128]{1,0:T(8,128)S(1)} custom-call(s32[2,8]{1,0:T(2,128)S(1)} %copy-done.4, s32[2,8]{1,0:T(2,128)S(1)} %bitcast.28, s32[2,8]{1,0:T(2,128)S(1)} %copy-done.6, f32[4096,128]{1,0:T(8,128)S(1)} %bitcast.19, f32[512,128]{1,0:T(8,128)S(1)} %bitcast.26, f32[3,8,8,8,128]{4,3,2,1,0:T(8,128)S(1)} %get-tuple-element.18.source_ref, ...), custom_call_target="tpu_custom_call" | custom-call | flops 32768000 | bytes 2621440 | tf_op jit(solution)/shard_map/soundings_partial/pallas_call | solution.py:219
  20.4 0.4 collective-permute-start.4
  20.8 0.0 collective-permute-start.6
  20.8 6.0 %collective-permute-done.4.refs_2_ = f32[16,32,128]{2,1,0:T(8,128)S(1)} collective-permute-done((f32[16,32,128]{2,1,0:T(8,128)S(1)}, f32[16,32,128]{2,1,0:T(8,128)S(1)}, u32[]{:S(2)}, u32[]{:S(2)}) %collective-permute-start.4) | collective-permute-done | bytes 262176 | tf_op jit(solution)/shard_map/ppermute | solution.py:58
  26.8 0.0 collective-permute-start.5
  26.8 0.0 collective-permute-done.6.refs_5_
  26.8 1.0 %first_sums.1.refs_6_ = f32[2592,128]{1,0:T(8,128)S(1)} custom-call(s32[2,8]{1,0:T(2,128)S(1)} %copy-done.4, s32[2,8]{1,0:T(2,128)S(1)} %bitcast.29, f32[16,32,128]{2,1,0:T(8,128)S(1)} %bitcast.23, s32[2,8]{1,0:T(2,128)S(1)} %get-tuple-element.34.refs_3_, s32[2,8]{1,0:T(2,128)S(1)} %get-tuple-element.33.refs_4_, ...), custom_call_target="tpu_custom_call" | custom-call | flops 331776 | bytes 2654208 | tf_op jit(solution)/shard_map/first_sums/pallas_call | solution.py:267
  27.8 0.6 %collective-permute-done.5.refs_5_ = f32[16,32,128]{2,1,0:T(8,128)S(1)} collective-permute-done((f32[16,32,128]{2,1,0:T(8,128)S(1)}, f32[16,32,128]{2,1,0:T(8,128)S(1)}, u32[]{:S(2)}, u32[]{:S(2)}) %collective-permute-start.5) | collective-permute-done | bytes 262176 | tf_op jit(solution)/shard_map/ppermute | solution.py:58
  28.4 0.9 %last_sums.1 = (f32[2592,128]{1,0:T(8,128)S(1)}, f32[4,128,128]{2,1,0:T(8,128)S(1)}, f32[4,128,128]{2,1,0:T(8,128)S(1)}, f32[4,128,128]{2,1,0:T(8,128)S(1)}, f32[4,128,128]{2,1,0:T(8,128)S(1)}) custom-call(s32[2,8]{1,0:T(2,128)S(1)} %collective-permute-done.starts_ref.refs_0_, s32[2,8]{1,0:T(2,128)S(1)} %bitcast.31, ...), custom_call_target="tpu_custom_call", output_to_operand_aliasing={{0}: (6, {})} | custom-call | flops 331776 | bytes 2654208 | tf_op jit(solution)/shard_map/last_sums/pallas_call | solution.py:291
  29.3 1.8 %collective-permute-start.7 = (f32[4,128,128]{2,1,0:T(8,128)S(1)}, f32[4,128,128]{2,1,0:T(8,128)S(1)}, u32[]{:S(2)}, u32[]{:S(2)}) collective-permute-start(f32[4,128,128]{2,1,0:T(8,128)S(1)} %get-tuple-element.21), channel_id=1, source_target_pairs={{0,4},{2,6},{4,0},{6,2},{8,12},{10,14},{12,8},{14,10},{16,20},{18,... | collective-permute-start | bytes 786440 | tf_op jit(solution)/shard_map/ppermute | solution.py:58
  31.1 1.6 %collective-permute-start.10 = (f32[4,128,128]{2,1,0:T(8,128)S(1)}, f32[4,128,128]{2,1,0:T(8,128)S(1)}, u32[]{:S(2)}, u32[]{:S(2)}) collective-permute-start(f32[4,128,128]{2,1,0:T(8,128)S(1)} %get-tuple-element.23), channel_id=1, source_target_pairs={{0,8},{2,10},{4,12},{6,14},{8,0},{10,2},{12,4},{14,6},{16,24},{18,... | collective-permute-start | bytes 786440 | tf_op jit(solution)/shard_map/ppermute | solution.py:58
  32.6 5.0 %collective-permute-done.7 = f32[4,128,128]{2,1,0:T(8,128)S(1)} collective-permute-done((f32[4,128,128]{2,1,0:T(8,128)S(1)}, f32[4,128,128]{2,1,0:T(8,128)S(1)}, u32[]{:S(2)}, u32[]{:S(2)}) %collective-permute-start.7) | collective-permute-done | bytes 262176 | tf_op jit(solution)/shard_map/ppermute | solution.py:58
  37.7 1.9 %collective-permute-start.8 = (f32[2,128,128]{2,1,0:T(8,128)S(1)}, f32[2,128,128]{2,1,0:T(8,128)S(1)}, u32[]{:S(2)}, u32[]{:S(2)}) collective-permute-start(f32[2,128,128]{2,1,0:T(8,128)S(1)} %get-tuple-element.27), channel_id=1, source_target_pairs={{0,8},{2,10},{4,12},{6,14},{8,0},{10,2},{12,4},{14,6},{16,24},{18,... | collective-permute-start | bytes 393224 | tf_op jit(solution)/shard_map/ppermute | solution.py:58
  39.6 0.0 collective-permute-done.10
  39.6 1.6 %collective-permute-start.11 = (f32[2,128,128]{2,1,0:T(8,128)S(1)}, f32[2,128,128]{2,1,0:T(8,128)S(1)}, u32[]{:S(2)}, u32[]{:S(2)}) collective-permute-start(f32[2,128,128]{2,1,0:T(8,128)S(1)} %get-tuple-element.25), channel_id=1, source_target_pairs={{0,4},{2,6},{4,0},{6,2},{8,12},{10,14},{12,8},{14,10},{16,20},{18,... | collective-permute-start | bytes 393224 | tf_op jit(solution)/shard_map/ppermute | solution.py:58
  41.2 1.6 %collective-permute-done.8 = f32[2,128,128]{2,1,0:T(8,128)S(1)} collective-permute-done((f32[2,128,128]{2,1,0:T(8,128)S(1)}, f32[2,128,128]{2,1,0:T(8,128)S(1)}, u32[]{:S(2)}, u32[]{:S(2)}) %collective-permute-start.8) | collective-permute-done | bytes 131104 | tf_op jit(solution)/shard_map/ppermute | solution.py:58
  42.8 2.9 %collective-permute-start.9 = (f32[1,128,128]{2,1,0:T(8,128)S(1)}, f32[1,128,128]{2,1,0:T(8,128)S(1)}, u32[]{:S(2)}, u32[]{:S(2)}) collective-permute-start(f32[1,128,128]{2,1,0:T(8,128)S(1)} %get-tuple-element.32), channel_id=1, source_target_pairs={{0,16},{2,18},{4,20},{6,22},{8,24},{10,26},{12,28},{14,30},{16,0},... | collective-permute-start | bytes 196616 | tf_op jit(solution)/shard_map/ppermute | solution.py:58
  45.6 0.0 collective-permute-done.11
  45.6 1.7 %collective-permute-start.12 = (f32[1,128,128]{2,1,0:T(8,128)S(1)}, f32[1,128,128]{2,1,0:T(8,128)S(1)}, u32[]{:S(2)}, u32[]{:S(2)}) collective-permute-start(f32[1,128,128]{2,1,0:T(8,128)S(1)} %get-tuple-element.30), channel_id=1, source_target_pairs={{0,16},{2,18},{4,20},{6,22},{8,24},{10,26},{12,28},{14,30},{16,0},... | collective-permute-start | bytes 196616 | tf_op jit(solution)/shard_map/ppermute | solution.py:58
  47.3 2.6 %collective-permute-done.9.got_low = f32[1,128,128]{2,1,0:T(8,128)S(1)} collective-permute-done((f32[1,128,128]{2,1,0:T(8,128)S(1)}, f32[1,128,128]{2,1,0:T(8,128)S(1)}, u32[]{:S(2)}, u32[]{:S(2)}) %collective-permute-start.9) | collective-permute-done | bytes 65568 | tf_op jit(solution)/shard_map/ppermute | solution.py:58
  49.9 1.0 %collective-permute-done.12.got_high = f32[1,128,128]{2,1,0:T(8,128)S(1)} collective-permute-done((f32[1,128,128]{2,1,0:T(8,128)S(1)}, f32[1,128,128]{2,1,0:T(8,128)S(1)}, u32[]{:S(2)}, u32[]{:S(2)}) %collective-permute-start.12) | collective-permute-done | bytes 65568 | tf_op jit(solution)/shard_map/ppermute | solution.py:58
  50.9 0.7 %finish.1 = f32[256,128]{1,0:T(8,128)} custom-call(f32[1,128,128]{2,1,0:T(8,128)S(1)} %collective-permute-done.9.got_low, f32[1,128,128]{2,1,0:T(8,128)S(1)} %get-tuple-element.31.low, f32[1,128,128]{2,1,0:T(8,128)S(1)} %collective-permute-done.12.got_high, f32[1,128,128]{2,1,0:T(8,128)S(1)} %get-tuple-element.29.high), custom_call_target="tpu_custom_call" | custom-call | flops 16384 | bytes 393216 | tf_op jit(solution)/shard_map/finish/pallas_call | solution.py:355
  (6 shorter events, 0.1 us)
Async XLA Ops:
  0.0 9.1 %copy-start.4 = (s32[2,8]{1,0:T(2,128)S(1)}, s32[2,8]{1,0:T(2,128)}, u32[]{:S(2)}) copy-start(s32[2,8]{1,0:T(2,128)} %refs_0_.1) | copy-start | bytes 196
  0.0 4.7 %collective-permute-start.1 = (s32[2,8,1]{1,2,0:T(1,128)}, s32[2,8,1]{1,2,0:T(1,128)S(1)}, u32[]{:S(2)}, u32[]{:S(2)}) collective-permute-start(s32[2,8,1]{1,2,0:T(1,128)} %param.9), channel_id=1, source_target_pairs={{0,1},{1,0},{2,3},{3,2},{4,5},{5,4},{6,7},{7,6},{8,9},{9,8},{10,11... | collective-permute-start | bytes 200 | tf_op jit(solution)/shard_map/ppermute | solution.py:58
  3.0 3.8 %collective-permute-start = (s32[2,8]{1,0:T(2,128)}, s32[2,8]{1,0:T(2,128)S(1)}, u32[]{:S(2)}, u32[]{:S(2)}) collective-permute-start(s32[2,8]{1,0:T(2,128)} %refs_0_.1), channel_id=1, source_target_pairs={{0,1},{1,0},{2,3},{3,2},{4,5},{5,4},{6,7},{7,6},{8,9},{9,8},{10,11... | collective-permute-start | bytes 200 | tf_op jit(solution)/shard_map/ppermute | solution.py:58
  6.8 1.6 %copy-start = (f32[4096,1,128]{2,1,0:T(1,128)S(1)}, f32[4096,1,128]{2,1,0:T(1,128)}, u32[]{:S(2)}) copy-start(f32[4096,1,128]{2,1,0:T(1,128)} %param.6) | copy-start | bytes 6291460
  8.3 0.7 %copy-start.5 = (s32[2,8,1]{1,2,0:T(1,128)S(1)}, s32[2,8,1]{1,2,0:T(1,128)}, u32[]{:S(2)}) copy-start(s32[2,8,1]{1,2,0:T(1,128)} %param.9) | copy-start | bytes 196
  8.3 7.3 %copy-start.1 = (f32[4096,1,128]{2,1,0:T(1,128)S(1)}, f32[4096,1,128]{2,1,0:T(1,128)}, u32[]{:S(2)}) copy-start(f32[4096,1,128]{2,1,0:T(1,128)} %param.6) | copy-start | bytes 6291460
  8.9 6.7 %copy-start.6 = (s32[2,8]{1,0:T(2,128)S(1)}, s32[2,8]{1,0:T(2,128)}, u32[]{:S(2)}) copy-start(s32[2,8]{1,0:T(2,128)} %lengths_ref.1) | copy-start | bytes 196
  8.9 6.7 %collective-permute-start.2 = (f32[16,32,128]{2,1,0:T(8,128)S(1)}, f32[16,32,128]{2,1,0:T(8,128)S(1)}, u32[]{:S(2)}, u32[]{:S(2)}) collective-permute-start(f32[16,32,128]{2,1,0:T(8,128)S(1)} %gather_rows.1), channel_id=1, source_target_pairs={{0,1},{1,0},{2,3},{3,2},{4,5},{5,4},{6,7},{7,6},{8,9},{9,8},{10,11... | collective-permute-start | bytes 786440 | tf_op jit(solution)/shard_map/ppermute | solution.py:58
  9.1 3.3 %collective-permute-start.3 = (s32[8,8]{1,0:T(8,128)S(1)}, s32[8,8]{1,0:T(8,128)S(1)}, u32[]{:S(2)}, u32[]{:S(2)}) collective-permute-start(s32[8,8]{1,0:T(8,128)S(1)} %pad_add_fusion), channel_id=1, source_target_pairs={{0,2},{2,0},{4,6},{6,4},{8,10},{10,8},{12,14},{14,12},{16,18},{18,... | collective-permute-start | bytes 776 | tf_op jit(solution)/shard_map/ppermute | solution.py:58
  9.2 1.1 %copy-start.2 = (f32[2,3,8,4096]{3,2,1,0:T(8,128)S(1)}, f32[2,3,8,4096]{3,2,1,0:T(8,128)}, u32[]{:S(2)}) copy-start(f32[2,3,8,4096]{3,2,1,0:T(8,128)} %param.7) | copy-start | bytes 2359300
  10.3 1.1 %copy-start.3 = (f32[2,3,8,4096]{3,2,1,0:T(8,128)S(1)}, f32[2,3,8,4096]{3,2,1,0:T(8,128)}, u32[]{:S(2)}) copy-start(f32[2,3,8,4096]{3,2,1,0:T(8,128)} %param.8) | copy-start | bytes 2359300
  20.4 6.4 %collective-permute-start.4 = (f32[16,32,128]{2,1,0:T(8,128)S(1)}, f32[16,32,128]{2,1,0:T(8,128)S(1)}, u32[]{:S(2)}, u32[]{:S(2)}) collective-permute-start(f32[16,32,128]{2,1,0:T(8,128)S(1)} %bitcast.21), channel_id=1, source_target_pairs={{0,1},{1,0},{2,3},{3,2},{4,5},{5,4},{6,7},{7,6},{8,9},{9,8},{10,11... | collective-permute-start | bytes 786440 | tf_op jit(solution)/shard_map/ppermute | solution.py:58
  20.8 6.0 %collective-permute-start.6 = (f32[16,32,128]{2,1,0:T(8,128)S(1)}, f32[16,32,128]{2,1,0:T(8,128)S(1)}, u32[]{:S(2)}, u32[]{:S(2)}) collective-permute-start(f32[16,32,128]{2,1,0:T(8,128)S(1)} %bitcast.22), channel_id=1, source_target_pairs={{0,2},{2,0},{4,6},{6,4},{8,10},{10,8},{12,14},{14,12},{16,18},{18,... | collective-permute-start | bytes 786440 | tf_op jit(solution)/shard_map/ppermute | solution.py:58
  26.8 1.5 %collective-permute-start.5 = (f32[16,32,128]{2,1,0:T(8,128)S(1)}, f32[16,32,128]{2,1,0:T(8,128)S(1)}, u32[]{:S(2)}, u32[]{:S(2)}) collective-permute-start(f32[16,32,128]{2,1,0:T(8,128)S(1)} %collective-permute-done.4.refs_2_), channel_id=1, source_target_pairs={{0,2},{2,0},{4,6},{6,4},{8,10},{10,8},{12,14},{14,12},{16,18},{18,... | collective-permute-start | bytes 786440 | tf_op jit(solution)/shard_map/ppermute | solution.py:58
  29.3 8.4 %collective-permute-start.7 = (f32[4,128,128]{2,1,0:T(8,128)S(1)}, f32[4,128,128]{2,1,0:T(8,128)S(1)}, u32[]{:S(2)}, u32[]{:S(2)}) collective-permute-start(f32[4,128,128]{2,1,0:T(8,128)S(1)} %get-tuple-element.21), channel_id=1, source_target_pairs={{0,4},{2,6},{4,0},{6,2},{8,12},{10,14},{12,8},{14,10},{16,20},{18,... | collective-permute-start | bytes 786440 | tf_op jit(solution)/shard_map/ppermute | solution.py:58
  31.1 8.5 %collective-permute-start.10 = (f32[4,128,128]{2,1,0:T(8,128)S(1)}, f32[4,128,128]{2,1,0:T(8,128)S(1)}, u32[]{:S(2)}, u32[]{:S(2)}) collective-permute-start(f32[4,128,128]{2,1,0:T(8,128)S(1)} %get-tuple-element.23), channel_id=1, source_target_pairs={{0,8},{2,10},{4,12},{6,14},{8,0},{10,2},{12,4},{14,6},{16,24},{18,... | collective-permute-start | bytes 786440 | tf_op jit(solution)/shard_map/ppermute | solution.py:58
  37.7 5.0 %collective-permute-start.8 = (f32[2,128,128]{2,1,0:T(8,128)S(1)}, f32[2,128,128]{2,1,0:T(8,128)S(1)}, u32[]{:S(2)}, u32[]{:S(2)}) collective-permute-start(f32[2,128,128]{2,1,0:T(8,128)S(1)} %get-tuple-element.27), channel_id=1, source_target_pairs={{0,8},{2,10},{4,12},{6,14},{8,0},{10,2},{12,4},{14,6},{16,24},{18,... | collective-permute-start | bytes 393224 | tf_op jit(solution)/shard_map/ppermute | solution.py:58
  39.6 6.0 %collective-permute-start.11 = (f32[2,128,128]{2,1,0:T(8,128)S(1)}, f32[2,128,128]{2,1,0:T(8,128)S(1)}, u32[]{:S(2)}, u32[]{:S(2)}) collective-permute-start(f32[2,128,128]{2,1,0:T(8,128)S(1)} %get-tuple-element.25), channel_id=1, source_target_pairs={{0,4},{2,6},{4,0},{6,2},{8,12},{10,14},{12,8},{14,10},{16,20},{18,... | collective-permute-start | bytes 393224 | tf_op jit(solution)/shard_map/ppermute | solution.py:58
  42.8 7.1 %collective-permute-start.9 = (f32[1,128,128]{2,1,0:T(8,128)S(1)}, f32[1,128,128]{2,1,0:T(8,128)S(1)}, u32[]{:S(2)}, u32[]{:S(2)}) collective-permute-start(f32[1,128,128]{2,1,0:T(8,128)S(1)} %get-tuple-element.32), channel_id=1, source_target_pairs={{0,16},{2,18},{4,20},{6,22},{8,24},{10,26},{12,28},{14,30},{16,0},... | collective-permute-start | bytes 196616 | tf_op jit(solution)/shard_map/ppermute | solution.py:58
  45.6 5.2 %collective-permute-start.12 = (f32[1,128,128]{2,1,0:T(8,128)S(1)}, f32[1,128,128]{2,1,0:T(8,128)S(1)}, u32[]{:S(2)}, u32[]{:S(2)}) collective-permute-start(f32[1,128,128]{2,1,0:T(8,128)S(1)} %get-tuple-element.30), channel_id=1, source_target_pairs={{0,16},{2,18},{4,20},{6,22},{8,24},{10,26},{12,28},{14,30},{16,0},... | collective-permute-start | bytes 196616 | tf_op jit(solution)/shard_map/ppermute | solution.py:58

commit v4 on v3

--- a/solution.py
+++ b/solution.py
@@ -6,6 +6,7 @@
 from jax.experimental import pallas as pl
 from jax.experimental.pallas import tpu as pltpu
 from jax.sharding import PartitionSpec as P
+
 
 LY = 64
 LZ = 8
@@ -28,7 +29,7 @@
 LIMIT = 16 << 20
 
 
-def call(body, name, out, in_specs, work, moved, **kwargs):
+def call(body, out, in_specs, work, moved, **kwargs):
     return pl.pallas_call(
         body,
         out_shape=out,
@@ -36,7 +37,6 @@
         out_specs=jax.tree.map(lambda _: VMEM, out),
         compiler_params=pltpu.CompilerParams(vmem_limit_bytes=LIMIT),
         cost_estimate=pl.CostEstimate(flops=work, bytes_accessed=moved, transcendentals=0),
-        name=name,
         **kwargs,
     )
 
@@ -67,7 +67,7 @@
 
 def gather_rows(starts, block):
     out = floats(starts.size, TILE, LANES)
-    return call(gather_body, "gather_rows", out, [SMEM, VMEM], 0, 8 * out.size)(starts, block)
+    return call(gather_body, out, [SMEM, VMEM], 0, 8 * out.size)(starts, block)
 
 
 def low_half():
@@ -105,13 +105,13 @@
 def prepare(source, observed):
     out = floats(3, LZ, PACKED, SUB, LANES)
     return call(
-        prepare_body, "prepare", (out, out), [VMEM, VMEM], 8 * source.size, 16 * source.size
+        prepare_body, (out, out), [VMEM, VMEM], 8 * source.size, 16 * source.size
     )(by_rows(source), by_rows(observed))
 
 
 def fields_body(
-    starts_ref, owners_ref, lengths_ref, table_ref, answer_ref, source_ref, observed_ref, out_ref,
-    field, adjoint, right, curl, scale, decay, weight,
+    starts_ref, owners_ref, lengths_ref, table_ref, answer_ref, source_ref, observed_ref, kept_ref,
+    given_ref, field, adjoint, right, curl, scale, decay, weight,
 ):
     me = lax.axis_index("mdl")
     lane = lax.broadcasted_iota(jnp.int32, (SUB, LANES), 1)
@@ -207,8 +207,11 @@
 
         for j in range(PARTS):
             first, second = pack(partial(2 * j), partial(2 * j + 1), low)
-            out_ref[pl.ds(z * TILE + j, SUB, stride=PARTS), :] = first
-            out_ref[pl.ds((LZ + z) * TILE + j, SUB, stride=PARTS), :] = second
+            for sounding, value in enumerate((first, second)):
+                mine = jnp.full((SUB, LANES), owners_ref[sounding, z] == me)
+                place = pl.ds((sounding * LZ + z) * TILE + j, SUB, stride=PARTS)
+                kept_ref[place, :] = jnp.where(mine, value, 0.0)
+                given_ref[place, :] = jnp.where(mine, 0.0, value)
 
 
 def soundings_partial(starts, owners, lengths, table, answer, source, observed):
@@ -216,12 +219,13 @@
     planes = pltpu.VMEM((3, LZ, PACKED, SUB, LANES), jnp.float32)
     single = pltpu.VMEM((LZ, PACKED, SUB, LANES), jnp.float32)
     cells = tiles * TILE * LANES
-    out = call(
-        fields_body, "soundings_partial", floats(tiles * TILE, LANES),
+    out = floats(tiles * TILE, LANES)
+    kept, given = call(
+        fields_body, (out, out),
         [SMEM] * 3 + [VMEM] * 4, 500 * cells, 40 * cells,
         scratch_shapes=[planes] * 4 + [single] * 3,
     )(starts, owners, lengths, table, answer.reshape(tiles * TILE, LANES), source, observed)
-    return out.reshape(tiles, TILE, LANES)
+    return kept.reshape(tiles, TILE, LANES), given.reshape(tiles, TILE, LANES)
 
 
 def arranged(order):
@@ -231,22 +235,21 @@
     return [slot | (1 << order[0]) for slot in rest] + rest
 
 
-def add_terms(starts_ref, owners_ref, terms_ref, total, share, slots):
-    owner, me = lax.axis_index("mdl"), lax.axis_index("grp")
+def add_terms(starts_ref, terms_ref, total, share, slots):
+    me = lax.axis_index("grp")
     span, wide = share + 2 * TILE, starts_ref.shape[1]
     for tile in range(terms_ref.shape[0]):
         start = starts_ref[tile // wide, tile % wide]
         first = lax.div(start, share)
         target = first + ((first ^ me) & 1)
         where = start - target * share
-        wanted = (owners_ref[tile // wide, tile % wide] == owner) & (where > -TILE)
         base = ((target >> 1) ^ (me >> 1)) * span + TILE + where
-        base = jnp.where(wanted, base, slots * span)
+        base = jnp.where(where > -TILE, base, slots * span)
         total[pl.ds(base, TILE), :] += terms_ref[tile]
 
 
 def first_body(groups, count, *refs):
-    model_ref, total = refs[3 * count], refs[-1]
+    model_ref, total = refs[2 * count], refs[-1]
     me = lax.axis_index("grp")
     share = model_ref.shape[0] // groups
     total[...] = jnp.zeros_like(total)
@@ -256,25 +259,25 @@
     right = jnp.where(lane == LANES - 1, local, pltpu.roll(local, LANES - 1, 1))
     total[TILE : TILE + share, :] = BETA * (2.0 * local - left - right)
     for i in range(count):
-        add_terms(*refs[3 * i : 3 * i + 3], total, share, groups // 2)
+        add_terms(*refs[2 * i : 2 * i + 2], total, share, groups // 2)
 
 
 def first_sums(groups_of, block):
     groups = lax.axis_size("grp")
     share = block.shape[0] // groups
     out = floats(groups // 2 * (share + 2 * TILE) + TILE, LANES)
-    flat = [a for triple in groups_of for a in triple]
+    flat = [a for pair in groups_of for a in pair]
     return call(
-        functools.partial(first_body, groups, len(groups_of)), "first_sums", out,
-        [SMEM, SMEM, VMEM] * len(groups_of) + [VMEM], out.size, 8 * out.size,
+        functools.partial(first_body, groups, len(groups_of)), out,
+        [SMEM, VMEM] * len(groups_of) + [VMEM], out.size, 8 * out.size,
     )(*flat, block)
 
 
 def last_body(orders, groups, share, count, *refs):
-    total, outs = refs[3 * count + 1], refs[3 * count + 2 :]
+    total, outs = refs[2 * count + 1], refs[2 * count + 2 :]
     span, slots, half = share + 2 * TILE, groups // 2, share // 2
     for i in range(count):
-        add_terms(*refs[3 * i : 3 * i + 3], total, share, slots)
+        add_terms(*refs[2 * i : 2 * i + 2], total, share, slots)
     for which, order in enumerate(orders):
         for place, slot in enumerate(arranged(order)):
             out = outs[2 * which + (place * 2 >= slots)]
@@ -286,38 +289,81 @@
     groups = lax.axis_size("grp")
     share, slots = rows // groups, groups // 2
     out = floats(slots // 2, share // 2, LANES)
-    flat = [a for triple in groups_of for a in triple]
+    flat = [a for pair in groups_of for a in pair]
     count = len(groups_of)
     return call(
-        functools.partial(last_body, orders, groups, share, count), "last_sums",
-        (floats(*total.shape),) + (out,) * 4, [SMEM, SMEM, VMEM] * count + [VMEM],
-        total.size, 8 * total.size, input_output_aliases={3 * count: 0},
+        functools.partial(last_body, orders, groups, share, count),
+        (floats(*total.shape),) + (out,) * 4, [SMEM, VMEM] * count + [VMEM],
+        total.size, 8 * total.size, input_output_aliases={2 * count: 0},
     )(*flat, total)[1:]
 
 
-def finish_body(got_low, low, got_high, high, out_ref):
-    half = out_ref.shape[0] // 2
-    out_ref[:half] = got_low[0] + low[0]
-    out_ref[half:] = got_high[0] + high[0]
+def join_body(got_low, low, got_high, high, give_ref, keep_ref):
+    cut = low.shape[0] // 2
+    for half, (got, held) in enumerate(((got_low, low), (got_high, high))):
+        give_ref[half] = got[:cut] + held[:cut]
+        keep_ref[half] = got[cut:] + held[cut:]
+
+
+def finish_body(got, held, out_ref):
+    out_ref[...] = got[...] + held[...]
+
+
+def halve(low_give, low, high_give, high, orders):
+    bit_pairs = list(zip(*orders))
+    for step, (low_bit, high_bit) in enumerate(bit_pairs[:2]):
+        got_low = swap_over("grp", 2 << low_bit)(low_give)
+        got_high = swap_over("grp", 2 << high_bit)(high_give)
+        cut = low.shape[0] // 2
+        if step == 0:
+            low_give, low = got_low[:cut] + low[:cut], got_low[cut:] + low[cut:]
+            high_give, high = got_high[:cut] + high[:cut], got_high[cut:] + high[cut:]
+    out = floats(2, cut, *low.shape[1:])
+    give, keep = call(
+        join_body, (out, out), [VMEM] * 4, low.size, 24 * low.size
+    )(got_low, low, got_high, high)
+    for bit, _ in bit_pairs[2:]:
+        got = swap_over("grp", 2 << bit)(give)
+        cut = keep.shape[1] // 2
+        if cut:
+            give, keep = got[:, :cut] + keep[:, :cut], got[:, cut:] + keep[:, cut:]
+    return call(finish_body, floats(*keep.shape), [VMEM] * 2, keep.size, 12 * keep.size)(got, keep)
+
+
+def hold_body(block_ref, out_ref, sem):
+    copy = pltpu.make_async_copy(block_ref, out_ref, sem)
+    copy.start()
+    copy.wait()
+
+
+def hold(block):
+    return call(
+        hold_body, floats(*block.shape), [pl.BlockSpec(memory_space=pltpu.HBM)], 0,
+        8 * block.size, scratch_shapes=[pltpu.SemaphoreType.DMA],
+    )(block)
 
 
 def per_device(model, source, observed, owner_ids, offsets, lengths):
     rows, owners_count, groups = model.shape[0], lax.axis_size("mdl"), lax.axis_size("grp")
-    block = model.reshape(rows, LANES)
     tiles = source.shape[0] * LZ
     across, beside = swap_over("mdl", 1), swap_over("grp", 1)
+    block = hold(model.reshape(rows, LANES))
+    source, observed = prepare(source, observed)
     if owners_count == 2:
-        asked, asked_ids = lax.optimization_barrier((across(offsets), across(owner_ids)))
-        owners, asked_owners = (ids.reshape(offsets.shape) for ids in (owner_ids, asked_ids))
-        source, observed = prepare(source, observed)
-        answer = across(gather_rows(asked, block))
-        told = beside(jnp.concatenate([offsets, owners, asked, asked_owners]))
+        asked = across(offsets)
+        asked, block = lax.optimization_barrier((asked, block))
+        given = gather_rows(asked, block)
+        answer = across(given)
+        told = beside(jnp.concatenate([offsets, asked]))
         answer, told = lax.optimization_barrier((answer, told))
-        told = told.reshape(4, *offsets.shape)
-        terms = soundings_partial(offsets, owners, lengths, block, answer, source, observed)
-        others = across(terms)
-        total = first_sums([(offsets, owners, terms), (told[0], told[1], beside(terms))], block)
-        final = [(asked, asked_owners, others), (told[2], told[3], beside(others))]
+        told = told.reshape(2, *offsets.shape)
+        kept, given = soundings_partial(
+            offsets, owner_ids.reshape(offsets.shape), lengths, block, answer, source, observed
+        )
+        others = across(given)
+        kept_beside = beside(kept)
+        total = first_sums([(offsets, kept), (told[0], kept_beside)], block)
+        final = [(asked, others), (told[1], beside(others))]
     else:
         capacity = max(4, 2 * tiles // owners_count)
         places = place_slots(owner_ids.reshape(tiles), owners_count, capacity)
@@ -328,34 +374,22 @@
             offsets.reshape(tiles)
         )
         asked = swap(request.reshape(owners_count, capacity))
-        source, observed = prepare(source, observed)
         given = gather_rows(asked, block).reshape(owners_count, capacity, TILE, LANES)
         fetched = swap(given).reshape(owners_count * capacity * TILE, LANES)
-        mine = jnp.full_like(asked, lax.axis_index("mdl"))
-        terms = soundings_partial(
+        terms, _ = soundings_partial(
             (places * TILE).reshape(offsets.shape), jnp.full_like(offsets, lax.axis_index("mdl")),
             lengths, fetched, jnp.zeros((tiles, TILE, LANES), jnp.float32), source, observed,
         )
         outgoing = jnp.zeros((owners_count * capacity, TILE, LANES), jnp.float32)
         outgoing = outgoing.at[places].set(terms).reshape(owners_count, capacity, TILE, LANES)
         arrived = swap(outgoing).reshape(owners_count * capacity, TILE, LANES)
-        total = first_sums([(asked, mine, arrived)], block)
-        final = [(beside(asked), mine, beside(arrived))]
+        total = first_sums([(asked, arrived)], block)
+        final = [(beside(asked), beside(arrived))]
 
     bits = tuple(range(groups.bit_length() - 2))
     orders = (bits, bits[1:2] + bits[0:1] + bits[2:])
-    low_give, low, high_give, high = last_sums(final, total, rows, orders)
-    for low_bit, high_bit in zip(*orders):
-        got_low = swap_over("grp", 2 << low_bit)(low_give)
-        got_high = swap_over("grp", 2 << high_bit)(high_give)
-        cut = low.shape[0] // 2
-        if cut:
-            low_give, low = got_low[:cut] + low[:cut], got_low[cut:] + low[cut:]
-            high_give, high = got_high[:cut] + high[:cut], got_high[cut:] + high[cut:]
-    out = call(
-        finish_body, "finish", floats(rows // groups, LANES), [VMEM] * 4, low.size, 24 * low.size
-    )(got_low, low, got_high, high)
-    return out[:, None, :]
+    sums = halve(*last_sums(final, total, rows, orders), orders)
+    return sums.reshape(rows // groups, 1, LANES)
 
 
 def solution(mesh):
@@ -367,6 +401,7 @@
         P(("grp", "mdl"), None),
         P(("grp", "mdl"), None),
     )
+
     return jax.shard_map(
         per_device, mesh=mesh, in_specs=placed, out_specs=P("grp", "mdl", None), check_vma=False
     )

time: 51.8 us -> 50.1 us (0.967)
  local copies, waits for them, and re-layouts: 3.87 us -> 1.63 us
  waiting for transfers between devices: 23.7 us -> 25 us
  starting transfers between devices: 15 us -> 14.3 us
    unnamed x14 -> x12, local copies, waits for them, and re-layouts: 3.87 us -> 1.62 us
    ppermute x13 -> x11, waiting for transfers between devices: 23.7 us -> 25 us  [swap_over(): return lambda value: lax.ppermute(value, axis, ring)]
    ppermute x13 -> x11, starting transfers between devices: 15 us -> 14.3 us  [swap_over(): return lambda value: lax.ppermute(value, axis, ring)]
    pallas_call x6 -> x8, Pallas kernels: 8.79 us -> 8.81 us  [the longest x1 4.76 us: soundings_partial(): call(fields_body, (out, out), [SMEM] * 3 + [VMEM] * 4, 500 * cells, 40 *...]
  transfers between devices with their start and end apart: 13 -> 11, of which waited for: 9 -> 8; matrix products, arithmetic and copies ran while one was open for 0% -> 0% of each run, Pallas kernels for 4% -> 4%
where the time goes in v4:
time: 50.1 us; the launch traced here: 50 us
  waiting for transfers between devices  25 us (50%)
  starting transfers between devices  14.3 us (29%)
  Pallas kernels  8.81 us (18%)
  local copies, waits for them, and re-layouts  1.63 us (3%)
    ppermute x11, waiting for transfers between devices, swap_over(): return lambda value: lax.ppermute(value, axis, ring)  25 us
    ppermute x11, starting transfers between devices, swap_over(): return lambda value: lax.ppermute(value, axis, ring)  14.3 us
    pallas_call x1, Pallas kernels, soundings_partial(): call(fields_body, (out, out), [SMEM] * 3 + [VMEM] * 4, 500 * cells, 40 *...  4.76 us
    unnamed x12, local copies, waits for them, and re-layouts  1.62 us
  transfers between devices with their start and end apart: 11, of which 8 were waited for; matrix products, arithmetic and copies ran while one was open for 0% of the time, Pallas kernels for 4%

profile of v4, /device:TPU:0, one launch (start us, length us, event | category | flops | bytes accessed | tf_op | source)
XLA Modules:
  0.0 50.0 jit_solution(10738585149258260369)
XLA Ops:
  0.0 3.0 %collective-permute-start = (s32[2,8]{1,0:T(2,128)}, s32[2,8]{1,0:T(2,128)S(1)}, u32[]{:S(2)}, u32[]{:S(2)}) collective-permute-start(s32[2,8]{1,0:T(2,128)} %refs_0_.1), channel_id=1, source_target_pairs={{0,1},{1,0},{2,3},{3,2},{4,5},{5,4},{6,7},{7,6},{8,9},{9,8},{10,11... | collective-permute-start | bytes 200 | tf_op jit(solution)/shard_map/ppermute | solution.py:58
  3.0 0.0 copy-start
  3.0 1.6 %copy-done = f32[4096,1,128]{2,1,0:T(1,128)S(1)} copy-done((f32[4096,1,128]{2,1,0:T(1,128)S(1)}, f32[4096,1,128]{2,1,0:T(1,128)}, u32[]{:S(2)}) %copy-start) | copy-done | bytes 2097176
  4.6 0.1 shard_map.64.block_ref.table_ref.refs_4_
  4.7 0.0 copy-start.3
  4.7 0.0 copy-start.1
  4.7 0.0 copy-start.2
  4.8 0.0 copy-start.4
  4.8 0.0 copy-start.5
  4.8 0.0 collective-permute-done.starts_ref.refs_0_
  4.8 0.6 %shard_map.65 = f32[16,32,128]{2,1,0:T(8,128)S(1)} custom-call(s32[2,8]{1,0:T(2,128)S(1)} %collective-permute-done.starts_ref.refs_0_, f32[4096,128]{1,0:T(8,128)S(1)} %shard_map.64.block_ref.table_ref.refs_4_), custom_call_target="tpu_custom_call" | custom-call | bytes 524288 | tf_op jit(solution)/shard_map/pallas_call | solution.py:70
  5.4 2.0 %collective-permute-start.1 = (f32[16,32,128]{2,1,0:T(8,128)S(1)}, f32[16,32,128]{2,1,0:T(8,128)S(1)}, u32[]{:S(2)}, u32[]{:S(2)}) collective-permute-start(f32[16,32,128]{2,1,0:T(8,128)S(1)} %shard_map.65), channel_id=1, source_target_pairs={{0,1},{1,0},{2,3},{3,2},{4,5},{5,4},{6,7},{7,6},{8,9},{9,8},{10,11... | collective-permute-start | bytes 786440 | tf_op jit(solution)/shard_map/ppermute | solution.py:58
  7.4 0.0 copy-done.3
  7.4 0.1 collective-permute-start.2
  7.5 0.0 copy-done.1
  7.5 0.0 copy-done.2
  7.5 0.9 %shard_map.66 = (f32[3,8,8,8,128]{4,3,2,1,0:T(8,128)S(1)}, f32[3,8,8,8,128]{4,3,2,1,0:T(8,128)S(1)}) custom-call(f32[1536,128]{1,0:T(8,128)S(1)} %bitcast.19, f32[1536,128]{1,0:T(8,128)S(1)} %bitcast.20), custom_call_target="tpu_custom_call" | custom-call | flops 1572864 | bytes 3145728 | tf_op jit(solution)/shard_map/pallas_call | solution.py:107
  8.5 0.2 collective-permute-done.2
  8.6 4.6 %collective-permute-done.1 = f32[16,32,128]{2,1,0:T(8,128)S(1)} collective-permute-done((f32[16,32,128]{2,1,0:T(8,128)S(1)}, f32[16,32,128]{2,1,0:T(8,128)S(1)}, u32[]{:S(2)}, u32[]{:S(2)}) %collective-permute-start.1) | collective-permute-done | bytes 262176 | tf_op jit(solution)/shard_map/ppermute | solution.py:58
  13.2 0.0 copy-done.4
  13.2 0.0 copy-done.5
  13.2 4.8 %shard_map.67 = (f32[512,128]{1,0:T(8,128)S(1)}, f32[512,128]{1,0:T(8,128)S(1)}) custom-call(s32[2,8]{1,0:T(2,128)S(1)} %copy-done.3, s32[2,8]{1,0:T(2,128)S(1)} %bitcast.24, s32[2,8]{1,0:T(2,128)S(1)} %copy-done.5, f32[4096,128]{1,0:T(8,128)S(1)} %shard_map.64.block_ref.table_ref.refs_4_, f32[512,128]{1,0:T(8,128)S(1)} %bitcast.23, ...), custom_call_target="tpu_custom_call" | custom-call | flops 32768000 | bytes 2621440 | tf_op jit(solution)/shard_map/pallas_call | solution.py:223
  18.0 1.2 %collective-permute-start.3 = (f32[16,32,128]{2,1,0:T(8,128)S(1)}, f32[16,32,128]{2,1,0:T(8,128)S(1)}, u32[]{:S(2)}, u32[]{:S(2)}) collective-permute-start(f32[16,32,128]{2,1,0:T(8,128)S(1)} %bitcast.25), channel_id=1, source_target_pairs={{0,1},{1,0},{2,3},{3,2},{4,5},{5,4},{6,7},{7,6},{8,9},{9,8},{10,11... | collective-permute-start | bytes 786440 | tf_op jit(solution)/shard_map/ppermute | solution.py:58
  19.1 0.0 collective-permute-start.5
  19.1 5.8 %collective-permute-done.3.refs_1_ = f32[16,32,128]{2,1,0:T(8,128)S(1)} collective-permute-done((f32[16,32,128]{2,1,0:T(8,128)S(1)}, f32[16,32,128]{2,1,0:T(8,128)S(1)}, u32[]{:S(2)}, u32[]{:S(2)}) %collective-permute-start.3) | collective-permute-done | bytes 262176 | tf_op jit(solution)/shard_map/ppermute | solution.py:58
  24.9 0.0 collective-permute-start.4
  25.0 0.0 collective-permute-done.5.refs_3_
  25.0 0.9 %shard_map.68.refs_4_ = f32[2592,128]{1,0:T(8,128)S(1)} custom-call(s32[2,8]{1,0:T(2,128)S(1)} %copy-done.3, f32[16,32,128]{2,1,0:T(8,128)S(1)} %bitcast.22, s32[2,8]{1,0:T(2,128)S(1)} %get-tuple-element.37.refs_2_, f32[16,32,128]{2,1,0:T(8,128)S(1)} %collective-permute-done.5.refs_3_, f32[4096,128]{1,0:T(8,128)S(1)} %shard_map.64.block_ref.table_ref.refs_4_), custom_call_target="tpu_custom_call" | custom-call | flops 331776 | bytes 2654208 | tf_op jit(solution)/shard_map/pallas_call | solution.py:270
  25.8 0.6 %collective-permute-done.4.refs_3_ = f32[16,32,128]{2,1,0:T(8,128)S(1)} collective-permute-done((f32[16,32,128]{2,1,0:T(8,128)S(1)}, f32[16,32,128]{2,1,0:T(8,128)S(1)}, u32[]{:S(2)}, u32[]{:S(2)}) %collective-permute-start.4) | collective-permute-done | bytes 262176 | tf_op jit(solution)/shard_map/ppermute | solution.py:58
  26.5 0.8 %shard_map.69 = (f32[2592,128]{1,0:T(8,128)S(1)}, f32[4,128,128]{2,1,0:T(8,128)S(1)}, f32[4,128,128]{2,1,0:T(8,128)S(1)}, f32[4,128,128]{2,1,0:T(8,128)S(1)}, f32[4,128,128]{2,1,0:T(8,128)S(1)}) custom-call(s32[2,8]{1,0:T(2,128)S(1)} %collective-permute-done.starts_ref.refs_0_, ...), custom_call_target="tpu_custom_call", output_to_operand_aliasing={{0}: (4, {})} | custom-call | flops 331776 | bytes 2654208 | tf_op jit(solution)/shard_map/pallas_call | solution.py:294
  27.3 1.2 %collective-permute-start.8 = (f32[4,128,128]{2,1,0:T(8,128)S(1)}, f32[4,128,128]{2,1,0:T(8,128)S(1)}, u32[]{:S(2)}, u32[]{:S(2)}) collective-permute-start(f32[4,128,128]{2,1,0:T(8,128)S(1)} %get-tuple-element.29), channel_id=1, source_target_pairs={{0,8},{2,10},{4,12},{6,14},{8,0},{10,2},{12,4},{14,6},{16,24},{18,... | collective-permute-start | bytes 786440 | tf_op jit(solution)/shard_map/ppermute | solution.py:58
  28.5 1.5 %collective-permute-start.6 = (f32[4,128,128]{2,1,0:T(8,128)S(1)}, f32[4,128,128]{2,1,0:T(8,128)S(1)}, u32[]{:S(2)}, u32[]{:S(2)}) collective-permute-start(f32[4,128,128]{2,1,0:T(8,128)S(1)} %get-tuple-element.27), channel_id=1, source_target_pairs={{0,4},{2,6},{4,0},{6,2},{8,12},{10,14},{12,8},{14,10},{16,20},{18,... | collective-permute-start | bytes 786440 | tf_op jit(solution)/shard_map/ppermute | solution.py:58
  30.0 5.7 %collective-permute-done.8 = f32[4,128,128]{2,1,0:T(8,128)S(1)} collective-permute-done((f32[4,128,128]{2,1,0:T(8,128)S(1)}, f32[4,128,128]{2,1,0:T(8,128)S(1)}, u32[]{:S(2)}, u32[]{:S(2)}) %collective-permute-start.8) | collective-permute-done | bytes 262176 | tf_op jit(solution)/shard_map/ppermute | solution.py:58
  35.8 1.1 %collective-permute-start.9 = (f32[2,128,128]{2,1,0:T(8,128)S(1)}, f32[2,128,128]{2,1,0:T(8,128)S(1)}, u32[]{:S(2)}, u32[]{:S(2)}) collective-permute-start(f32[2,128,128]{2,1,0:T(8,128)S(1)} %get-tuple-element.34), channel_id=1, source_target_pairs={{0,4},{2,6},{4,0},{6,2},{8,12},{10,14},{12,8},{14,10},{16,20},{18,... | collective-permute-start | bytes 393224 | tf_op jit(solution)/shard_map/ppermute | solution.py:58
  36.9 0.0 collective-permute-done.6
  36.9 1.6 %collective-permute-start.7 = (f32[2,128,128]{2,1,0:T(8,128)S(1)}, f32[2,128,128]{2,1,0:T(8,128)S(1)}, u32[]{:S(2)}, u32[]{:S(2)}) collective-permute-start(f32[2,128,128]{2,1,0:T(8,128)S(1)} %get-tuple-element.36), channel_id=1, source_target_pairs={{0,8},{2,10},{4,12},{6,14},{8,0},{10,2},{12,4},{14,6},{16,24},{18,... | collective-permute-start | bytes 393224 | tf_op jit(solution)/shard_map/ppermute | solution.py:58
  38.6 2.2 %collective-permute-done.9.got_high = f32[2,128,128]{2,1,0:T(8,128)S(1)} collective-permute-done((f32[2,128,128]{2,1,0:T(8,128)S(1)}, f32[2,128,128]{2,1,0:T(8,128)S(1)}, u32[]{:S(2)}, u32[]{:S(2)}) %collective-permute-start.9) | collective-permute-done | bytes 131104 | tf_op jit(solution)/shard_map/ppermute | solution.py:58
  40.8 1.2 %collective-permute-done.7.got_low = f32[2,128,128]{2,1,0:T(8,128)S(1)} collective-permute-done((f32[2,128,128]{2,1,0:T(8,128)S(1)}, f32[2,128,128]{2,1,0:T(8,128)S(1)}, u32[]{:S(2)}, u32[]{:S(2)}) %collective-permute-start.7) | collective-permute-done | bytes 131104 | tf_op jit(solution)/shard_map/ppermute | solution.py:58
  42.0 2.7 %collective-permute-start.10 = (f32[2,1,128,128]{3,2,1,0:T(8,128)S(1)}, f32[2,1,128,128]{3,2,1,0:T(8,128)S(1)}, u32[]{:S(2)}, u32[]{:S(2)}) collective-permute-start(f32[2,1,128,128]{3,2,1,0:T(8,128)S(1)} %get-tuple-element.31), channel_id=1, source_target_pairs={{0,16},{2,18},{4,20},{6,22},{8,24},{10,26},{12,28},{14,30},{16,0},... | collective-permute-start | bytes 393224 | tf_op jit(solution)/shard_map/ppermute | solution.py:58
  44.6 4.7 %collective-permute-done.10.got = f32[2,1,128,128]{3,2,1,0:T(8,128)S(1)} collective-permute-done((f32[2,1,128,128]{3,2,1,0:T(8,128)S(1)}, f32[2,1,128,128]{3,2,1,0:T(8,128)S(1)}, u32[]{:S(2)}, u32[]{:S(2)}) %collective-permute-start.10) | collective-permute-done | bytes 131104 | tf_op jit(solution)/shard_map/ppermute | solution.py:58
  49.3 0.7 %shard_map.71 = f32[2,1,128,128]{3,2,1,0:T(8,128)} custom-call(f32[2,1,128,128]{3,2,1,0:T(8,128)S(1)} %collective-permute-done.10.got, f32[2,1,128,128]{3,2,1,0:T(8,128)S(1)} %get-tuple-element.32.held), custom_call_target="tpu_custom_call" | custom-call | flops 32768 | bytes 393216 | tf_op jit(solution)/shard_map/pallas_call | solution.py:330
  (5 shorter events, 0.1 us)
Async XLA Ops:
  0.0 4.8 %collective-permute-start = (s32[2,8]{1,0:T(2,128)}, s32[2,8]{1,0:T(2,128)S(1)}, u32[]{:S(2)}, u32[]{:S(2)}) collective-permute-start(s32[2,8]{1,0:T(2,128)} %refs_0_.1), channel_id=1, source_target_pairs={{0,1},{1,0},{2,3},{3,2},{4,5},{5,4},{6,7},{7,6},{8,9},{9,8},{10,11... | collective-permute-start | bytes 200 | tf_op jit(solution)/shard_map/ppermute | solution.py:58
  3.0 1.6 %copy-start = (f32[4096,1,128]{2,1,0:T(1,128)S(1)}, f32[4096,1,128]{2,1,0:T(1,128)}, u32[]{:S(2)}) copy-start(f32[4096,1,128]{2,1,0:T(1,128)} %param.6) | copy-start | bytes 6291460
  4.7 2.7 %copy-start.3 = (s32[2,8]{1,0:T(2,128)S(1)}, s32[2,8]{1,0:T(2,128)}, u32[]{:S(2)}) copy-start(s32[2,8]{1,0:T(2,128)} %refs_0_.1) | copy-start | bytes 196
  4.7 2.8 %copy-start.1 = (f32[2,3,8,4096]{3,2,1,0:T(8,128)S(1)}, f32[2,3,8,4096]{3,2,1,0:T(8,128)}, u32[]{:S(2)}) copy-start(f32[2,3,8,4096]{3,2,1,0:T(8,128)} %param.7) | copy-start | bytes 2359300
  4.7 2.8 %copy-start.2 = (f32[2,3,8,4096]{3,2,1,0:T(8,128)S(1)}, f32[2,3,8,4096]{3,2,1,0:T(8,128)}, u32[]{:S(2)}) copy-start(f32[2,3,8,4096]{3,2,1,0:T(8,128)} %param.8) | copy-start | bytes 2359300
  4.8 8.4 %copy-start.4 = (s32[2,8,1]{1,2,0:T(1,128)S(1)}, s32[2,8,1]{1,2,0:T(1,128)}, u32[]{:S(2)}) copy-start(s32[2,8,1]{1,2,0:T(1,128)} %param.9) | copy-start | bytes 196
  4.8 8.4 %copy-start.5 = (s32[2,8]{1,0:T(2,128)S(1)}, s32[2,8]{1,0:T(2,128)}, u32[]{:S(2)}) copy-start(s32[2,8]{1,0:T(2,128)} %lengths_ref.1) | copy-start | bytes 196
  5.4 7.8 %collective-permute-start.1 = (f32[16,32,128]{2,1,0:T(8,128)S(1)}, f32[16,32,128]{2,1,0:T(8,128)S(1)}, u32[]{:S(2)}, u32[]{:S(2)}) collective-permute-start(f32[16,32,128]{2,1,0:T(8,128)S(1)} %shard_map.65), channel_id=1, source_target_pairs={{0,1},{1,0},{2,3},{3,2},{4,5},{5,4},{6,7},{7,6},{8,9},{9,8},{10,11... | collective-permute-start | bytes 786440 | tf_op jit(solution)/shard_map/ppermute | solution.py:58
  7.4 1.2 %collective-permute-start.2 = (s32[4,8]{1,0:T(4,128)S(1)}, s32[4,8]{1,0:T(4,128)S(1)}, u32[]{:S(2)}, u32[]{:S(2)}) collective-permute-start(s32[4,8]{1,0:T(4,128)S(1)} %pad_add_fusion), channel_id=1, source_target_pairs={{0,2},{2,0},{4,6},{6,4},{8,10},{10,8},{12,14},{14,12},{16,18},{18,... | collective-permute-start | bytes 392 | tf_op jit(solution)/shard_map/ppermute | solution.py:58
  18.0 7.0 %collective-permute-start.3 = (f32[16,32,128]{2,1,0:T(8,128)S(1)}, f32[16,32,128]{2,1,0:T(8,128)S(1)}, u32[]{:S(2)}, u32[]{:S(2)}) collective-permute-start(f32[16,32,128]{2,1,0:T(8,128)S(1)} %bitcast.25), channel_id=1, source_target_pairs={{0,1},{1,0},{2,3},{3,2},{4,5},{5,4},{6,7},{7,6},{8,9},{9,8},{10,11... | collective-permute-start | bytes 786440 | tf_op jit(solution)/shard_map/ppermute | solution.py:58
  19.1 5.8 %collective-permute-start.5 = (f32[16,32,128]{2,1,0:T(8,128)S(1)}, f32[16,32,128]{2,1,0:T(8,128)S(1)}, u32[]{:S(2)}, u32[]{:S(2)}) collective-permute-start(f32[16,32,128]{2,1,0:T(8,128)S(1)} %bitcast.21), channel_id=1, source_target_pairs={{0,2},{2,0},{4,6},{6,4},{8,10},{10,8},{12,14},{14,12},{16,18},{18,... | collective-permute-start | bytes 786440 | tf_op jit(solution)/shard_map/ppermute | solution.py:58
  24.9 1.5 %collective-permute-start.4 = (f32[16,32,128]{2,1,0:T(8,128)S(1)}, f32[16,32,128]{2,1,0:T(8,128)S(1)}, u32[]{:S(2)}, u32[]{:S(2)}) collective-permute-start(f32[16,32,128]{2,1,0:T(8,128)S(1)} %collective-permute-done.3.refs_1_), channel_id=1, source_target_pairs={{0,2},{2,0},{4,6},{6,4},{8,10},{10,8},{12,14},{14,12},{16,18},{18,... | collective-permute-start | bytes 786440 | tf_op jit(solution)/shard_map/ppermute | solution.py:58
  27.3 8.4 %collective-permute-start.8 = (f32[4,128,128]{2,1,0:T(8,128)S(1)}, f32[4,128,128]{2,1,0:T(8,128)S(1)}, u32[]{:S(2)}, u32[]{:S(2)}) collective-permute-start(f32[4,128,128]{2,1,0:T(8,128)S(1)} %get-tuple-element.29), channel_id=1, source_target_pairs={{0,8},{2,10},{4,12},{6,14},{8,0},{10,2},{12,4},{14,6},{16,24},{18,... | collective-permute-start | bytes 786440 | tf_op jit(solution)/shard_map/ppermute | solution.py:58
  28.5 8.4 %collective-permute-start.6 = (f32[4,128,128]{2,1,0:T(8,128)S(1)}, f32[4,128,128]{2,1,0:T(8,128)S(1)}, u32[]{:S(2)}, u32[]{:S(2)}) collective-permute-start(f32[4,128,128]{2,1,0:T(8,128)S(1)} %get-tuple-element.27), channel_id=1, source_target_pairs={{0,4},{2,6},{4,0},{6,2},{8,12},{10,14},{12,8},{14,10},{16,20},{18,... | collective-permute-start | bytes 786440 | tf_op jit(solution)/shard_map/ppermute | solution.py:58
  35.8 5.0 %collective-permute-start.9 = (f32[2,128,128]{2,1,0:T(8,128)S(1)}, f32[2,128,128]{2,1,0:T(8,128)S(1)}, u32[]{:S(2)}, u32[]{:S(2)}) collective-permute-start(f32[2,128,128]{2,1,0:T(8,128)S(1)} %get-tuple-element.34), channel_id=1, source_target_pairs={{0,4},{2,6},{4,0},{6,2},{8,12},{10,14},{12,8},{14,10},{16,20},{18,... | collective-permute-start | bytes 393224 | tf_op jit(solution)/shard_map/ppermute | solution.py:58
  36.9 5.0 %collective-permute-start.7 = (f32[2,128,128]{2,1,0:T(8,128)S(1)}, f32[2,128,128]{2,1,0:T(8,128)S(1)}, u32[]{:S(2)}, u32[]{:S(2)}) collective-permute-start(f32[2,128,128]{2,1,0:T(8,128)S(1)} %get-tuple-element.36), channel_id=1, source_target_pairs={{0,8},{2,10},{4,12},{6,14},{8,0},{10,2},{12,4},{14,6},{16,24},{18,... | collective-permute-start | bytes 393224 | tf_op jit(solution)/shard_map/ppermute | solution.py:58
  42.0 7.3 %collective-permute-start.10 = (f32[2,1,128,128]{3,2,1,0:T(8,128)S(1)}, f32[2,1,128,128]{3,2,1,0:T(8,128)S(1)}, u32[]{:S(2)}, u32[]{:S(2)}) collective-permute-start(f32[2,1,128,128]{3,2,1,0:T(8,128)S(1)} %get-tuple-element.31), channel_id=1, source_target_pairs={{0,16},{2,18},{4,20},{6,22},{8,24},{10,26},{12,28},{14,30},{16,0},... | collective-permute-start | bytes 393224 | tf_op jit(solution)/shard_map/ppermute | solution.py:58

commit v5 on v4

--- a/solution.py
+++ b/solution.py
@@ -235,6 +235,12 @@
     return [slot | (1 << order[0]) for slot in rest] + rest
 
 
+def slot_of(target, me):
+    far = (target >> 1) ^ (me >> 1)
+    flip = (far ^ (far >> 1)) & (me & 1)
+    return far ^ (flip | (flip << 1))
+
+
 def add_terms(starts_ref, terms_ref, total, share, slots):
     me = lax.axis_index("grp")
     span, wide = share + 2 * TILE, starts_ref.shape[1]
@@ -243,7 +249,7 @@
         first = lax.div(start, share)
         target = first + ((first ^ me) & 1)
         where = start - target * share
-        base = ((target >> 1) ^ (me >> 1)) * span + TILE + where
+        base = slot_of(target, me) * span + TILE + where
         base = jnp.where(where > -TILE, base, slots * span)
         total[pl.ds(base, TILE), :] += terms_ref[tile]
 
@@ -273,61 +279,47 @@
     )(*flat, block)
 
 
-def last_body(orders, groups, share, count, *refs):
-    total, outs = refs[2 * count + 1], refs[2 * count + 2 :]
-    span, slots, half = share + 2 * TILE, groups // 2, share // 2
+def last_body(groups, share, count, *refs):
+    total, give, keep = refs[2 * count + 1 :]
+    span, slots = share + 2 * TILE, groups // 2
     for i in range(count):
         add_terms(*refs[2 * i : 2 * i + 2], total, share, slots)
-    for which, order in enumerate(orders):
-        for place, slot in enumerate(arranged(order)):
-            out = outs[2 * which + (place * 2 >= slots)]
-            begin = slot * span + TILE + which * half
-            out[place % (slots // 2)] = total[begin : begin + half, :]
-
-
-def last_sums(groups_of, total, rows, orders):
+    for place, slot in enumerate(arranged(tuple(range(slots.bit_length() - 1)))):
+        begin = slot * span + TILE
+        out = keep if place * 2 >= slots else give
+        out[place % (slots // 2)] = total[begin : begin + share, :]
+
+
+def last_sums(groups_of, total, rows):
     groups = lax.axis_size("grp")
     share, slots = rows // groups, groups // 2
-    out = floats(slots // 2, share // 2, LANES)
+    out = floats(slots // 2, share, LANES)
     flat = [a for pair in groups_of for a in pair]
     count = len(groups_of)
     return call(
-        functools.partial(last_body, orders, groups, share, count),
-        (floats(*total.shape),) + (out,) * 4, [SMEM, VMEM] * count + [VMEM],
+        functools.partial(last_body, groups, share, count),
+        (floats(*total.shape), out, out), [SMEM, VMEM] * count + [VMEM],
         total.size, 8 * total.size, input_output_aliases={2 * count: 0},
     )(*flat, total)[1:]
 
 
-def join_body(got_low, low, got_high, high, give_ref, keep_ref):
-    cut = low.shape[0] // 2
-    for half, (got, held) in enumerate(((got_low, low), (got_high, high))):
-        give_ref[half] = got[:cut] + held[:cut]
-        keep_ref[half] = got[cut:] + held[cut:]
-
-
 def finish_body(got, held, out_ref):
-    out_ref[...] = got[...] + held[...]
-
-
-def halve(low_give, low, high_give, high, orders):
-    bit_pairs = list(zip(*orders))
-    for step, (low_bit, high_bit) in enumerate(bit_pairs[:2]):
-        got_low = swap_over("grp", 2 << low_bit)(low_give)
-        got_high = swap_over("grp", 2 << high_bit)(high_give)
-        cut = low.shape[0] // 2
-        if step == 0:
-            low_give, low = got_low[:cut] + low[:cut], got_low[cut:] + low[cut:]
-            high_give, high = got_high[:cut] + high[:cut], got_high[cut:] + high[cut:]
-    out = floats(2, cut, *low.shape[1:])
-    give, keep = call(
-        join_body, (out, out), [VMEM] * 4, low.size, 24 * low.size
-    )(got_low, low, got_high, high)
-    for bit, _ in bit_pairs[2:]:
-        got = swap_over("grp", 2 << bit)(give)
-        cut = keep.shape[1] // 2
+    out_ref[...] = got[0] + held[0]
+
+
+def halve(give, keep):
+    groups = lax.axis_size("grp")
+    bits = groups.bit_length() - 2
+    for step in range(bits):
+        other = 1 - step if step < 2 else step
+        ring = [(i, i ^ (2 << (other if i & 1 else step))) for i in range(groups)]
+        got = lax.ppermute(give, "grp", ring)
+        cut = keep.shape[0] // 2
         if cut:
-            give, keep = got[:, :cut] + keep[:, :cut], got[:, cut:] + keep[:, cut:]
-    return call(finish_body, floats(*keep.shape), [VMEM] * 2, keep.size, 12 * keep.size)(got, keep)
+            give, keep = got[:cut] + keep[:cut], got[cut:] + keep[cut:]
+    return call(
+        finish_body, floats(*keep.shape[1:]), [VMEM] * 2, keep.size, 12 * keep.size
+    )(got, keep)
 
 
 def hold_body(block_ref, out_ref, sem):
@@ -344,7 +336,7 @@
 
 
 def per_device(model, source, observed, owner_ids, offsets, lengths):
-    rows, owners_count, groups = model.shape[0], lax.axis_size("mdl"), lax.axis_size("grp")
+    rows, owners_count = model.shape[0], lax.axis_size("mdl")
     tiles = source.shape[0] * LZ
     across, beside = swap_over("mdl", 1), swap_over("grp", 1)
     block = hold(model.reshape(rows, LANES))
@@ -386,10 +378,7 @@
         total = first_sums([(asked, arrived)], block)
         final = [(beside(asked), beside(arrived))]
 
-    bits = tuple(range(groups.bit_length() - 2))
-    orders = (bits, bits[1:2] + bits[0:1] + bits[2:])
-    sums = halve(*last_sums(final, total, rows, orders), orders)
-    return sums.reshape(rows // groups, 1, LANES)
+    return halve(*last_sums(final, total, rows))[:, None, :]
 
 
 def solution(mesh):

time: 50.1 us -> 51.6 us (1.030)
  waiting for transfers between devices: 25 us -> 30 us
  starting transfers between devices: 14.3 us -> 10.7 us
    ppermute x0 -> x3, waiting for transfers between devices: none -> 18.8 us  [halve(): got = lax.ppermute(give, 'grp', ring)]
    ppermute x11 -> x6, waiting for transfers between devices: 25 us -> 11.2 us  [swap_over(): return lambda value: lax.ppermute(value, axis, ring)]
    ppermute x11 -> x6, starting transfers between devices: 14.3 us -> 6.23 us  [swap_over(): return lambda value: lax.ppermute(value, axis, ring)]
    ppermute x0 -> x3, starting transfers between devices: none -> 4.46 us  [halve(): got = lax.ppermute(give, 'grp', ring)]
    pallas_call x3 -> x2, Pallas kernels: 1.52 us -> 1.53 us  [the longest x1 0.86 us: last_sums(): call(functools.partial(last_body, groups, share, count), (floats(*total.s...]
  transfers between devices with their start and end apart: 11 -> 9, of which waited for: 8 -> 7; matrix products, arithmetic and copies ran while one was open for 0% -> 0% of each run, Pallas kernels for 4% -> 4%
where the time goes in v5:
time: 51.6 us; the launch traced here: 51.4 us
  waiting for transfers between devices  30 us (58%)
  starting transfers between devices  10.7 us (21%)
  Pallas kernels  8.87 us (17%)
  local copies, waits for them, and re-layouts  1.63 us (3%)
    ppermute x3, waiting for transfers between devices, halve(): got = lax.ppermute(give, 'grp', ring)  18.8 us
    ppermute x6, waiting for transfers between devices, swap_over(): return lambda value: lax.ppermute(value, axis, ring)  11.2 us
    ppermute x6, starting transfers between devices, swap_over(): return lambda value: lax.ppermute(value, axis, ring)  6.23 us
    pallas_call x1, Pallas kernels, soundings_partial(): call(fields_body, (out, out), [SMEM] * 3 + [VMEM] * 4, 500 * cells, 40 *...  4.76 us
    ppermute x3, starting transfers between devices, halve(): got = lax.ppermute(give, 'grp', ring)  4.46 us
    unnamed x12, local copies, waits for them, and re-layouts  1.62 us
  transfers between devices with their start and end apart: 9, of which 7 were waited for; matrix products, arithmetic and copies ran while one was open for 0% of the time, Pallas kernels for 4%

profile of v5, /device:TPU:0, one launch (start us, length us, event | category | flops | bytes accessed | tf_op | source)
XLA Modules:
  0.0 51.4 jit_solution(9823044380825785184)
XLA Ops:
  0.0 3.0 %collective-permute-start = (s32[2,8]{1,0:T(2,128)}, s32[2,8]{1,0:T(2,128)S(1)}, u32[]{:S(2)}, u32[]{:S(2)}) collective-permute-start(s32[2,8]{1,0:T(2,128)} %refs_0_.1), channel_id=1, source_target_pairs={{0,1},{1,0},{2,3},{3,2},{4,5},{5,4},{6,7},{7,6},{8,9},{9,8},{10,11... | collective-permute-start | bytes 200 | tf_op jit(solution)/shard_map/ppermute | solution.py:58
  3.0 0.0 copy-start
  3.0 1.6 %copy-done = f32[4096,1,128]{2,1,0:T(1,128)S(1)} copy-done((f32[4096,1,128]{2,1,0:T(1,128)S(1)}, f32[4096,1,128]{2,1,0:T(1,128)}, u32[]{:S(2)}) %copy-start) | copy-done | bytes 2097176
  4.6 0.1 shard_map.64.block_ref.table_ref.refs_4_
  4.7 0.0 copy-start.3
  4.7 0.0 copy-start.1
  4.7 0.0 copy-start.2
  4.8 0.0 copy-start.4
  4.8 0.0 copy-start.5
  4.8 0.0 collective-permute-done.starts_ref.refs_0_
  4.8 0.6 %shard_map.65 = f32[16,32,128]{2,1,0:T(8,128)S(1)} custom-call(s32[2,8]{1,0:T(2,128)S(1)} %collective-permute-done.starts_ref.refs_0_, f32[4096,128]{1,0:T(8,128)S(1)} %shard_map.64.block_ref.table_ref.refs_4_), custom_call_target="tpu_custom_call" | custom-call | bytes 524288 | tf_op jit(solution)/shard_map/pallas_call | solution.py:70
  5.4 2.0 %collective-permute-start.1 = (f32[16,32,128]{2,1,0:T(8,128)S(1)}, f32[16,32,128]{2,1,0:T(8,128)S(1)}, u32[]{:S(2)}, u32[]{:S(2)}) collective-permute-start(f32[16,32,128]{2,1,0:T(8,128)S(1)} %shard_map.65), channel_id=1, source_target_pairs={{0,1},{1,0},{2,3},{3,2},{4,5},{5,4},{6,7},{7,6},{8,9},{9,8},{10,11... | collective-permute-start | bytes 786440 | tf_op jit(solution)/shard_map/ppermute | solution.py:58
  7.4 0.0 copy-done.3
  7.4 0.1 collective-permute-start.2
  7.5 0.0 copy-done.1
  7.5 0.0 copy-done.2
  7.5 0.9 %shard_map.66 = (f32[3,8,8,8,128]{4,3,2,1,0:T(8,128)S(1)}, f32[3,8,8,8,128]{4,3,2,1,0:T(8,128)S(1)}) custom-call(f32[1536,128]{1,0:T(8,128)S(1)} %bitcast.19, f32[1536,128]{1,0:T(8,128)S(1)} %bitcast.20), custom_call_target="tpu_custom_call" | custom-call | flops 1572864 | bytes 3145728 | tf_op jit(solution)/shard_map/pallas_call | solution.py:107
  8.5 0.2 collective-permute-done.2
  8.6 4.6 %collective-permute-done.1 = f32[16,32,128]{2,1,0:T(8,128)S(1)} collective-permute-done((f32[16,32,128]{2,1,0:T(8,128)S(1)}, f32[16,32,128]{2,1,0:T(8,128)S(1)}, u32[]{:S(2)}, u32[]{:S(2)}) %collective-permute-start.1) | collective-permute-done | bytes 262176 | tf_op jit(solution)/shard_map/ppermute | solution.py:58
  13.2 0.0 copy-done.4
  13.2 0.0 copy-done.5
  13.2 4.8 %shard_map.67 = (f32[512,128]{1,0:T(8,128)S(1)}, f32[512,128]{1,0:T(8,128)S(1)}) custom-call(s32[2,8]{1,0:T(2,128)S(1)} %copy-done.3, s32[2,8]{1,0:T(2,128)S(1)} %bitcast.24, s32[2,8]{1,0:T(2,128)S(1)} %copy-done.5, f32[4096,128]{1,0:T(8,128)S(1)} %shard_map.64.block_ref.table_ref.refs_4_, f32[512,128]{1,0:T(8,128)S(1)} %bitcast.23, ...), custom_call_target="tpu_custom_call" | custom-call | flops 32768000 | bytes 2621440 | tf_op jit(solution)/shard_map/pallas_call | solution.py:223
  18.0 1.2 %collective-permute-start.3 = (f32[16,32,128]{2,1,0:T(8,128)S(1)}, f32[16,32,128]{2,1,0:T(8,128)S(1)}, u32[]{:S(2)}, u32[]{:S(2)}) collective-permute-start(f32[16,32,128]{2,1,0:T(8,128)S(1)} %bitcast.25), channel_id=1, source_target_pairs={{0,1},{1,0},{2,3},{3,2},{4,5},{5,4},{6,7},{7,6},{8,9},{9,8},{10,11... | collective-permute-start | bytes 786440 | tf_op jit(solution)/shard_map/ppermute | solution.py:58
  19.1 0.0 collective-permute-start.5
  19.1 5.8 %collective-permute-done.3.refs_1_ = f32[16,32,128]{2,1,0:T(8,128)S(1)} collective-permute-done((f32[16,32,128]{2,1,0:T(8,128)S(1)}, f32[16,32,128]{2,1,0:T(8,128)S(1)}, u32[]{:S(2)}, u32[]{:S(2)}) %collective-permute-start.3) | collective-permute-done | bytes 262176 | tf_op jit(solution)/shard_map/ppermute | solution.py:58
  24.9 0.0 collective-permute-start.4
  25.0 0.0 collective-permute-done.5.refs_3_
  25.0 0.9 %shard_map.68.refs_4_ = f32[2592,128]{1,0:T(8,128)S(1)} custom-call(s32[2,8]{1,0:T(2,128)S(1)} %copy-done.3, f32[16,32,128]{2,1,0:T(8,128)S(1)} %bitcast.22, s32[2,8]{1,0:T(2,128)S(1)} %get-tuple-element.29.refs_2_, f32[16,32,128]{2,1,0:T(8,128)S(1)} %collective-permute-done.5.refs_3_, f32[4096,128]{1,0:T(8,128)S(1)} %shard_map.64.block_ref.table_ref.refs_4_), custom_call_target="tpu_custom_call" | custom-call | flops 331776 | bytes 2654208 | tf_op jit(solution)/shard_map/pallas_call | solution.py:276
  25.9 0.6 %collective-permute-done.4.refs_3_ = f32[16,32,128]{2,1,0:T(8,128)S(1)} collective-permute-done((f32[16,32,128]{2,1,0:T(8,128)S(1)}, f32[16,32,128]{2,1,0:T(8,128)S(1)}, u32[]{:S(2)}, u32[]{:S(2)}) %collective-permute-start.4) | collective-permute-done | bytes 262176 | tf_op jit(solution)/shard_map/ppermute | solution.py:58
  26.5 0.9 %shard_map.69 = (f32[2592,128]{1,0:T(8,128)S(1)}, f32[4,256,128]{2,1,0:T(8,128)S(1)}, f32[4,256,128]{2,1,0:T(8,128)S(1)}) custom-call(s32[2,8]{1,0:T(2,128)S(1)} %collective-permute-done.starts_ref.refs_0_, f32[16,32,128]{2,1,0:T(8,128)S(1)} %collective-permute-done.3.refs_1_, ...), custom_call_target="tpu_custom_call", output_to_operand_aliasing={{0}: (4, {})} | custom-call | flops 331776 | bytes 2654208 | tf_op jit(solution)/shard_map/pallas_call | solution.py:299
  27.3 1.1 %collective-permute-start.6 = (f32[4,256,128]{2,1,0:T(8,128)S(1)}, f32[4,256,128]{2,1,0:T(8,128)S(1)}, u32[]{:S(2)}, u32[]{:S(2)}) collective-permute-start(f32[4,256,128]{2,1,0:T(8,128)S(1)} %get-tuple-element.23), channel_id=1, source_target_pairs={{0,4},{2,10},{4,0},{6,14},{8,12},{10,2},{12,8},{14,6},{16,20},{18,... | collective-permute-start | bytes 1572872 | tf_op jit(solution)/shard_map/ppermute | solution.py:316
  28.5 8.1 %collective-permute-done.6 = f32[4,256,128]{2,1,0:T(8,128)S(1)} collective-permute-done((f32[4,256,128]{2,1,0:T(8,128)S(1)}, f32[4,256,128]{2,1,0:T(8,128)S(1)}, u32[]{:S(2)}, u32[]{:S(2)}) %collective-permute-start.6) | collective-permute-done | bytes 524320 | tf_op jit(solution)/shard_map/ppermute | solution.py:316
  36.6 0.1 slice_add_fusion.1
  36.7 1.2 %collective-permute-start.7 = (f32[2,256,128]{2,1,0:T(8,128)S(1)}, f32[2,256,128]{2,1,0:T(8,128)S(1)}, u32[]{:S(2)}, u32[]{:S(2)}) collective-permute-start(f32[2,256,128]{2,1,0:T(8,128)S(1)} %get-tuple-element.25), channel_id=1, source_target_pairs={{0,8},{2,6},{4,12},{6,2},{8,0},{10,14},{12,4},{14,10},{16,24},{18,... | collective-permute-start | bytes 786440 | tf_op jit(solution)/shard_map/ppermute | solution.py:316
  37.8 5.3 %collective-permute-done.7 = f32[2,256,128]{2,1,0:T(8,128)S(1)} collective-permute-done((f32[2,256,128]{2,1,0:T(8,128)S(1)}, f32[2,256,128]{2,1,0:T(8,128)S(1)}, u32[]{:S(2)}, u32[]{:S(2)}) %collective-permute-start.7) | collective-permute-done | bytes 262176 | tf_op jit(solution)/shard_map/ppermute | solution.py:316
  43.1 2.2 %collective-permute-start.8 = (f32[1,256,128]{2,1,0:T(8,128)S(1)}, f32[1,256,128]{2,1,0:T(8,128)S(1)}, u32[]{:S(2)}, u32[]{:S(2)}) collective-permute-start(f32[1,256,128]{2,1,0:T(8,128)S(1)} %get-tuple-element.28), channel_id=1, source_target_pairs={{0,16},{2,18},{4,20},{6,22},{8,24},{10,26},{12,28},{14,30},{16,0},... | collective-permute-start | bytes 393224 | tf_op jit(solution)/shard_map/ppermute | solution.py:316
  45.3 5.4 %collective-permute-done.8.got = f32[1,256,128]{2,1,0:T(8,128)S(1)} collective-permute-done((f32[1,256,128]{2,1,0:T(8,128)S(1)}, f32[1,256,128]{2,1,0:T(8,128)S(1)}, u32[]{:S(2)}, u32[]{:S(2)}) %collective-permute-start.8) | collective-permute-done | bytes 131104 | tf_op jit(solution)/shard_map/ppermute | solution.py:316
  50.7 0.7 %shard_map.70 = f32[256,128]{1,0:T(8,128)} custom-call(f32[1,256,128]{2,1,0:T(8,128)S(1)} %collective-permute-done.8.got, f32[1,256,128]{2,1,0:T(8,128)S(1)} %get-tuple-element.27.held), custom_call_target="tpu_custom_call" | custom-call | flops 32768 | bytes 393216 | tf_op jit(solution)/shard_map/pallas_call | solution.py:320
  (3 shorter events, 0.0 us)
Async XLA Ops:
  0.0 4.8 %collective-permute-start = (s32[2,8]{1,0:T(2,128)}, s32[2,8]{1,0:T(2,128)S(1)}, u32[]{:S(2)}, u32[]{:S(2)}) collective-permute-start(s32[2,8]{1,0:T(2,128)} %refs_0_.1), channel_id=1, source_target_pairs={{0,1},{1,0},{2,3},{3,2},{4,5},{5,4},{6,7},{7,6},{8,9},{9,8},{10,11... | collective-permute-start | bytes 200 | tf_op jit(solution)/shard_map/ppermute | solution.py:58
  3.0 1.6 %copy-start = (f32[4096,1,128]{2,1,0:T(1,128)S(1)}, f32[4096,1,128]{2,1,0:T(1,128)}, u32[]{:S(2)}) copy-start(f32[4096,1,128]{2,1,0:T(1,128)} %param.6) | copy-start | bytes 6291460
  4.7 2.7 %copy-start.3 = (s32[2,8]{1,0:T(2,128)S(1)}, s32[2,8]{1,0:T(2,128)}, u32[]{:S(2)}) copy-start(s32[2,8]{1,0:T(2,128)} %refs_0_.1) | copy-start | bytes 196
  4.7 2.8 %copy-start.1 = (f32[2,3,8,4096]{3,2,1,0:T(8,128)S(1)}, f32[2,3,8,4096]{3,2,1,0:T(8,128)}, u32[]{:S(2)}) copy-start(f32[2,3,8,4096]{3,2,1,0:T(8,128)} %param.7) | copy-start | bytes 2359300
  4.7 2.8 %copy-start.2 = (f32[2,3,8,4096]{3,2,1,0:T(8,128)S(1)}, f32[2,3,8,4096]{3,2,1,0:T(8,128)}, u32[]{:S(2)}) copy-start(f32[2,3,8,4096]{3,2,1,0:T(8,128)} %param.8) | copy-start | bytes 2359300
  4.8 8.4 %copy-start.4 = (s32[2,8,1]{1,2,0:T(1,128)S(1)}, s32[2,8,1]{1,2,0:T(1,128)}, u32[]{:S(2)}) copy-start(s32[2,8,1]{1,2,0:T(1,128)} %param.9) | copy-start | bytes 196
  4.8 8.4 %copy-start.5 = (s32[2,8]{1,0:T(2,128)S(1)}, s32[2,8]{1,0:T(2,128)}, u32[]{:S(2)}) copy-start(s32[2,8]{1,0:T(2,128)} %lengths_ref.1) | copy-start | bytes 196
  5.4 7.8 %collective-permute-start.1 = (f32[16,32,128]{2,1,0:T(8,128)S(1)}, f32[16,32,128]{2,1,0:T(8,128)S(1)}, u32[]{:S(2)}, u32[]{:S(2)}) collective-permute-start(f32[16,32,128]{2,1,0:T(8,128)S(1)} %shard_map.65), channel_id=1, source_target_pairs={{0,1},{1,0},{2,3},{3,2},{4,5},{5,4},{6,7},{7,6},{8,9},{9,8},{10,11... | collective-permute-start | bytes 786440 | tf_op jit(solution)/shard_map/ppermute | solution.py:58
  7.4 1.2 %collective-permute-start.2 = (s32[4,8]{1,0:T(4,128)S(1)}, s32[4,8]{1,0:T(4,128)S(1)}, u32[]{:S(2)}, u32[]{:S(2)}) collective-permute-start(s32[4,8]{1,0:T(4,128)S(1)} %pad_add_fusion), channel_id=1, source_target_pairs={{0,2},{2,0},{4,6},{6,4},{8,10},{10,8},{12,14},{14,12},{16,18},{18,... | collective-permute-start | bytes 392 | tf_op jit(solution)/shard_map/ppermute | solution.py:58
  18.0 7.0 %collective-permute-start.3 = (f32[16,32,128]{2,1,0:T(8,128)S(1)}, f32[16,32,128]{2,1,0:T(8,128)S(1)}, u32[]{:S(2)}, u32[]{:S(2)}) collective-permute-start(f32[16,32,128]{2,1,0:T(8,128)S(1)} %bitcast.25), channel_id=1, source_target_pairs={{0,1},{1,0},{2,3},{3,2},{4,5},{5,4},{6,7},{7,6},{8,9},{9,8},{10,11... | collective-permute-start | bytes 786440 | tf_op jit(solution)/shard_map/ppermute | solution.py:58
  19.1 5.8 %collective-permute-start.5 = (f32[16,32,128]{2,1,0:T(8,128)S(1)}, f32[16,32,128]{2,1,0:T(8,128)S(1)}, u32[]{:S(2)}, u32[]{:S(2)}) collective-permute-start(f32[16,32,128]{2,1,0:T(8,128)S(1)} %bitcast.21), channel_id=1, source_target_pairs={{0,2},{2,0},{4,6},{6,4},{8,10},{10,8},{12,14},{14,12},{16,18},{18,... | collective-permute-start | bytes 786440 | tf_op jit(solution)/shard_map/ppermute | solution.py:58
  24.9 1.5 %collective-permute-start.4 = (f32[16,32,128]{2,1,0:T(8,128)S(1)}, f32[16,32,128]{2,1,0:T(8,128)S(1)}, u32[]{:S(2)}, u32[]{:S(2)}) collective-permute-start(f32[16,32,128]{2,1,0:T(8,128)S(1)} %collective-permute-done.3.refs_1_), channel_id=1, source_target_pairs={{0,2},{2,0},{4,6},{6,4},{8,10},{10,8},{12,14},{14,12},{16,18},{18,... | collective-permute-start | bytes 786440 | tf_op jit(solution)/shard_map/ppermute | solution.py:58
  27.3 9.2 %collective-permute-start.6 = (f32[4,256,128]{2,1,0:T(8,128)S(1)}, f32[4,256,128]{2,1,0:T(8,128)S(1)}, u32[]{:S(2)}, u32[]{:S(2)}) collective-permute-start(f32[4,256,128]{2,1,0:T(8,128)S(1)} %get-tuple-element.23), channel_id=1, source_target_pairs={{0,4},{2,10},{4,0},{6,14},{8,12},{10,2},{12,8},{14,6},{16,20},{18,... | collective-permute-start | bytes 1572872 | tf_op jit(solution)/shard_map/ppermute | solution.py:316
  36.7 6.4 %collective-permute-start.7 = (f32[2,256,128]{2,1,0:T(8,128)S(1)}, f32[2,256,128]{2,1,0:T(8,128)S(1)}, u32[]{:S(2)}, u32[]{:S(2)}) collective-permute-start(f32[2,256,128]{2,1,0:T(8,128)S(1)} %get-tuple-element.25), channel_id=1, source_target_pairs={{0,8},{2,6},{4,12},{6,2},{8,0},{10,14},{12,4},{14,10},{16,24},{18,... | collective-permute-start | bytes 786440 | tf_op jit(solution)/shard_map/ppermute | solution.py:316
  43.1 7.6 %collective-permute-start.8 = (f32[1,256,128]{2,1,0:T(8,128)S(1)}, f32[1,256,128]{2,1,0:T(8,128)S(1)}, u32[]{:S(2)}, u32[]{:S(2)}) collective-permute-start(f32[1,256,128]{2,1,0:T(8,128)S(1)} %get-tuple-element.28), channel_id=1, source_target_pairs={{0,16},{2,18},{4,20},{6,22},{8,24},{10,26},{12,28},{14,30},{16,0},... | collective-permute-start | bytes 393224 | tf_op jit(solution)/shard_map/ppermute | solution.py:316

commit v6 on v4

--- a/solution.py
+++ b/solution.py
@@ -27,6 +27,9 @@
 VMEM = pl.BlockSpec(memory_space=pltpu.VMEM)
 SMEM = pl.BlockSpec(memory_space=pltpu.SMEM)
 LIMIT = 16 << 20
+
+EARTH = LZ * TILE * 3 // 4
+PADDED = EARTH + TILE
 
 
 def call(body, out, in_specs, work, moved, **kwargs):
@@ -70,6 +73,42 @@
     return call(gather_body, out, [SMEM, VMEM], 0, 8 * out.size)(starts, block)
 
 
+def earth_gather_body(index_ref, block_ref, out_ref, padded):
+    count = index_ref.shape[0] // 2
+    for sounding in range(count):
+        place = sounding * PADDED
+        for z in range(LZ):
+            rows = block_ref[pl.ds(index_ref[sounding, z], TILE), :]
+            padded[pl.ds(place, TILE), :] = rows
+            place += index_ref[count + sounding, z]
+    unpad(padded, out_ref, count)
+
+
+def unpad(padded, out_ref, count):
+    for sounding in range(count):
+        begin, first = sounding * EARTH, sounding * PADDED
+        out_ref[begin : begin + EARTH, :] = padded[first : first + EARTH, :]
+
+
+def pad_end(rows_ref, padded):
+    count = rows_ref.shape[0]
+    padded[:count, :] = rows_ref[...]
+    padded[count:, :] = jnp.zeros((TILE, LANES), jnp.float32)
+
+
+def padded_rows(count):
+    return pltpu.VMEM((count, LANES), jnp.float32)
+
+
+def gather_earth(index, block):
+    count = index.shape[0] // 2
+    out = floats(count * EARTH, LANES)
+    return call(
+        earth_gather_body, out, [SMEM, VMEM], 0, 8 * out.size,
+        scratch_shapes=[padded_rows(count * PADDED)],
+    )(index, block)
+
+
 def low_half():
     return lax.broadcasted_iota(jnp.int32, (SUB, LANES), 1) < LY
 
@@ -110,8 +149,8 @@
 
 
 def fields_body(
-    starts_ref, owners_ref, lengths_ref, table_ref, answer_ref, source_ref, observed_ref, kept_ref,
-    given_ref, field, adjoint, right, curl, scale, decay, weight,
+    packed, starts_ref, owners_ref, lengths_ref, table_ref, answer_ref, source_ref, observed_ref, kept_ref,
+    given_ref, field, adjoint, right, curl, scale, decay, weight, sent_rows, given_rows,
 ):
     me = lax.axis_index("mdl")
     lane = lax.broadcasted_iota(jnp.int32, (SUB, LANES), 1)
@@ -159,11 +198,25 @@
                 state[1, z, k] = d * state[1, z, k] + (right[1, z, k] - s * back_y)
                 state[2, z, k] = d * state[2, z, k] + (right[2, z, k] - s * back_z)
 
+    count = starts_ref.shape[0]
+    sent_at, given_at = [], []
+    for sounding in range(count):
+        place = 0
+        for z in range(LZ):
+            tile = sounding * LZ + z
+            sent_at.append(sounding * EARTH + place if packed else tile * TILE)
+            given_at.append(sounding * PADDED + place if packed else tile * TILE)
+            place += lengths_ref[sounding, z]
+    if packed:
+        pad_end(answer_ref, sent_rows)
+    sent_from = sent_rows if packed else answer_ref
+    given_to = given_rows if packed else given_ref
+
     for z in range(LZ):
 
         def layer(sounding, j):
             raw = rows_of(table_ref, starts_ref[sounding, z] + j, 1)
-            sent = rows_of(answer_ref, (sounding * LZ + z) * TILE + j, 1)
+            sent = rows_of(sent_from, sent_at[sounding * LZ + z] + j, 1)
             mine = jnp.full((SUB, LANES), owners_ref[sounding, z] == me)
             return jnp.where(mine, raw, sent)
 
@@ -209,23 +262,28 @@
             first, second = pack(partial(2 * j), partial(2 * j + 1), low)
             for sounding, value in enumerate((first, second)):
                 mine = jnp.full((SUB, LANES), owners_ref[sounding, z] == me)
-                place = pl.ds((sounding * LZ + z) * TILE + j, SUB, stride=PARTS)
-                kept_ref[place, :] = jnp.where(mine, value, 0.0)
-                given_ref[place, :] = jnp.where(mine, 0.0, value)
+                tile = sounding * LZ + z
+                kept_ref[pl.ds(tile * TILE + j, SUB, stride=PARTS), :] = jnp.where(mine, value, 0.0)
+                place = pl.ds(given_at[tile] + j, SUB, stride=PARTS)
+                given_to[place, :] = jnp.where(mine, 0.0, value)
+    if packed:
+        unpad(given_rows, given_ref, count)
 
 
 def soundings_partial(starts, owners, lengths, table, answer, source, observed):
-    tiles = starts.size
+    count, tiles = starts.shape[0], starts.size
+    packed = answer.shape[0] == count * EARTH
     planes = pltpu.VMEM((3, LZ, PACKED, SUB, LANES), jnp.float32)
     single = pltpu.VMEM((LZ, PACKED, SUB, LANES), jnp.float32)
     cells = tiles * TILE * LANES
-    out = floats(tiles * TILE, LANES)
     kept, given = call(
-        fields_body, (out, out),
+        functools.partial(fields_body, packed),
+        (floats(tiles * TILE, LANES), floats(*answer.shape)),
         [SMEM] * 3 + [VMEM] * 4, 500 * cells, 40 * cells,
-        scratch_shapes=[planes] * 4 + [single] * 3,
-    )(starts, owners, lengths, table, answer.reshape(tiles * TILE, LANES), source, observed)
-    return kept.reshape(tiles, TILE, LANES), given.reshape(tiles, TILE, LANES)
+        scratch_shapes=[planes] * 4 + [single] * 3
+        + [padded_rows(count * EARTH + TILE), padded_rows(count * PADDED)],
+    )(starts, owners, lengths, table, answer, source, observed)
+    return kept.reshape(tiles, TILE, LANES), given
 
 
 def arranged(order):
@@ -235,17 +293,28 @@
     return [slot | (1 << order[0]) for slot in rest] + rest
 
 
-def add_terms(starts_ref, terms_ref, total, share, slots):
+def add_terms(index_ref, terms_ref, total, share, slots, padded):
     me = lax.axis_index("grp")
-    span, wide = share + 2 * TILE, starts_ref.shape[1]
-    for tile in range(terms_ref.shape[0]):
-        start = starts_ref[tile // wide, tile % wide]
+    packed = len(terms_ref.shape) == 2
+    span, wide = share + 2 * TILE, index_ref.shape[1]
+    tiles = terms_ref.shape[0] // EARTH * LZ if packed else terms_ref.shape[0]
+    row = lax.broadcasted_iota(jnp.int32, (TILE, LANES), 0)
+    if packed:
+        pad_end(terms_ref, padded)
+    for tile in range(tiles):
+        start = index_ref[tile // wide, tile % wide]
         first = lax.div(start, share)
         target = first + ((first ^ me) & 1)
         where = start - target * share
         base = ((target >> 1) ^ (me >> 1)) * span + TILE + where
         base = jnp.where(where > -TILE, base, slots * span)
-        total[pl.ds(base, TILE), :] += terms_ref[tile]
+        if packed:
+            place = tile // LZ * EARTH if tile % LZ == 0 else place + length
+            length = index_ref[tiles // LZ + tile // LZ, tile % LZ]
+            terms = jnp.where(row < length, padded[pl.ds(place, TILE), :], 0.0)
+        else:
+            terms = terms_ref[tile]
+        total[pl.ds(base, TILE), :] += terms
 
 
 def first_body(groups, count, *refs):
@@ -259,7 +328,7 @@
     right = jnp.where(lane == LANES - 1, local, pltpu.roll(local, LANES - 1, 1))
     total[TILE : TILE + share, :] = BETA * (2.0 * local - left - right)
     for i in range(count):
-        add_terms(*refs[2 * i : 2 * i + 2], total, share, groups // 2)
+        add_terms(*refs[2 * i : 2 * i + 2], total, share, groups // 2, None)
 
 
 def first_sums(groups_of, block):
@@ -273,40 +342,46 @@
     )(*flat, block)
 
 
+def low_rows(share):
+    return max(1, share * 7 // 128) * SUB
+
+
 def last_body(orders, groups, share, count, *refs):
-    total, outs = refs[2 * count + 1], refs[2 * count + 2 :]
-    span, slots, half = share + 2 * TILE, groups // 2, share // 2
+    total, outs, padded = refs[2 * count + 1], refs[2 * count + 2 : -1], refs[-1]
+    span, slots, half = share + 2 * TILE, groups // 2, low_rows(share)
     for i in range(count):
-        add_terms(*refs[2 * i : 2 * i + 2], total, share, slots)
+        add_terms(*refs[2 * i : 2 * i + 2], total, share, slots, padded)
     for which, order in enumerate(orders):
         for place, slot in enumerate(arranged(order)):
             out = outs[2 * which + (place * 2 >= slots)]
             begin = slot * span + TILE + which * half
-            out[place % (slots // 2)] = total[begin : begin + half, :]
+            out[place % (slots // 2)] = total[begin : begin + out.shape[1], :]
 
 
 def last_sums(groups_of, total, rows, orders):
     groups = lax.axis_size("grp")
     share, slots = rows // groups, groups // 2
-    out = floats(slots // 2, share // 2, LANES)
+    low, high = (floats(slots // 2, r, LANES) for r in (low_rows(share), share - low_rows(share)))
+    terms_rows = max(a.shape[0] for _, a in groups_of)
     flat = [a for pair in groups_of for a in pair]
     count = len(groups_of)
     return call(
         functools.partial(last_body, orders, groups, share, count),
-        (floats(*total.shape),) + (out,) * 4, [SMEM, VMEM] * count + [VMEM],
+        (floats(*total.shape), low, low, high, high), [SMEM, VMEM] * count + [VMEM],
         total.size, 8 * total.size, input_output_aliases={2 * count: 0},
+        scratch_shapes=[padded_rows(terms_rows + TILE)],
     )(*flat, total)[1:]
 
 
 def join_body(got_low, low, got_high, high, give_ref, keep_ref):
-    cut = low.shape[0] // 2
-    for half, (got, held) in enumerate(((got_low, low), (got_high, high))):
-        give_ref[half] = got[:cut] + held[:cut]
-        keep_ref[half] = got[cut:] + held[cut:]
+    cut, split = low.shape[0] // 2, low.shape[1]
+    for got, held, rows in ((got_low, low, slice(0, split)), (got_high, high, slice(split, None))):
+        give_ref[:, rows] = got[:cut] + held[:cut]
+        keep_ref[:, rows] = got[cut:] + held[cut:]
 
 
 def finish_body(got, held, out_ref):
-    out_ref[...] = got[...] + held[...]
+    out_ref[...] = got[0] + held[0]
 
 
 def halve(low_give, low, high_give, high, orders):
@@ -318,16 +393,18 @@
         if step == 0:
             low_give, low = got_low[:cut] + low[:cut], got_low[cut:] + low[cut:]
             high_give, high = got_high[:cut] + high[:cut], got_high[cut:] + high[cut:]
-    out = floats(2, cut, *low.shape[1:])
+    out = floats(cut, low.shape[1] + high.shape[1], LANES)
     give, keep = call(
         join_body, (out, out), [VMEM] * 4, low.size, 24 * low.size
     )(got_low, low, got_high, high)
     for bit, _ in bit_pairs[2:]:
         got = swap_over("grp", 2 << bit)(give)
-        cut = keep.shape[1] // 2
+        cut = keep.shape[0] // 2
         if cut:
-            give, keep = got[:, :cut] + keep[:, :cut], got[:, cut:] + keep[:, cut:]
-    return call(finish_body, floats(*keep.shape), [VMEM] * 2, keep.size, 12 * keep.size)(got, keep)
+            give, keep = got[:cut] + keep[:cut], got[cut:] + keep[cut:]
+    return call(
+        finish_body, floats(*keep.shape[1:]), [VMEM] * 2, keep.size, 12 * keep.size
+    )(got, keep)
 
 
 def hold_body(block_ref, out_ref, sem):
@@ -350,20 +427,20 @@
     block = hold(model.reshape(rows, LANES))
     source, observed = prepare(source, observed)
     if owners_count == 2:
-        asked = across(offsets)
+        asked = across(jnp.concatenate([offsets, lengths]))
         asked, block = lax.optimization_barrier((asked, block))
-        given = gather_rows(asked, block)
+        given = gather_earth(asked, block)
         answer = across(given)
         told = beside(jnp.concatenate([offsets, asked]))
         answer, told = lax.optimization_barrier((answer, told))
-        told = told.reshape(2, *offsets.shape)
+        held = offsets.shape[0]
         kept, given = soundings_partial(
             offsets, owner_ids.reshape(offsets.shape), lengths, block, answer, source, observed
         )
         others = across(given)
         kept_beside = beside(kept)
-        total = first_sums([(offsets, kept), (told[0], kept_beside)], block)
-        final = [(asked, others), (told[1], beside(others))]
+        total = first_sums([(offsets, kept), (told[:held], kept_beside)], block)
+        final = [(asked, others), (told[held:], beside(others))]
     else:
         capacity = max(4, 2 * tiles // owners_count)
         places = place_slots(owner_ids.reshape(tiles), owners_count, capacity)
@@ -378,7 +455,7 @@
         fetched = swap(given).reshape(owners_count * capacity * TILE, LANES)
         terms, _ = soundings_partial(
             (places * TILE).reshape(offsets.shape), jnp.full_like(offsets, lax.axis_index("mdl")),
-            lengths, fetched, jnp.zeros((tiles, TILE, LANES), jnp.float32), source, observed,
+            lengths, fetched, jnp.zeros((tiles * TILE, LANES), jnp.float32), source, observed,
         )
         outgoing = jnp.zeros((owners_count * capacity, TILE, LANES), jnp.float32)
         outgoing = outgoing.at[places].set(terms).reshape(owners_count, capacity, TILE, LANES)
@@ -389,7 +466,7 @@
     bits = tuple(range(groups.bit_length() - 2))
     orders = (bits, bits[1:2] + bits[0:1] + bits[2:])
     sums = halve(*last_sums(final, total, rows, orders), orders)
-    return sums.reshape(rows // groups, 1, LANES)
+    return sums[:, None, :]
 
 
 def solution(mesh):

time: 50.1 us -> 49.2 us (0.982)
  waiting for transfers between devices: 25 us -> 22.5 us
  other arithmetic: 0.07 us -> 0.79 us
  starting transfers between devices: 14.3 us -> 15 us
    ppermute x11, waiting for transfers between devices: 25 us -> 22.5 us  [swap_over(): return lambda value: lax.ppermute(value, axis, ring)]
    ppermute x11, starting transfers between devices: 14.3 us -> 15 us  [swap_over(): return lambda value: lax.ppermute(value, axis, ring)]
    concatenate x0 -> x1, other arithmetic: none -> 0.7 us  [per_device(): asked = across(jnp.concatenate([offsets, lengths]))]
  transfers between devices with their start and end apart: 11 -> 11, of which waited for: 8 -> 7; matrix products, arithmetic and copies ran while one was open for 0% -> 0% of each run, Pallas kernels for 4% -> 4%
where the time goes in v6:
time: 49.2 us; the launch traced here: 49.1 us
  waiting for transfers between devices  22.5 us (46%)
  starting transfers between devices  15 us (30%)
  Pallas kernels  8.91 us (18%)
  local copies, waits for them, and re-layouts  1.63 us (3%)
  other arithmetic  0.79 us (2%)
    ppermute x11, waiting for transfers between devices, swap_over(): return lambda value: lax.ppermute(value, axis, ring)  22.5 us
    ppermute x11, starting transfers between devices, swap_over(): return lambda value: lax.ppermute(value, axis, ring)  15 us
    pallas_call x1, Pallas kernels, soundings_partial(): call(functools.partial(fields_body, packed), (floats(tiles * TILE, LANES)...  4.77 us
    unnamed x12, local copies, waits for them, and re-layouts  1.62 us
  transfers between devices with their start and end apart: 11, of which 7 were waited for; matrix products, arithmetic and copies ran while one was open for 0% of the time, Pallas kernels for 4%

profile of v6, /device:TPU:0, one launch (start us, length us, event | category | flops | bytes accessed | tf_op | source)
XLA Modules:
  0.0 49.1 jit_solution(199170435289174545)
XLA Ops:
  0.0 0.7 %pad_add_fusion.1 = s32[4,8]{1,0:T(4,128)S(1)} fusion(s32[2,8]{1,0:T(2,128)} %lengths_ref.1, s32[2,8]{1,0:T(2,128)} %refs_0_.1), kind=kLoop, calls=%fused_computation.5 | loop fusion | flops 32 | bytes 256 | tf_op jit(solution)/shard_map/concatenate | solution.py:430
  0.7 3.0 %collective-permute-start = (s32[4,8]{1,0:T(4,128)S(1)}, s32[4,8]{1,0:T(4,128)S(1)}, u32[]{:S(2)}, u32[]{:S(2)}) collective-permute-start(s32[4,8]{1,0:T(4,128)S(1)} %pad_add_fusion.1), channel_id=1, source_target_pairs={{0,1},{1,0},{2,3},{3,2},{4,5},{5,4},{6,7},{7,6},{8,9},{9,8},{10,11... | collective-permute-start | bytes 392 | tf_op jit(solution)/shard_map/ppermute | solution.py:61
  3.7 0.0 copy-start
  3.7 1.6 %copy-done = f32[4096,1,128]{2,1,0:T(1,128)S(1)} copy-done((f32[4096,1,128]{2,1,0:T(1,128)S(1)}, f32[4096,1,128]{2,1,0:T(1,128)}, u32[]{:S(2)}) %copy-start) | copy-done | bytes 2097176
  5.3 0.1 shard_map.64.block_ref.table_ref.refs_4_
  5.4 0.0 copy-start.3
  5.4 0.0 copy-start.1
  5.4 0.0 copy-start.2
  5.5 0.0 copy-start.4
  5.5 0.0 copy-start.5
  5.5 0.0 collective-permute-done.index_ref.refs_0_
  5.5 0.6 %shard_map.65 = f32[384,128]{1,0:T(8,128)S(1)} custom-call(s32[4,8]{1,0:T(4,128)S(1)} %collective-permute-done.index_ref.refs_0_, f32[4096,128]{1,0:T(8,128)S(1)} %shard_map.64.block_ref.table_ref.refs_4_), custom_call_target="tpu_custom_call" | custom-call | bytes 393216 | tf_op jit(solution)/shard_map/pallas_call | solution.py:106
  6.1 1.8 %collective-permute-start.1 = (f32[384,128]{1,0:T(8,128)S(1)}, f32[384,128]{1,0:T(8,128)S(1)}, u32[]{:S(2)}, u32[]{:S(2)}) collective-permute-start(f32[384,128]{1,0:T(8,128)S(1)} %shard_map.65), channel_id=1, source_target_pairs={{0,1},{1,0},{2,3},{3,2},{4,5},{5,4},{6,7},{7,6},{8,9},{9,8},{10,11... | collective-permute-start | bytes 589832 | tf_op jit(solution)/shard_map/ppermute | solution.py:61
  7.9 0.0 copy-done.3
  7.9 0.1 collective-permute-start.2
  8.0 0.0 copy-done.1
  8.0 0.0 copy-done.2
  8.0 0.9 %shard_map.66 = (f32[3,8,8,8,128]{4,3,2,1,0:T(8,128)S(1)}, f32[3,8,8,8,128]{4,3,2,1,0:T(8,128)S(1)}) custom-call(f32[1536,128]{1,0:T(8,128)S(1)} %bitcast.17, f32[1536,128]{1,0:T(8,128)S(1)} %bitcast.18), custom_call_target="tpu_custom_call" | custom-call | flops 1572864 | bytes 3145728 | tf_op jit(solution)/shard_map/pallas_call | solution.py:146
  9.0 0.2 collective-permute-done.2
  9.2 3.4 %collective-permute-done.1.answer_ref = f32[384,128]{1,0:T(8,128)S(1)} collective-permute-done((f32[384,128]{1,0:T(8,128)S(1)}, f32[384,128]{1,0:T(8,128)S(1)}, u32[]{:S(2)}, u32[]{:S(2)}) %collective-permute-start.1) | collective-permute-done | bytes 196640 | tf_op jit(solution)/shard_map/ppermute | solution.py:61
  12.5 0.0 copy-done.4
  12.5 0.0 copy-done.5
  12.5 4.8 %shard_map.67 = (f32[512,128]{1,0:T(8,128)S(1)}, f32[384,128]{1,0:T(8,128)S(1)}) custom-call(s32[2,8]{1,0:T(2,128)S(1)} %copy-done.3, s32[2,8]{1,0:T(2,128)S(1)} %bitcast.21, s32[2,8]{1,0:T(2,128)S(1)} %copy-done.4, f32[4096,128]{1,0:T(8,128)S(1)} %shard_map.64.block_ref.table_ref.refs_4_, f32[384,128]{1,0:T(8,128)S(1)} %collective-permute-done.1.answer_ref, ...), custom_call_target="tpu_custom_call" | custom-call | flops 32768000 | bytes 2621440 | tf_op jit(solution)/shard_map/pallas_call | solution.py:279
  17.3 1.1 %collective-permute-start.3 = (f32[384,128]{1,0:T(8,128)S(1)}, f32[384,128]{1,0:T(8,128)S(1)}, u32[]{:S(2)}, u32[]{:S(2)}) collective-permute-start(f32[384,128]{1,0:T(8,128)S(1)} %get-tuple-element.24), channel_id=1, source_target_pairs={{0,1},{1,0},{2,3},{3,2},{4,5},{5,4},{6,7},{7,6},{8,9},{9,8},{10,11... | collective-permute-start | bytes 589832 | tf_op jit(solution)/shard_map/ppermute | solution.py:61
  18.5 0.0 collective-permute-start.5
  18.5 4.6 %collective-permute-done.3.refs_1_ = f32[384,128]{1,0:T(8,128)S(1)} collective-permute-done((f32[384,128]{1,0:T(8,128)S(1)}, f32[384,128]{1,0:T(8,128)S(1)}, u32[]{:S(2)}, u32[]{:S(2)}) %collective-permute-start.3) | collective-permute-done | bytes 196640 | tf_op jit(solution)/shard_map/ppermute | solution.py:61
  23.1 0.0 collective-permute-start.4
  23.1 0.0 collective-permute-done.5.refs_3_
  23.1 0.9 %shard_map.68.refs_4_ = f32[2592,128]{1,0:T(8,128)S(1)} custom-call(s32[2,8]{1,0:T(2,128)S(1)} %copy-done.3, f32[16,32,128]{2,1,0:T(8,128)S(1)} %bitcast.20, s32[2,8]{1,0:T(2,128)S(1)} %slice.31.refs_2_, f32[16,32,128]{2,1,0:T(8,128)S(1)} %collective-permute-done.5.refs_3_, f32[4096,128]{1,0:T(8,128)S(1)} %shard_map.64.block_ref.table_ref.refs_4_), custom_call_target="tpu_custom_call" | custom-call | flops 331776 | bytes 2654208 | tf_op jit(solution)/shard_map/pallas_call | solution.py:339
  24.0 0.5 %collective-permute-done.4.refs_3_ = f32[384,128]{1,0:T(8,128)S(1)} collective-permute-done((f32[384,128]{1,0:T(8,128)S(1)}, f32[384,128]{1,0:T(8,128)S(1)}, u32[]{:S(2)}, u32[]{:S(2)}) %collective-permute-start.4) | collective-permute-done | bytes 196640 | tf_op jit(solution)/shard_map/ppermute | solution.py:61
  24.5 0.9 %shard_map.69 = (f32[2592,128]{1,0:T(8,128)S(1)}, f32[4,112,128]{2,1,0:T(8,128)S(1)}, f32[4,112,128]{2,1,0:T(8,128)S(1)}, f32[4,144,128]{2,1,0:T(8,128)S(1)}, f32[4,144,128]{2,1,0:T(8,128)S(1)}) custom-call(s32[4,8]{1,0:T(4,128)S(1)} %collective-permute-done.index_ref.refs_0_, ...), custom_call_target="tpu_custom_call", output_to_operand_aliasing={{0}: (4, {})} | custom-call | flops 331776 | bytes 2654208 | tf_op jit(solution)/shard_map/pallas_call | solution.py:368
  25.4 1.6 %collective-permute-start.8 = (f32[4,144,128]{2,1,0:T(8,128)S(1)}, f32[4,144,128]{2,1,0:T(8,128)S(1)}, u32[]{:S(2)}, u32[]{:S(2)}) collective-permute-start(f32[4,144,128]{2,1,0:T(8,128)S(1)} %get-tuple-element.29), channel_id=1, source_target_pairs={{0,8},{2,10},{4,12},{6,14},{8,0},{10,2},{12,4},{14,6},{16,24},{18,... | collective-permute-start | bytes 884744 | tf_op jit(solution)/shard_map/ppermute | solution.py:61
  27.0 1.5 %collective-permute-start.6 = (f32[4,112,128]{2,1,0:T(8,128)S(1)}, f32[4,112,128]{2,1,0:T(8,128)S(1)}, u32[]{:S(2)}, u32[]{:S(2)}) collective-permute-start(f32[4,112,128]{2,1,0:T(8,128)S(1)} %get-tuple-element.27), channel_id=1, source_target_pairs={{0,4},{2,6},{4,0},{6,2},{8,12},{10,14},{12,8},{14,10},{16,20},{18,... | collective-permute-start | bytes 688136 | tf_op jit(solution)/shard_map/ppermute | solution.py:61
  28.5 5.9 %collective-permute-done.8 = f32[4,144,128]{2,1,0:T(8,128)S(1)} collective-permute-done((f32[4,144,128]{2,1,0:T(8,128)S(1)}, f32[4,144,128]{2,1,0:T(8,128)S(1)}, u32[]{:S(2)}, u32[]{:S(2)}) %collective-permute-start.8) | collective-permute-done | bytes 294944 | tf_op jit(solution)/shard_map/ppermute | solution.py:61
  34.5 1.6 %collective-permute-start.9 = (f32[2,144,128]{2,1,0:T(8,128)S(1)}, f32[2,144,128]{2,1,0:T(8,128)S(1)}, u32[]{:S(2)}, u32[]{:S(2)}) collective-permute-start(f32[2,144,128]{2,1,0:T(8,128)S(1)} %get-tuple-element.34), channel_id=1, source_target_pairs={{0,4},{2,6},{4,0},{6,2},{8,12},{10,14},{12,8},{14,10},{16,20},{18,... | collective-permute-start | bytes 442376 | tf_op jit(solution)/shard_map/ppermute | solution.py:61
  36.1 0.0 collective-permute-done.6
  36.2 1.6 %collective-permute-start.7 = (f32[2,112,128]{2,1,0:T(8,128)S(1)}, f32[2,112,128]{2,1,0:T(8,128)S(1)}, u32[]{:S(2)}, u32[]{:S(2)}) collective-permute-start(f32[2,112,128]{2,1,0:T(8,128)S(1)} %get-tuple-element.36), channel_id=1, source_target_pairs={{0,8},{2,10},{4,12},{6,14},{8,0},{10,2},{12,4},{14,6},{16,24},{18,... | collective-permute-start | bytes 344072 | tf_op jit(solution)/shard_map/ppermute | solution.py:61
  37.8 3.2 %collective-permute-done.7.got_low = f32[2,112,128]{2,1,0:T(8,128)S(1)} collective-permute-done((f32[2,112,128]{2,1,0:T(8,128)S(1)}, f32[2,112,128]{2,1,0:T(8,128)S(1)}, u32[]{:S(2)}, u32[]{:S(2)}) %collective-permute-start.7) | collective-permute-done | bytes 114720 | tf_op jit(solution)/shard_map/ppermute | solution.py:61
  41.0 0.0 collective-permute-done.9.got_high
  41.0 2.7 %collective-permute-start.10 = (f32[1,256,128]{2,1,0:T(8,128)S(1)}, f32[1,256,128]{2,1,0:T(8,128)S(1)}, u32[]{:S(2)}, u32[]{:S(2)}) collective-permute-start(f32[1,256,128]{2,1,0:T(8,128)S(1)} %get-tuple-element.31), channel_id=1, source_target_pairs={{0,16},{2,18},{4,20},{6,22},{8,24},{10,26},{12,28},{14,30},{16,0},... | collective-permute-start | bytes 393224 | tf_op jit(solution)/shard_map/ppermute | solution.py:61
  43.7 4.7 %collective-permute-done.10.got = f32[1,256,128]{2,1,0:T(8,128)S(1)} collective-permute-done((f32[1,256,128]{2,1,0:T(8,128)S(1)}, f32[1,256,128]{2,1,0:T(8,128)S(1)}, u32[]{:S(2)}, u32[]{:S(2)}) %collective-permute-start.10) | collective-permute-done | bytes 131104 | tf_op jit(solution)/shard_map/ppermute | solution.py:61
  48.4 0.7 %shard_map.71 = f32[256,128]{1,0:T(8,128)} custom-call(f32[1,256,128]{2,1,0:T(8,128)S(1)} %collective-permute-done.10.got, f32[1,256,128]{2,1,0:T(8,128)S(1)} %get-tuple-element.32.held), custom_call_target="tpu_custom_call" | custom-call | flops 32768 | bytes 393216 | tf_op jit(solution)/shard_map/pallas_call | solution.py:405
  (6 shorter events, 0.1 us)
Async XLA Ops:
  0.7 4.8 %collective-permute-start = (s32[4,8]{1,0:T(4,128)S(1)}, s32[4,8]{1,0:T(4,128)S(1)}, u32[]{:S(2)}, u32[]{:S(2)}) collective-permute-start(s32[4,8]{1,0:T(4,128)S(1)} %pad_add_fusion.1), channel_id=1, source_target_pairs={{0,1},{1,0},{2,3},{3,2},{4,5},{5,4},{6,7},{7,6},{8,9},{9,8},{10,11... | collective-permute-start | bytes 392 | tf_op jit(solution)/shard_map/ppermute | solution.py:61
  3.7 1.6 %copy-start = (f32[4096,1,128]{2,1,0:T(1,128)S(1)}, f32[4096,1,128]{2,1,0:T(1,128)}, u32[]{:S(2)}) copy-start(f32[4096,1,128]{2,1,0:T(1,128)} %param.6) | copy-start | bytes 6291460
  5.4 2.5 %copy-start.3 = (s32[2,8]{1,0:T(2,128)S(1)}, s32[2,8]{1,0:T(2,128)}, u32[]{:S(2)}) copy-start(s32[2,8]{1,0:T(2,128)} %refs_0_.1) | copy-start | bytes 196
  5.4 2.6 %copy-start.1 = (f32[2,3,8,4096]{3,2,1,0:T(8,128)S(1)}, f32[2,3,8,4096]{3,2,1,0:T(8,128)}, u32[]{:S(2)}) copy-start(f32[2,3,8,4096]{3,2,1,0:T(8,128)} %param.7) | copy-start | bytes 2359300
  5.4 2.6 %copy-start.2 = (f32[2,3,8,4096]{3,2,1,0:T(8,128)S(1)}, f32[2,3,8,4096]{3,2,1,0:T(8,128)}, u32[]{:S(2)}) copy-start(f32[2,3,8,4096]{3,2,1,0:T(8,128)} %param.8) | copy-start | bytes 2359300
  5.5 7.1 %copy-start.4 = (s32[2,8]{1,0:T(2,128)S(1)}, s32[2,8]{1,0:T(2,128)}, u32[]{:S(2)}) copy-start(s32[2,8]{1,0:T(2,128)} %lengths_ref.1) | copy-start | bytes 196
  5.5 7.1 %copy-start.5 = (s32[2,8,1]{1,2,0:T(1,128)S(1)}, s32[2,8,1]{1,2,0:T(1,128)}, u32[]{:S(2)}) copy-start(s32[2,8,1]{1,2,0:T(1,128)} %param.9) | copy-start | bytes 196
  6.1 6.4 %collective-permute-start.1 = (f32[384,128]{1,0:T(8,128)S(1)}, f32[384,128]{1,0:T(8,128)S(1)}, u32[]{:S(2)}, u32[]{:S(2)}) collective-permute-start(f32[384,128]{1,0:T(8,128)S(1)} %shard_map.65), channel_id=1, source_target_pairs={{0,1},{1,0},{2,3},{3,2},{4,5},{5,4},{6,7},{7,6},{8,9},{9,8},{10,11... | collective-permute-start | bytes 589832 | tf_op jit(solution)/shard_map/ppermute | solution.py:61
  7.9 1.2 %collective-permute-start.2 = (s32[6,8]{1,0:T(8,128)S(1)}, s32[6,8]{1,0:T(8,128)S(1)}, u32[]{:S(2)}, u32[]{:S(2)}) collective-permute-start(s32[6,8]{1,0:T(8,128)S(1)} %pad_add_fusion), channel_id=1, source_target_pairs={{0,2},{2,0},{4,6},{6,4},{8,10},{10,8},{12,14},{14,12},{16,18},{18,... | collective-permute-start | bytes 584 | tf_op jit(solution)/shard_map/ppermute | solution.py:61
  17.3 5.7 %collective-permute-start.3 = (f32[384,128]{1,0:T(8,128)S(1)}, f32[384,128]{1,0:T(8,128)S(1)}, u32[]{:S(2)}, u32[]{:S(2)}) collective-permute-start(f32[384,128]{1,0:T(8,128)S(1)} %get-tuple-element.24), channel_id=1, source_target_pairs={{0,1},{1,0},{2,3},{3,2},{4,5},{5,4},{6,7},{7,6},{8,9},{9,8},{10,11... | collective-permute-start | bytes 589832 | tf_op jit(solution)/shard_map/ppermute | solution.py:61
  18.5 4.6 %collective-permute-start.5 = (f32[16,32,128]{2,1,0:T(8,128)S(1)}, f32[16,32,128]{2,1,0:T(8,128)S(1)}, u32[]{:S(2)}, u32[]{:S(2)}) collective-permute-start(f32[16,32,128]{2,1,0:T(8,128)S(1)} %bitcast.19), channel_id=1, source_target_pairs={{0,2},{2,0},{4,6},{6,4},{8,10},{10,8},{12,14},{14,12},{16,18},{18,... | collective-permute-start | bytes 786440 | tf_op jit(solution)/shard_map/ppermute | solution.py:61
  23.1 1.4 %collective-permute-start.4 = (f32[384,128]{1,0:T(8,128)S(1)}, f32[384,128]{1,0:T(8,128)S(1)}, u32[]{:S(2)}, u32[]{:S(2)}) collective-permute-start(f32[384,128]{1,0:T(8,128)S(1)} %collective-permute-done.3.refs_1_), channel_id=1, source_target_pairs={{0,2},{2,0},{4,6},{6,4},{8,10},{10,8},{12,14},{14,12},{16,18},{18,... | collective-permute-start | bytes 589832 | tf_op jit(solution)/shard_map/ppermute | solution.py:61
  25.4 9.1 %collective-permute-start.8 = (f32[4,144,128]{2,1,0:T(8,128)S(1)}, f32[4,144,128]{2,1,0:T(8,128)S(1)}, u32[]{:S(2)}, u32[]{:S(2)}) collective-permute-start(f32[4,144,128]{2,1,0:T(8,128)S(1)} %get-tuple-element.29), channel_id=1, source_target_pairs={{0,8},{2,10},{4,12},{6,14},{8,0},{10,2},{12,4},{14,6},{16,24},{18,... | collective-permute-start | bytes 884744 | tf_op jit(solution)/shard_map/ppermute | solution.py:61
  27.0 9.1 %collective-permute-start.6 = (f32[4,112,128]{2,1,0:T(8,128)S(1)}, f32[4,112,128]{2,1,0:T(8,128)S(1)}, u32[]{:S(2)}, u32[]{:S(2)}) collective-permute-start(f32[4,112,128]{2,1,0:T(8,128)S(1)} %get-tuple-element.27), channel_id=1, source_target_pairs={{0,4},{2,6},{4,0},{6,2},{8,12},{10,14},{12,8},{14,10},{16,20},{18,... | collective-permute-start | bytes 688136 | tf_op jit(solution)/shard_map/ppermute | solution.py:61
  34.5 6.5 %collective-permute-start.9 = (f32[2,144,128]{2,1,0:T(8,128)S(1)}, f32[2,144,128]{2,1,0:T(8,128)S(1)}, u32[]{:S(2)}, u32[]{:S(2)}) collective-permute-start(f32[2,144,128]{2,1,0:T(8,128)S(1)} %get-tuple-element.34), channel_id=1, source_target_pairs={{0,4},{2,6},{4,0},{6,2},{8,12},{10,14},{12,8},{14,10},{16,20},{18,... | collective-permute-start | bytes 442376 | tf_op jit(solution)/shard_map/ppermute | solution.py:61
  36.2 4.9 %collective-permute-start.7 = (f32[2,112,128]{2,1,0:T(8,128)S(1)}, f32[2,112,128]{2,1,0:T(8,128)S(1)}, u32[]{:S(2)}, u32[]{:S(2)}) collective-permute-start(f32[2,112,128]{2,1,0:T(8,128)S(1)} %get-tuple-element.36), channel_id=1, source_target_pairs={{0,8},{2,10},{4,12},{6,14},{8,0},{10,2},{12,4},{14,6},{16,24},{18,... | collective-permute-start | bytes 344072 | tf_op jit(solution)/shard_map/ppermute | solution.py:61
  41.0 7.3 %collective-permute-start.10 = (f32[1,256,128]{2,1,0:T(8,128)S(1)}, f32[1,256,128]{2,1,0:T(8,128)S(1)}, u32[]{:S(2)}, u32[]{:S(2)}) collective-permute-start(f32[1,256,128]{2,1,0:T(8,128)S(1)} %get-tuple-element.31), channel_id=1, source_target_pairs={{0,16},{2,18},{4,20},{6,22},{8,24},{10,26},{12,28},{14,30},{16,0},... | collective-permute-start | bytes 393224 | tf_op jit(solution)/shard_map/ppermute | solution.py:61

commit v7 on v6

--- a/solution.py
+++ b/solution.py
@@ -342,35 +342,35 @@
     )(*flat, block)
 
 
-def low_rows(share):
-    return max(1, share * 7 // 128) * SUB
+PIECES = 4
 
 
 def last_body(orders, groups, share, count, *refs):
     total, outs, padded = refs[2 * count + 1], refs[2 * count + 2 : -1], refs[-1]
-    span, slots, half = share + 2 * TILE, groups // 2, low_rows(share)
+    span, slots, piece = share + 2 * TILE, groups // 2, share // PIECES
     for i in range(count):
         add_terms(*refs[2 * i : 2 * i + 2], total, share, slots, padded)
-    for which, order in enumerate(orders):
-        for place, slot in enumerate(arranged(order)):
+    for which in range(PIECES):
+        for place, slot in enumerate(arranged(orders[which % 2])):
             out = outs[2 * which + (place * 2 >= slots)]
-            begin = slot * span + TILE + which * half
-            out[place % (slots // 2)] = total[begin : begin + out.shape[1], :]
+            begin = slot * span + TILE + which * piece
+            out[place % (slots // 2)] = total[begin : begin + piece, :]
 
 
 def last_sums(groups_of, total, rows, orders):
     groups = lax.axis_size("grp")
     share, slots = rows // groups, groups // 2
-    low, high = (floats(slots // 2, r, LANES) for r in (low_rows(share), share - low_rows(share)))
-    terms_rows = max(a.shape[0] for _, a in groups_of)
+    out = floats(slots // 2, share // PIECES, LANES)
     flat = [a for pair in groups_of for a in pair]
     count = len(groups_of)
-    return call(
+    terms_rows = max(a.shape[0] for _, a in groups_of)
+    outs = call(
         functools.partial(last_body, orders, groups, share, count),
-        (floats(*total.shape), low, low, high, high), [SMEM, VMEM] * count + [VMEM],
+        (floats(*total.shape),) + (out,) * (2 * PIECES), [SMEM, VMEM] * count + [VMEM],
         total.size, 8 * total.size, input_output_aliases={2 * count: 0},
         scratch_shapes=[padded_rows(terms_rows + TILE)],
     )(*flat, total)[1:]
+    return [outs[4 * i : 4 * i + 4] for i in range(PIECES // 2)]
 
 
 def join_body(got_low, low, got_high, high, give_ref, keep_ref):
@@ -380,31 +380,41 @@
         keep_ref[:, rows] = got[cut:] + held[cut:]
 
 
-def finish_body(got, held, out_ref):
-    out_ref[...] = got[0] + held[0]
-
-
-def halve(low_give, low, high_give, high, orders):
+def finish_body(*refs):
+    out_ref = refs[-1]
+    for i in range(0, len(refs) - 1, 2):
+        got, held = refs[i : i + 2]
+        rows = got.shape[1]
+        out_ref[i // 2 * rows : (i // 2 + 1) * rows] = got[0] + held[0]
+
+
+def halve(stages, orders):
     bit_pairs = list(zip(*orders))
+    state = list(stages)
     for step, (low_bit, high_bit) in enumerate(bit_pairs[:2]):
-        got_low = swap_over("grp", 2 << low_bit)(low_give)
-        got_high = swap_over("grp", 2 << high_bit)(high_give)
-        cut = low.shape[0] // 2
-        if step == 0:
-            low_give, low = got_low[:cut] + low[:cut], got_low[cut:] + low[cut:]
-            high_give, high = got_high[:cut] + high[:cut], got_high[cut:] + high[cut:]
-    out = floats(cut, low.shape[1] + high.shape[1], LANES)
-    give, keep = call(
-        join_body, (out, out), [VMEM] * 4, low.size, 24 * low.size
-    )(got_low, low, got_high, high)
-    for bit, _ in bit_pairs[2:]:
-        got = swap_over("grp", 2 << bit)(give)
-        cut = keep.shape[0] // 2
-        if cut:
-            give, keep = got[:cut] + keep[:cut], got[cut:] + keep[cut:]
-    return call(
-        finish_body, floats(*keep.shape[1:]), [VMEM] * 2, keep.size, 12 * keep.size
-    )(got, keep)
+        for i, (low_give, low, high_give, high) in enumerate(state):
+            got_low = swap_over("grp", 2 << low_bit)(low_give)
+            got_high = swap_over("grp", 2 << high_bit)(high_give)
+            cut = low.shape[0] // 2
+            if step == 0:
+                low_give, low = got_low[:cut] + low[:cut], got_low[cut:] + low[cut:]
+                high_give, high = got_high[:cut] + high[:cut], got_high[cut:] + high[cut:]
+                state[i] = low_give, low, high_give, high
+            else:
+                out = floats(cut, low.shape[1] + high.shape[1], LANES)
+                state[i] = call(
+                    join_body, (out, out), [VMEM] * 4, low.size, 24 * low.size
+                )(got_low, low, got_high, high)
+    last = []
+    for give, keep in state:
+        for bit, _ in bit_pairs[2:]:
+            got = swap_over("grp", 2 << bit)(give)
+            cut = keep.shape[0] // 2
+            if cut:
+                give, keep = got[:cut] + keep[:cut], got[cut:] + keep[cut:]
+        last += [got, keep]
+    out = floats(sum(a.shape[1] for a in last) // 2, LANES)
+    return call(finish_body, out, [VMEM] * len(last), out.size, 12 * out.size)(*last)
 
 
 def hold_body(block_ref, out_ref, sem):
@@ -465,7 +475,7 @@
 
     bits = tuple(range(groups.bit_length() - 2))
     orders = (bits, bits[1:2] + bits[0:1] + bits[2:])
-    sums = halve(*last_sums(final, total, rows, orders), orders)
+    sums = halve(last_sums(final, total, rows, orders), orders)
     return sums[:, None, :]
 
 

time: 49.2 us -> 47.2 us (0.959)
  waiting for transfers between devices: 22.5 us -> 15 us
  starting transfers between devices: 15 us -> 20.6 us
    ppermute x11 -> x16, waiting for transfers between devices: 22.5 us -> 15 us  [swap_over(): return lambda value: lax.ppermute(value, axis, ring)]
    ppermute x11 -> x16, starting transfers between devices: 15 us -> 20.6 us  [swap_over(): return lambda value: lax.ppermute(value, axis, ring)]
  transfers between devices with their start and end apart: 11 -> 16, of which waited for: 7 -> 9; matrix products, arithmetic and copies ran while one was open for 0% -> 0% of each run, Pallas kernels for 4% -> 4%
where the time goes in v7:
time: 47.2 us; the launch traced here: 47.1 us
  starting transfers between devices  20.6 us (44%)
  waiting for transfers between devices  15 us (32%)
  Pallas kernels  8.92 us (19%)
  local copies, waits for them, and re-layouts  1.63 us (3%)
  other arithmetic  0.78 us (2%)
    ppermute x16, starting transfers between devices, swap_over(): return lambda value: lax.ppermute(value, axis, ring)  20.6 us
    ppermute x16, waiting for transfers between devices, swap_over(): return lambda value: lax.ppermute(value, axis, ring)  15 us
    pallas_call x1, Pallas kernels, soundings_partial(): call(functools.partial(fields_body, packed), (floats(tiles * TILE, LANES)...  4.77 us
    unnamed x12, local copies, waits for them, and re-layouts  1.62 us
  transfers between devices with their start and end apart: 16, of which 9 were waited for; matrix products, arithmetic and copies ran while one was open for 0% of the time, Pallas kernels for 4%

profile of v7, /device:TPU:0, one launch (start us, length us, event | category | flops | bytes accessed | tf_op | source)
XLA Modules:
  0.0 47.1 jit_solution(12111130490268186672)
XLA Ops:
  0.0 0.7 %pad_add_fusion.1 = s32[4,8]{1,0:T(4,128)S(1)} fusion(s32[2,8]{1,0:T(2,128)} %lengths_ref.1, s32[2,8]{1,0:T(2,128)} %refs_0_.1), kind=kLoop, calls=%fused_computation.9 | loop fusion | flops 32 | bytes 256 | tf_op jit(solution)/shard_map/concatenate | solution.py:440
  0.7 3.0 %collective-permute-start = (s32[4,8]{1,0:T(4,128)S(1)}, s32[4,8]{1,0:T(4,128)S(1)}, u32[]{:S(2)}, u32[]{:S(2)}) collective-permute-start(s32[4,8]{1,0:T(4,128)S(1)} %pad_add_fusion.1), channel_id=1, source_target_pairs={{0,1},{1,0},{2,3},{3,2},{4,5},{5,4},{6,7},{7,6},{8,9},{9,8},{10,11... | collective-permute-start | bytes 392 | tf_op jit(solution)/shard_map/ppermute | solution.py:61
  3.7 1.6 %copy-done = f32[4096,1,128]{2,1,0:T(1,128)S(1)} copy-done((f32[4096,1,128]{2,1,0:T(1,128)S(1)}, f32[4096,1,128]{2,1,0:T(1,128)}, u32[]{:S(2)}) %copy-start) | copy-done | bytes 2097176
  5.3 0.1 shard_map.64.block_ref.table_ref.refs_4_
  5.4 0.0 copy-start.3
  5.4 0.0 copy-start.1
  5.4 0.0 copy-start.2
  5.5 0.0 copy-start.4
  5.5 0.0 copy-start.5
  5.5 0.0 collective-permute-done.index_ref.refs_0_
  5.5 0.6 %shard_map.65 = f32[384,128]{1,0:T(8,128)S(1)} custom-call(s32[4,8]{1,0:T(4,128)S(1)} %collective-permute-done.index_ref.refs_0_, f32[4096,128]{1,0:T(8,128)S(1)} %shard_map.64.block_ref.table_ref.refs_4_), custom_call_target="tpu_custom_call" | custom-call | bytes 393216 | tf_op jit(solution)/shard_map/pallas_call | solution.py:106
  6.1 1.8 %collective-permute-start.1 = (f32[384,128]{1,0:T(8,128)S(1)}, f32[384,128]{1,0:T(8,128)S(1)}, u32[]{:S(2)}, u32[]{:S(2)}) collective-permute-start(f32[384,128]{1,0:T(8,128)S(1)} %shard_map.65), channel_id=1, source_target_pairs={{0,1},{1,0},{2,3},{3,2},{4,5},{5,4},{6,7},{7,6},{8,9},{9,8},{10,11... | collective-permute-start | bytes 589832 | tf_op jit(solution)/shard_map/ppermute | solution.py:61
  7.9 0.0 copy-done.3
  7.9 0.1 collective-permute-start.2
  8.0 0.0 copy-done.1
  8.0 0.9 %shard_map.66 = (f32[3,8,8,8,128]{4,3,2,1,0:T(8,128)S(1)}, f32[3,8,8,8,128]{4,3,2,1,0:T(8,128)S(1)}) custom-call(f32[1536,128]{1,0:T(8,128)S(1)} %bitcast.17, f32[1536,128]{1,0:T(8,128)S(1)} %bitcast.18), custom_call_target="tpu_custom_call" | custom-call | flops 1572864 | bytes 3145728 | tf_op jit(solution)/shard_map/pallas_call | solution.py:146
  9.0 0.2 collective-permute-done.2
  9.2 3.4 %collective-permute-done.1.answer_ref = f32[384,128]{1,0:T(8,128)S(1)} collective-permute-done((f32[384,128]{1,0:T(8,128)S(1)}, f32[384,128]{1,0:T(8,128)S(1)}, u32[]{:S(2)}, u32[]{:S(2)}) %collective-permute-start.1) | collective-permute-done | bytes 196640 | tf_op jit(solution)/shard_map/ppermute | solution.py:61
  12.5 4.8 %shard_map.67 = (f32[512,128]{1,0:T(8,128)S(1)}, f32[384,128]{1,0:T(8,128)S(1)}) custom-call(s32[2,8]{1,0:T(2,128)S(1)} %copy-done.3, s32[2,8]{1,0:T(2,128)S(1)} %bitcast.21, s32[2,8]{1,0:T(2,128)S(1)} %copy-done.4, f32[4096,128]{1,0:T(8,128)S(1)} %shard_map.64.block_ref.table_ref.refs_4_, f32[384,128]{1,0:T(8,128)S(1)} %collective-permute-done.1.answer_ref, ...), custom_call_target="tpu_custom_call" | custom-call | flops 32768000 | bytes 2621440 | tf_op jit(solution)/shard_map/pallas_call | solution.py:279
  17.3 1.1 %collective-permute-start.3 = (f32[384,128]{1,0:T(8,128)S(1)}, f32[384,128]{1,0:T(8,128)S(1)}, u32[]{:S(2)}, u32[]{:S(2)}) collective-permute-start(f32[384,128]{1,0:T(8,128)S(1)} %get-tuple-element.30), channel_id=1, source_target_pairs={{0,1},{1,0},{2,3},{3,2},{4,5},{5,4},{6,7},{7,6},{8,9},{9,8},{10,11... | collective-permute-start | bytes 589832 | tf_op jit(solution)/shard_map/ppermute | solution.py:61
  18.5 0.0 collective-permute-start.5
  18.5 4.6 %collective-permute-done.3.refs_1_ = f32[384,128]{1,0:T(8,128)S(1)} collective-permute-done((f32[384,128]{1,0:T(8,128)S(1)}, f32[384,128]{1,0:T(8,128)S(1)}, u32[]{:S(2)}, u32[]{:S(2)}) %collective-permute-start.3) | collective-permute-done | bytes 196640 | tf_op jit(solution)/shard_map/ppermute | solution.py:61
  23.1 0.0 collective-permute-start.4
  23.1 0.0 collective-permute-done.5.refs_3_
  23.1 0.9 %shard_map.68.refs_4_ = f32[2592,128]{1,0:T(8,128)S(1)} custom-call(s32[2,8]{1,0:T(2,128)S(1)} %copy-done.3, f32[16,32,128]{2,1,0:T(8,128)S(1)} %bitcast.20, s32[2,8]{1,0:T(2,128)S(1)} %slice.55.refs_2_, f32[16,32,128]{2,1,0:T(8,128)S(1)} %collective-permute-done.5.refs_3_, f32[4096,128]{1,0:T(8,128)S(1)} %shard_map.64.block_ref.table_ref.refs_4_), custom_call_target="tpu_custom_call" | custom-call | flops 331776 | bytes 2654208 | tf_op jit(solution)/shard_map/pallas_call | solution.py:339
  24.0 0.5 %collective-permute-done.4.refs_3_ = f32[384,128]{1,0:T(8,128)S(1)} collective-permute-done((f32[384,128]{1,0:T(8,128)S(1)}, f32[384,128]{1,0:T(8,128)S(1)}, u32[]{:S(2)}, u32[]{:S(2)}) %collective-permute-start.4) | collective-permute-done | bytes 196640 | tf_op jit(solution)/shard_map/ppermute | solution.py:61
  24.5 0.9 %shard_map.69 = (f32[2592,128]{1,0:T(8,128)S(1)}, f32[4,64,128]{2,1,0:T(8,128)S(1)}, f32[4,64,128]{2,1,0:T(8,128)S(1)}, f32[4,64,128]{2,1,0:T(8,128)S(1)}, f32[4...) custom-call(s32[4,8]{1,0:T(4,128)S(1)} %collective-permute-done.inde, ...), custom_call_target="tpu_custom_call", output_to_operand_aliasing={{0}: (4, {})} | custom-call | flops 331776 | bytes 2654208 | tf_op jit(solution)/shard_map/pallas_call | solution.py:367
  25.4 1.6 %collective-permute-start.13 = (f32[4,64,128]{2,1,0:T(8,128)S(1)}, f32[4,64,128]{2,1,0:T(8,128)S(1)}, u32[]{:S(2)}, u32[]{:S(2)}) collective-permute-start(f32[4,64,128]{2,1,0:T(8,128)S(1)} %get-tuple-element.41), channel_id=1, source_target_pairs={{0,8},{2,10},{4,12},{6,14},{8,0},{10,2},{12,4},{14,6},{16,24},{18,... | collective-permute-start | bytes 393224 | tf_op jit(solution)/shard_map/ppermute | solution.py:61
  27.0 1.5 %collective-permute-start.11 = (f32[4,64,128]{2,1,0:T(8,128)S(1)}, f32[4,64,128]{2,1,0:T(8,128)S(1)}, u32[]{:S(2)}, u32[]{:S(2)}) collective-permute-start(f32[4,64,128]{2,1,0:T(8,128)S(1)} %get-tuple-element.39), channel_id=1, source_target_pairs={{0,4},{2,6},{4,0},{6,2},{8,12},{10,14},{12,8},{14,10},{16,20},{18,... | collective-permute-start | bytes 393224 | tf_op jit(solution)/shard_map/ppermute | solution.py:61
  28.5 0.4 collective-permute-start.8
  29.0 0.5 %collective-permute-start.6 = (f32[4,64,128]{2,1,0:T(8,128)S(1)}, f32[4,64,128]{2,1,0:T(8,128)S(1)}, u32[]{:S(2)}, u32[]{:S(2)}) collective-permute-start(f32[4,64,128]{2,1,0:T(8,128)S(1)} %get-tuple-element.33), channel_id=1, source_target_pairs={{0,4},{2,6},{4,0},{6,2},{8,12},{10,14},{12,8},{14,10},{16,20},{18,... | collective-permute-start | bytes 393224 | tf_op jit(solution)/shard_map/ppermute | solution.py:61
  29.5 1.8 %collective-permute-done.13 = f32[4,64,128]{2,1,0:T(8,128)S(1)} collective-permute-done((f32[4,64,128]{2,1,0:T(8,128)S(1)}, f32[4,64,128]{2,1,0:T(8,128)S(1)}, u32[]{:S(2)}, u32[]{:S(2)}) %collective-permute-start.13) | collective-permute-done | bytes 131104 | tf_op jit(solution)/shard_map/ppermute | solution.py:61
  31.3 2.1 %collective-permute-start.14 = (f32[2,64,128]{2,1,0:T(8,128)S(1)}, f32[2,64,128]{2,1,0:T(8,128)S(1)}, u32[]{:S(2)}, u32[]{:S(2)}) collective-permute-start(f32[2,64,128]{2,1,0:T(8,128)S(1)} %get-tuple-element.46), channel_id=1, source_target_pairs={{0,4},{2,6},{4,0},{6,2},{8,12},{10,14},{12,8},{14,10},{16,20},{18,... | collective-permute-start | bytes 196616 | tf_op jit(solution)/shard_map/ppermute | solution.py:61
  33.4 0.0 collective-permute-done.11
  33.4 1.6 %collective-permute-start.12 = (f32[2,64,128]{2,1,0:T(8,128)S(1)}, f32[2,64,128]{2,1,0:T(8,128)S(1)}, u32[]{:S(2)}, u32[]{:S(2)}) collective-permute-start(f32[2,64,128]{2,1,0:T(8,128)S(1)} %get-tuple-element.48), channel_id=1, source_target_pairs={{0,8},{2,10},{4,12},{6,14},{8,0},{10,2},{12,4},{14,6},{16,24},{18,... | collective-permute-start | bytes 196616 | tf_op jit(solution)/shard_map/ppermute | solution.py:61
  35.1 0.0 collective-permute-done.8
  35.1 0.6 %collective-permute-start.9 = (f32[2,64,128]{2,1,0:T(8,128)S(1)}, f32[2,64,128]{2,1,0:T(8,128)S(1)}, u32[]{:S(2)}, u32[]{:S(2)}) collective-permute-start(f32[2,64,128]{2,1,0:T(8,128)S(1)} %get-tuple-element.50), channel_id=1, source_target_pairs={{0,4},{2,6},{4,0},{6,2},{8,12},{10,14},{12,8},{14,10},{16,20},{18,... | collective-permute-start | bytes 196616 | tf_op jit(solution)/shard_map/ppermute | solution.py:61
  35.7 0.3 collective-permute-done.6
  35.9 1.6 %collective-permute-start.7 = (f32[2,64,128]{2,1,0:T(8,128)S(1)}, f32[2,64,128]{2,1,0:T(8,128)S(1)}, u32[]{:S(2)}, u32[]{:S(2)}) collective-permute-start(f32[2,64,128]{2,1,0:T(8,128)S(1)} %get-tuple-element.52), channel_id=1, source_target_pairs={{0,8},{2,10},{4,12},{6,14},{8,0},{10,2},{12,4},{14,6},{16,24},{18,... | collective-permute-start | bytes 196616 | tf_op jit(solution)/shard_map/ppermute | solution.py:61
  37.6 0.0 collective-permute-done.14.got_high
  37.6 0.9 %collective-permute-done.12.got_low = f32[2,64,128]{2,1,0:T(8,128)S(1)} collective-permute-done((f32[2,64,128]{2,1,0:T(8,128)S(1)}, f32[2,64,128]{2,1,0:T(8,128)S(1)}, u32[]{:S(2)}, u32[]{:S(2)}) %collective-permute-start.12) | collective-permute-done | bytes 65568 | tf_op jit(solution)/shard_map/ppermute | solution.py:61
  38.5 2.7 %collective-permute-start.15 = (f32[1,128,128]{2,1,0:T(8,128)S(1)}, f32[1,128,128]{2,1,0:T(8,128)S(1)}, u32[]{:S(2)}, u32[]{:S(2)}) collective-permute-start(f32[1,128,128]{2,1,0:T(8,128)S(1)} %get-tuple-element.43), channel_id=1, source_target_pairs={{0,16},{2,18},{4,20},{6,22},{8,24},{10,26},{12,28},{14,30},{16,0},... | collective-permute-start | bytes 196616 | tf_op jit(solution)/shard_map/ppermute | solution.py:61
  41.1 0.0 collective-permute-done.9.got_high
  41.1 0.0 collective-permute-done.7.got_low
  41.2 1.8 %collective-permute-start.10 = (f32[1,128,128]{2,1,0:T(8,128)S(1)}, f32[1,128,128]{2,1,0:T(8,128)S(1)}, u32[]{:S(2)}, u32[]{:S(2)}) collective-permute-start(f32[1,128,128]{2,1,0:T(8,128)S(1)} %get-tuple-element.37), channel_id=1, source_target_pairs={{0,16},{2,18},{4,20},{6,22},{8,24},{10,26},{12,28},{14,30},{16,0},... | collective-permute-start | bytes 196616 | tf_op jit(solution)/shard_map/ppermute | solution.py:61
  43.0 0.7 %collective-permute-done.15.refs_2_ = f32[1,128,128]{2,1,0:T(8,128)S(1)} collective-permute-done((f32[1,128,128]{2,1,0:T(8,128)S(1)}, f32[1,128,128]{2,1,0:T(8,128)S(1)}, u32[]{:S(2)}, u32[]{:S(2)}) %collective-permute-start.15) | collective-permute-done | bytes 65568 | tf_op jit(solution)/shard_map/ppermute | solution.py:61
  43.7 2.7 %collective-permute-done.10.refs_0_ = f32[1,128,128]{2,1,0:T(8,128)S(1)} collective-permute-done((f32[1,128,128]{2,1,0:T(8,128)S(1)}, f32[1,128,128]{2,1,0:T(8,128)S(1)}, u32[]{:S(2)}, u32[]{:S(2)}) %collective-permute-start.10) | collective-permute-done | bytes 65568 | tf_op jit(solution)/shard_map/ppermute | solution.py:61
  46.4 0.7 %shard_map.72 = f32[256,128]{1,0:T(8,128)} custom-call(f32[1,128,128]{2,1,0:T(8,128)S(1)} %collective-permute-done.10.refs_0_, f32[1,128,128]{2,1,0:T(8,128)S(1)} %get-tuple-element.38.refs_1_, f32[1,128,128]{2,1,0:T(8,128)S(1)} %collective-permute-done.15.refs_2_, f32[1,128,128]{2,1,0:T(8,128)S(1)} %get-tuple-element.44.refs_3_), custom_call_target="tpu_custom_call" | custom-call | flops 32768 | bytes 393216 | tf_op jit(solution)/shard_map/pallas_call | solution.py:417
  (13 shorter events, 0.1 us)
Async XLA Ops:
  0.7 4.8 %collective-permute-start = (s32[4,8]{1,0:T(4,128)S(1)}, s32[4,8]{1,0:T(4,128)S(1)}, u32[]{:S(2)}, u32[]{:S(2)}) collective-permute-start(s32[4,8]{1,0:T(4,128)S(1)} %pad_add_fusion.1), channel_id=1, source_target_pairs={{0,1},{1,0},{2,3},{3,2},{4,5},{5,4},{6,7},{7,6},{8,9},{9,8},{10,11... | collective-permute-start | bytes 392 | tf_op jit(solution)/shard_map/ppermute | solution.py:61
  3.7 1.6 %copy-start = (f32[4096,1,128]{2,1,0:T(1,128)S(1)}, f32[4096,1,128]{2,1,0:T(1,128)}, u32[]{:S(2)}) copy-start(f32[4096,1,128]{2,1,0:T(1,128)} %param.6) | copy-start | bytes 6291460
  5.4 2.5 %copy-start.3 = (s32[2,8]{1,0:T(2,128)S(1)}, s32[2,8]{1,0:T(2,128)}, u32[]{:S(2)}) copy-start(s32[2,8]{1,0:T(2,128)} %refs_0_.1) | copy-start | bytes 196
  5.4 2.6 %copy-start.1 = (f32[2,3,8,4096]{3,2,1,0:T(8,128)S(1)}, f32[2,3,8,4096]{3,2,1,0:T(8,128)}, u32[]{:S(2)}) copy-start(f32[2,3,8,4096]{3,2,1,0:T(8,128)} %param.7) | copy-start | bytes 2359300
  5.4 2.6 %copy-start.2 = (f32[2,3,8,4096]{3,2,1,0:T(8,128)S(1)}, f32[2,3,8,4096]{3,2,1,0:T(8,128)}, u32[]{:S(2)}) copy-start(f32[2,3,8,4096]{3,2,1,0:T(8,128)} %param.8) | copy-start | bytes 2359300
  5.5 7.1 %copy-start.4 = (s32[2,8]{1,0:T(2,128)S(1)}, s32[2,8]{1,0:T(2,128)}, u32[]{:S(2)}) copy-start(s32[2,8]{1,0:T(2,128)} %lengths_ref.1) | copy-start | bytes 196
  5.5 7.1 %copy-start.5 = (s32[2,8,1]{1,2,0:T(1,128)S(1)}, s32[2,8,1]{1,2,0:T(1,128)}, u32[]{:S(2)}) copy-start(s32[2,8,1]{1,2,0:T(1,128)} %param.9) | copy-start | bytes 196
  6.1 6.4 %collective-permute-start.1 = (f32[384,128]{1,0:T(8,128)S(1)}, f32[384,128]{1,0:T(8,128)S(1)}, u32[]{:S(2)}, u32[]{:S(2)}) collective-permute-start(f32[384,128]{1,0:T(8,128)S(1)} %shard_map.65), channel_id=1, source_target_pairs={{0,1},{1,0},{2,3},{3,2},{4,5},{5,4},{6,7},{7,6},{8,9},{9,8},{10,11... | collective-permute-start | bytes 589832 | tf_op jit(solution)/shard_map/ppermute | solution.py:61
  7.9 1.2 %collective-permute-start.2 = (s32[6,8]{1,0:T(8,128)S(1)}, s32[6,8]{1,0:T(8,128)S(1)}, u32[]{:S(2)}, u32[]{:S(2)}) collective-permute-start(s32[6,8]{1,0:T(8,128)S(1)} %pad_add_fusion), channel_id=1, source_target_pairs={{0,2},{2,0},{4,6},{6,4},{8,10},{10,8},{12,14},{14,12},{16,18},{18,... | collective-permute-start | bytes 584 | tf_op jit(solution)/shard_map/ppermute | solution.py:61
  17.3 5.7 %collective-permute-start.3 = (f32[384,128]{1,0:T(8,128)S(1)}, f32[384,128]{1,0:T(8,128)S(1)}, u32[]{:S(2)}, u32[]{:S(2)}) collective-permute-start(f32[384,128]{1,0:T(8,128)S(1)} %get-tuple-element.30), channel_id=1, source_target_pairs={{0,1},{1,0},{2,3},{3,2},{4,5},{5,4},{6,7},{7,6},{8,9},{9,8},{10,11... | collective-permute-start | bytes 589832 | tf_op jit(solution)/shard_map/ppermute | solution.py:61
  18.5 4.6 %collective-permute-start.5 = (f32[16,32,128]{2,1,0:T(8,128)S(1)}, f32[16,32,128]{2,1,0:T(8,128)S(1)}, u32[]{:S(2)}, u32[]{:S(2)}) collective-permute-start(f32[16,32,128]{2,1,0:T(8,128)S(1)} %bitcast.19), channel_id=1, source_target_pairs={{0,2},{2,0},{4,6},{6,4},{8,10},{10,8},{12,14},{14,12},{16,18},{18,... | collective-permute-start | bytes 786440 | tf_op jit(solution)/shard_map/ppermute | solution.py:61
  23.1 1.4 %collective-permute-start.4 = (f32[384,128]{1,0:T(8,128)S(1)}, f32[384,128]{1,0:T(8,128)S(1)}, u32[]{:S(2)}, u32[]{:S(2)}) collective-permute-start(f32[384,128]{1,0:T(8,128)S(1)} %collective-permute-done.3.refs_1_), channel_id=1, source_target_pairs={{0,2},{2,0},{4,6},{6,4},{8,10},{10,8},{12,14},{14,12},{16,18},{18,... | collective-permute-start | bytes 589832 | tf_op jit(solution)/shard_map/ppermute | solution.py:61
  25.4 5.9 %collective-permute-start.13 = (f32[4,64,128]{2,1,0:T(8,128)S(1)}, f32[4,64,128]{2,1,0:T(8,128)S(1)}, u32[]{:S(2)}, u32[]{:S(2)}) collective-permute-start(f32[4,64,128]{2,1,0:T(8,128)S(1)} %get-tuple-element.41), channel_id=1, source_target_pairs={{0,8},{2,10},{4,12},{6,14},{8,0},{10,2},{12,4},{14,6},{16,24},{18,... | collective-permute-start | bytes 393224 | tf_op jit(solution)/shard_map/ppermute | solution.py:61
  27.0 6.4 %collective-permute-start.11 = (f32[4,64,128]{2,1,0:T(8,128)S(1)}, f32[4,64,128]{2,1,0:T(8,128)S(1)}, u32[]{:S(2)}, u32[]{:S(2)}) collective-permute-start(f32[4,64,128]{2,1,0:T(8,128)S(1)} %get-tuple-element.39), channel_id=1, source_target_pairs={{0,4},{2,6},{4,0},{6,2},{8,12},{10,14},{12,8},{14,10},{16,20},{18,... | collective-permute-start | bytes 393224 | tf_op jit(solution)/shard_map/ppermute | solution.py:61
  28.5 6.5 %collective-permute-start.8 = (f32[4,64,128]{2,1,0:T(8,128)S(1)}, f32[4,64,128]{2,1,0:T(8,128)S(1)}, u32[]{:S(2)}, u32[]{:S(2)}) collective-permute-start(f32[4,64,128]{2,1,0:T(8,128)S(1)} %get-tuple-element.35), channel_id=1, source_target_pairs={{0,8},{2,10},{4,12},{6,14},{8,0},{10,2},{12,4},{14,6},{16,24},{18,... | collective-permute-start | bytes 393224 | tf_op jit(solution)/shard_map/ppermute | solution.py:61
  29.0 6.9 %collective-permute-start.6 = (f32[4,64,128]{2,1,0:T(8,128)S(1)}, f32[4,64,128]{2,1,0:T(8,128)S(1)}, u32[]{:S(2)}, u32[]{:S(2)}) collective-permute-start(f32[4,64,128]{2,1,0:T(8,128)S(1)} %get-tuple-element.33), channel_id=1, source_target_pairs={{0,4},{2,6},{4,0},{6,2},{8,12},{10,14},{12,8},{14,10},{16,20},{18,... | collective-permute-start | bytes 393224 | tf_op jit(solution)/shard_map/ppermute | solution.py:61
  31.3 6.3 %collective-permute-start.14 = (f32[2,64,128]{2,1,0:T(8,128)S(1)}, f32[2,64,128]{2,1,0:T(8,128)S(1)}, u32[]{:S(2)}, u32[]{:S(2)}) collective-permute-start(f32[2,64,128]{2,1,0:T(8,128)S(1)} %get-tuple-element.46), channel_id=1, source_target_pairs={{0,4},{2,6},{4,0},{6,2},{8,12},{10,14},{12,8},{14,10},{16,20},{18,... | collective-permute-start | bytes 196616 | tf_op jit(solution)/shard_map/ppermute | solution.py:61
  33.4 5.0 %collective-permute-start.12 = (f32[2,64,128]{2,1,0:T(8,128)S(1)}, f32[2,64,128]{2,1,0:T(8,128)S(1)}, u32[]{:S(2)}, u32[]{:S(2)}) collective-permute-start(f32[2,64,128]{2,1,0:T(8,128)S(1)} %get-tuple-element.48), channel_id=1, source_target_pairs={{0,8},{2,10},{4,12},{6,14},{8,0},{10,2},{12,4},{14,6},{16,24},{18,... | collective-permute-start | bytes 196616 | tf_op jit(solution)/shard_map/ppermute | solution.py:61
  35.1 6.0 %collective-permute-start.9 = (f32[2,64,128]{2,1,0:T(8,128)S(1)}, f32[2,64,128]{2,1,0:T(8,128)S(1)}, u32[]{:S(2)}, u32[]{:S(2)}) collective-permute-start(f32[2,64,128]{2,1,0:T(8,128)S(1)} %get-tuple-element.50), channel_id=1, source_target_pairs={{0,4},{2,6},{4,0},{6,2},{8,12},{10,14},{12,8},{14,10},{16,20},{18,... | collective-permute-start | bytes 196616 | tf_op jit(solution)/shard_map/ppermute | solution.py:61
  35.9 5.2 %collective-permute-start.7 = (f32[2,64,128]{2,1,0:T(8,128)S(1)}, f32[2,64,128]{2,1,0:T(8,128)S(1)}, u32[]{:S(2)}, u32[]{:S(2)}) collective-permute-start(f32[2,64,128]{2,1,0:T(8,128)S(1)} %get-tuple-element.52), channel_id=1, source_target_pairs={{0,8},{2,10},{4,12},{6,14},{8,0},{10,2},{12,4},{14,6},{16,24},{18,... | collective-permute-start | bytes 196616 | tf_op jit(solution)/shard_map/ppermute | solution.py:61
  38.5 5.2 %collective-permute-start.15 = (f32[1,128,128]{2,1,0:T(8,128)S(1)}, f32[1,128,128]{2,1,0:T(8,128)S(1)}, u32[]{:S(2)}, u32[]{:S(2)}) collective-permute-start(f32[1,128,128]{2,1,0:T(8,128)S(1)} %get-tuple-element.43), channel_id=1, source_target_pairs={{0,16},{2,18},{4,20},{6,22},{8,24},{10,26},{12,28},{14,30},{16,0},... | collective-permute-start | bytes 196616 | tf_op jit(solution)/shard_map/ppermute | solution.py:61
  41.2 5.2 %collective-permute-start.10 = (f32[1,128,128]{2,1,0:T(8,128)S(1)}, f32[1,128,128]{2,1,0:T(8,128)S(1)}, u32[]{:S(2)}, u32[]{:S(2)}) collective-permute-start(f32[1,128,128]{2,1,0:T(8,128)S(1)} %get-tuple-element.37), channel_id=1, source_target_pairs={{0,16},{2,18},{4,20},{6,22},{8,24},{10,26},{12,28},{14,30},{16,0},... | collective-permute-start | bytes 196616 | tf_op jit(solution)/shard_map/ppermute | solution.py:61

commit v8 on v7

--- a/solution.py
+++ b/solution.py
@@ -172,31 +172,41 @@
             return ref[part, z, k + 1]
         return jnp.where(bottom, pltpu.roll(ref[part, z, 0], SUB - 1, 0), 0.0)
 
-    def x_prev(ref, part, z, k):
-        if k > 0:
-            return ref[part, z, k - 1]
-        return jnp.where(top, pltpu.roll(ref[part, z, PACKED - 1], 1, 0), 0.0)
-
-    def sweep(state):
+    def sweep(state, start):
+        above = None
         for z in range(LZ):
+            curls = []
             for k in range(PACKED):
-                east, north, vert = state[0, z, k], state[1, z, k], state[2, z, k]
-                east_d = state[0, z + 1, k] if z + 1 < LZ else zero
-                north_d = state[1, z + 1, k] if z + 1 < LZ else zero
-                curl[0, z, k] = (y_next(vert) - vert) - (north_d - north)
-                curl[1, z, k] = (east_d - east) - (x_next(state, 2, z, k) - vert)
-                curl[2, z, k] = (x_next(state, 1, z, k) - north) - (y_next(east) - east)
+                east, north, vert = start[0, z, k], start[1, z, k], start[2, z, k]
+                east_d = start[0, z + 1, k] if z + 1 < LZ else zero
+                north_d = start[1, z + 1, k] if z + 1 < LZ else zero
+                curls.append((
+                    (y_next(vert) - vert) - (north_d - north),
+                    (east_d - east) - (x_next(start, 2, z, k) - vert),
+                    (x_next(start, 1, z, k) - north) - (y_next(east) - east),
+                ))
             for k in range(PACKED):
-                curl_x, curl_y, curl_z = curl[0, z, k], curl[1, z, k], curl[2, z, k]
-                up_x = curl[0, z - 1, k] if z else zero
-                up_y = curl[1, z - 1, k] if z else zero
+                curl_x, curl_y, curl_z = curls[k]
+                up_x, up_y = above[k][:2] if z else (zero, zero)
+                if k:
+                    before_y, before_z = curls[k - 1][1:]
+                else:
+                    before_y, before_z = (jnp.where(top, pltpu.roll(c, 1, 0), 0.0) for c in curls[-1][1:])
                 back_x = (up_y - curl_y) - (y_prev(curl_z) - curl_z)
-                back_y = (x_prev(curl, 2, z, k) - curl_z) - (up_x - curl_x)
-                back_z = (y_prev(curl_x) - curl_x) - (x_prev(curl, 1, z, k) - curl_y)
+                back_y = (before_z - curl_z) - (up_x - curl_x)
+                back_z = (y_prev(curl_x) - curl_x) - (before_y - curl_y)
                 s, d = scale[z, k], decay[z, k]
-                state[0, z, k] = d * state[0, z, k] + (right[0, z, k] - s * back_x)
-                state[1, z, k] = d * state[1, z, k] + (right[1, z, k] - s * back_y)
-                state[2, z, k] = d * state[2, z, k] + (right[2, z, k] - s * back_z)
+                state[0, z, k] = d * start[0, z, k] + (right[0, z, k] - s * back_x)
+                state[1, z, k] = d * start[1, z, k] + (right[1, z, k] - s * back_y)
+                state[2, z, k] = d * start[2, z, k] + (right[2, z, k] - s * back_z)
+            above = curls
+
+    def relax(state, steps):
+        sweep(state, right)
+
+        @pl.loop(0, steps - 2)
+        def _(step):
+            sweep(state, state)
 
     count = starts_ref.shape[0]
     sent_at, given_at = [], []
@@ -233,22 +243,16 @@
                 for part in range(3):
                     value = s * source_ref[part, z, k]
                     right[part, z, k] = value
-                    field[part, z, k] = value
-
-    @pl.loop(0, STEPS_FWD - 1)
-    def _(step):
-        sweep(field)
+
+    relax(field, STEPS_FWD)
 
     for z in range(LZ):
         for k in range(PACKED):
             for part in range(3):
                 value = scale[z, k] * (field[part, z, k] - observed_ref[part, z, k])
                 right[part, z, k] = value
-                adjoint[part, z, k] = value
-
-    @pl.loop(0, STEPS_ADJ - 1)
-    def _(step):
-        sweep(adjoint)
+
+    relax(adjoint, STEPS_ADJ)
 
     for z in range(LZ):
 
@@ -340,6 +344,19 @@
         functools.partial(first_body, groups, len(groups_of)), out,
         [SMEM, VMEM] * len(groups_of) + [VMEM], out.size, 8 * out.size,
     )(*flat, block)
+
+
+def more_body(groups, share, index_ref, terms_ref, given_total, total, padded):
+    add_terms(index_ref, terms_ref, total, share, groups // 2, padded)
+
+
+def more_sums(index, terms, total, rows):
+    groups = lax.axis_size("grp")
+    return call(
+        functools.partial(more_body, groups, rows // groups), floats(*total.shape),
+        [SMEM, VMEM, VMEM], total.size, 8 * total.size, input_output_aliases={2: 0},
+        scratch_shapes=[padded_rows(terms.shape[0] + TILE)],
+    )(index, terms, total)
 
 
 PIECES = 4
@@ -450,7 +467,9 @@
         others = across(given)
         kept_beside = beside(kept)
         total = first_sums([(offsets, kept), (told[:held], kept_beside)], block)
-        final = [(asked, others), (told[held:], beside(others))]
+        others_beside = beside(others)
+        total = more_sums(asked, others, total, rows)
+        final = [(told[held:], others_beside)]
     else:
         capacity = max(4, 2 * tiles // owners_count)
         places = place_slots(owner_ids.reshape(tiles), owners_count, capacity)

time: 47.2 us -> 47.6 us (level)
    pallas_call x0 -> x1, Pallas kernels: none -> 0.68 us  [more_sums(): call(functools.partial(more_body, groups, rows // groups), floats(*total....]
  transfers between devices with their start and end apart: 16 -> 16, of which waited for: 9 -> 9; matrix products, arithmetic and copies ran while one was open for 0% -> 0% of each run, Pallas kernels for 4% -> 6%
where the time goes in v8:
time: 47.6 us; the launch traced here: 47.5 us
  starting transfers between devices  20.5 us (43%)
  waiting for transfers between devices  15.1 us (32%)
  Pallas kernels  9.25 us (19%)
  local copies, waits for them, and re-layouts  1.63 us (3%)
  other arithmetic  0.79 us (2%)
    ppermute x16, starting transfers between devices, swap_over(): return lambda value: lax.ppermute(value, axis, ring)  20.5 us
    ppermute x16, waiting for transfers between devices, swap_over(): return lambda value: lax.ppermute(value, axis, ring)  15.1 us
    pallas_call x1, Pallas kernels, soundings_partial(): call(functools.partial(fields_body, packed), (floats(tiles * TILE, LANES)...  4.55 us
    unnamed x12, local copies, waits for them, and re-layouts  1.62 us
  transfers between devices with their start and end apart: 16, of which 9 were waited for; matrix products, arithmetic and copies ran while one was open for 0% of the time, Pallas kernels for 6%

profile of v8, /device:TPU:0, one launch (start us, length us, event | category | flops | bytes accessed | tf_op | source)
XLA Modules:
  0.0 47.5 jit_solution(14981464283871985505)
XLA Ops:
  0.0 0.7 %pad_add_fusion.1 = s32[4,8]{1,0:T(4,128)S(1)} fusion(s32[2,8]{1,0:T(2,128)} %lengths_ref.1, s32[2,8]{1,0:T(2,128)} %refs_0_.1), kind=kLoop, calls=%fused_computation.9 | loop fusion | flops 32 | bytes 256 | tf_op jit(solution)/shard_map/concatenate | solution.py:457
  0.7 3.0 %collective-permute-start = (s32[4,8]{1,0:T(4,128)S(1)}, s32[4,8]{1,0:T(4,128)S(1)}, u32[]{:S(2)}, u32[]{:S(2)}) collective-permute-start(s32[4,8]{1,0:T(4,128)S(1)} %pad_add_fusion.1), channel_id=1, source_target_pairs={{0,1},{1,0},{2,3},{3,2},{4,5},{5,4},{6,7},{7,6},{8,9},{9,8},{10,11... | collective-permute-start | bytes 392 | tf_op jit(solution)/shard_map/ppermute | solution.py:61
  3.7 1.6 %copy-done = f32[4096,1,128]{2,1,0:T(1,128)S(1)} copy-done((f32[4096,1,128]{2,1,0:T(1,128)S(1)}, f32[4096,1,128]{2,1,0:T(1,128)}, u32[]{:S(2)}) %copy-start) | copy-done | bytes 2097176
  5.3 0.1 shard_map.64.block_ref.table_ref.refs_4_
  5.4 0.0 copy-start.3
  5.4 0.0 copy-start.1
  5.4 0.0 copy-start.2
  5.5 0.0 collective-permute-done.index_ref
  5.5 0.6 %shard_map.65 = f32[384,128]{1,0:T(8,128)S(1)} custom-call(s32[4,8]{1,0:T(4,128)S(1)} %collective-permute-done.index_ref, f32[4096,128]{1,0:T(8,128)S(1)} %shard_map.64.block_ref.table_ref.refs_4_), custom_call_target="tpu_custom_call" | custom-call | bytes 393216 | tf_op jit(solution)/shard_map/pallas_call | solution.py:106
  6.1 0.0 copy-start.4
  6.1 0.0 copy-start.5
  6.1 1.9 %collective-permute-start.1 = (f32[384,128]{1,0:T(8,128)S(1)}, f32[384,128]{1,0:T(8,128)S(1)}, u32[]{:S(2)}, u32[]{:S(2)}) collective-permute-start(f32[384,128]{1,0:T(8,128)S(1)} %shard_map.65), channel_id=1, source_target_pairs={{0,1},{1,0},{2,3},{3,2},{4,5},{5,4},{6,7},{7,6},{8,9},{9,8},{10,11... | collective-permute-start | bytes 589832 | tf_op jit(solution)/shard_map/ppermute | solution.py:61
  8.0 0.1 collective-permute-start.2
  8.1 0.9 %shard_map.66 = (f32[3,8,8,8,128]{4,3,2,1,0:T(8,128)S(1)}, f32[3,8,8,8,128]{4,3,2,1,0:T(8,128)S(1)}) custom-call(f32[1536,128]{1,0:T(8,128)S(1)} %bitcast.17, f32[1536,128]{1,0:T(8,128)S(1)} %bitcast.18), custom_call_target="tpu_custom_call" | custom-call | flops 1572864 | bytes 3145728 | tf_op jit(solution)/shard_map/pallas_call | solution.py:146
  9.0 0.2 collective-permute-done.2
  9.2 3.3 %collective-permute-done.1.answer_ref = f32[384,128]{1,0:T(8,128)S(1)} collective-permute-done((f32[384,128]{1,0:T(8,128)S(1)}, f32[384,128]{1,0:T(8,128)S(1)}, u32[]{:S(2)}, u32[]{:S(2)}) %collective-permute-start.1) | collective-permute-done | bytes 196640 | tf_op jit(solution)/shard_map/ppermute | solution.py:61
  12.5 0.0 copy-done.4
  12.5 4.6 %shard_map.67 = (f32[512,128]{1,0:T(8,128)S(1)}, f32[384,128]{1,0:T(8,128)S(1)}) custom-call(s32[2,8]{1,0:T(2,128)S(1)} %copy-done.3, s32[2,8]{1,0:T(2,128)S(1)} %bitcast.21, s32[2,8]{1,0:T(2,128)S(1)} %copy-done.4, f32[4096,128]{1,0:T(8,128)S(1)} %shard_map.64.block_ref.table_ref.refs_4_, f32[384,128]{1,0:T(8,128)S(1)} %collective-permute-done.1.answer_ref, ...), custom_call_target="tpu_custom_call" | custom-call | flops 32768000 | bytes 2621440 | tf_op jit(solution)/shard_map/pallas_call | solution.py:283
  17.1 1.2 %collective-permute-start.3 = (f32[384,128]{1,0:T(8,128)S(1)}, f32[384,128]{1,0:T(8,128)S(1)}, u32[]{:S(2)}, u32[]{:S(2)}) collective-permute-start(f32[384,128]{1,0:T(8,128)S(1)} %get-tuple-element.31), channel_id=1, source_target_pairs={{0,1},{1,0},{2,3},{3,2},{4,5},{5,4},{6,7},{7,6},{8,9},{9,8},{10,11... | collective-permute-start | bytes 589832 | tf_op jit(solution)/shard_map/ppermute | solution.py:61
  18.3 0.0 collective-permute-start.5
  18.3 4.6 %collective-permute-done.3.terms_ref = f32[384,128]{1,0:T(8,128)S(1)} collective-permute-done((f32[384,128]{1,0:T(8,128)S(1)}, f32[384,128]{1,0:T(8,128)S(1)}, u32[]{:S(2)}, u32[]{:S(2)}) %collective-permute-start.3) | collective-permute-done | bytes 196640 | tf_op jit(solution)/shard_map/ppermute | solution.py:61
  22.8 0.0 collective-permute-start.4
  22.8 0.0 collective-permute-done.5.refs_3_
  22.8 0.9 %shard_map.68.given_total = f32[2592,128]{1,0:T(8,128)S(1)} custom-call(s32[2,8]{1,0:T(2,128)S(1)} %copy-done.3, f32[16,32,128]{2,1,0:T(8,128)S(1)} %bitcast.20, s32[2,8]{1,0:T(2,128)S(1)} %slice.55.refs_2_, f32[16,32,128]{2,1,0:T(8,128)S(1)} %collective-permute-done.5.refs_3_, f32[4096,128]{1,0:T(8,128)S(1)} %shard_map.64.block_ref.table_ref.refs_4_), custom_call_target="tpu_custom_call" | custom-call | flops 331776 | bytes 2654208 | tf_op jit(solution)/shard_map/pallas_call | solution.py:343
  23.7 0.7 %shard_map.69.refs_2_ = f32[2592,128]{1,0:T(8,128)S(1)} custom-call(s32[4,8]{1,0:T(4,128)S(1)} %collective-permute-done.index_ref, f32[384,128]{1,0:T(8,128)S(1)} %collective-permute-done.3.terms_ref, f32[2592,128]{1,0:T(8,128)S(1)} %shard_map.68.given_total), custom_call_target="tpu_custom_call", output_to_operand_aliasing={{}: (2, {})} | custom-call | flops 331776 | bytes 2654208 | tf_op jit(solution)/shard_map/pallas_call | solution.py:355
  24.4 0.0 collective-permute-done.4.refs_1_
  24.4 0.7 %shard_map.70 = (f32[2592,128]{1,0:T(8,128)S(1)}, f32[4,64,128]{2,1,0:T(8,128)S(1)}, f32[4,64,128]{2,1,0:T(8,128)S(1)}, f32[4,64,128]{2,1,0:T(8,128)S(1)}, f32[4...) custom-call(s32[4,8]{1,0:T(4,128)S(1)} %slice.54.refs_0_, ...), custom_call_target="tpu_custom_call", output_to_operand_aliasing={{0}: (2, {})} | custom-call | flops 331776 | bytes 2654208 | tf_op jit(solution)/shard_map/pallas_call | solution.py:384
  25.2 1.6 %collective-permute-start.13 = (f32[4,64,128]{2,1,0:T(8,128)S(1)}, f32[4,64,128]{2,1,0:T(8,128)S(1)}, u32[]{:S(2)}, u32[]{:S(2)}) collective-permute-start(f32[4,64,128]{2,1,0:T(8,128)S(1)} %get-tuple-element.41), channel_id=1, source_target_pairs={{0,8},{2,10},{4,12},{6,14},{8,0},{10,2},{12,4},{14,6},{16,24},{18,... | collective-permute-start | bytes 393224 | tf_op jit(solution)/shard_map/ppermute | solution.py:61
  26.8 1.5 %collective-permute-start.11 = (f32[4,64,128]{2,1,0:T(8,128)S(1)}, f32[4,64,128]{2,1,0:T(8,128)S(1)}, u32[]{:S(2)}, u32[]{:S(2)}) collective-permute-start(f32[4,64,128]{2,1,0:T(8,128)S(1)} %get-tuple-element.39), channel_id=1, source_target_pairs={{0,4},{2,6},{4,0},{6,2},{8,12},{10,14},{12,8},{14,10},{16,20},{18,... | collective-permute-start | bytes 393224 | tf_op jit(solution)/shard_map/ppermute | solution.py:61
  28.3 0.4 collective-permute-start.8
  28.8 0.5 %collective-permute-start.6 = (f32[4,64,128]{2,1,0:T(8,128)S(1)}, f32[4,64,128]{2,1,0:T(8,128)S(1)}, u32[]{:S(2)}, u32[]{:S(2)}) collective-permute-start(f32[4,64,128]{2,1,0:T(8,128)S(1)} %get-tuple-element.33), channel_id=1, source_target_pairs={{0,4},{2,6},{4,0},{6,2},{8,12},{10,14},{12,8},{14,10},{16,20},{18,... | collective-permute-start | bytes 393224 | tf_op jit(solution)/shard_map/ppermute | solution.py:61
  29.3 2.1 %collective-permute-done.13 = f32[4,64,128]{2,1,0:T(8,128)S(1)} collective-permute-done((f32[4,64,128]{2,1,0:T(8,128)S(1)}, f32[4,64,128]{2,1,0:T(8,128)S(1)}, u32[]{:S(2)}, u32[]{:S(2)}) %collective-permute-start.13) | collective-permute-done | bytes 131104 | tf_op jit(solution)/shard_map/ppermute | solution.py:61
  31.4 1.8 %collective-permute-start.14 = (f32[2,64,128]{2,1,0:T(8,128)S(1)}, f32[2,64,128]{2,1,0:T(8,128)S(1)}, u32[]{:S(2)}, u32[]{:S(2)}) collective-permute-start(f32[2,64,128]{2,1,0:T(8,128)S(1)} %get-tuple-element.46), channel_id=1, source_target_pairs={{0,4},{2,6},{4,0},{6,2},{8,12},{10,14},{12,8},{14,10},{16,20},{18,... | collective-permute-start | bytes 196616 | tf_op jit(solution)/shard_map/ppermute | solution.py:61
  33.2 0.0 collective-permute-done.11
  33.2 1.6 %collective-permute-start.12 = (f32[2,64,128]{2,1,0:T(8,128)S(1)}, f32[2,64,128]{2,1,0:T(8,128)S(1)}, u32[]{:S(2)}, u32[]{:S(2)}) collective-permute-start(f32[2,64,128]{2,1,0:T(8,128)S(1)} %get-tuple-element.48), channel_id=1, source_target_pairs={{0,8},{2,10},{4,12},{6,14},{8,0},{10,2},{12,4},{14,6},{16,24},{18,... | collective-permute-start | bytes 196616 | tf_op jit(solution)/shard_map/ppermute | solution.py:61
  34.9 0.0 collective-permute-done.8
  34.9 0.6 %collective-permute-start.9 = (f32[2,64,128]{2,1,0:T(8,128)S(1)}, f32[2,64,128]{2,1,0:T(8,128)S(1)}, u32[]{:S(2)}, u32[]{:S(2)}) collective-permute-start(f32[2,64,128]{2,1,0:T(8,128)S(1)} %get-tuple-element.50), channel_id=1, source_target_pairs={{0,4},{2,6},{4,0},{6,2},{8,12},{10,14},{12,8},{14,10},{16,20},{18,... | collective-permute-start | bytes 196616 | tf_op jit(solution)/shard_map/ppermute | solution.py:61
  35.6 0.4 collective-permute-done.6
  36.0 1.4 %collective-permute-start.7 = (f32[2,64,128]{2,1,0:T(8,128)S(1)}, f32[2,64,128]{2,1,0:T(8,128)S(1)}, u32[]{:S(2)}, u32[]{:S(2)}) collective-permute-start(f32[2,64,128]{2,1,0:T(8,128)S(1)} %get-tuple-element.52), channel_id=1, source_target_pairs={{0,8},{2,10},{4,12},{6,14},{8,0},{10,2},{12,4},{14,6},{16,24},{18,... | collective-permute-start | bytes 196616 | tf_op jit(solution)/shard_map/ppermute | solution.py:61
  37.4 0.0 collective-permute-done.14.got_high
  37.4 0.2 collective-permute-done.12.got_low
  37.6 2.7 %collective-permute-start.15 = (f32[1,128,128]{2,1,0:T(8,128)S(1)}, f32[1,128,128]{2,1,0:T(8,128)S(1)}, u32[]{:S(2)}, u32[]{:S(2)}) collective-permute-start(f32[1,128,128]{2,1,0:T(8,128)S(1)} %get-tuple-element.43), channel_id=1, source_target_pairs={{0,16},{2,18},{4,20},{6,22},{8,24},{10,26},{12,28},{14,30},{16,0},... | collective-permute-start | bytes 196616 | tf_op jit(solution)/shard_map/ppermute | solution.py:61
  40.2 0.0 collective-permute-done.9.got_high
  40.3 0.6 %collective-permute-done.7.got_low = f32[2,64,128]{2,1,0:T(8,128)S(1)} collective-permute-done((f32[2,64,128]{2,1,0:T(8,128)S(1)}, f32[2,64,128]{2,1,0:T(8,128)S(1)}, u32[]{:S(2)}, u32[]{:S(2)}) %collective-permute-start.7) | collective-permute-done | bytes 65568 | tf_op jit(solution)/shard_map/ppermute | solution.py:61
  40.9 2.1 %collective-permute-start.10 = (f32[1,128,128]{2,1,0:T(8,128)S(1)}, f32[1,128,128]{2,1,0:T(8,128)S(1)}, u32[]{:S(2)}, u32[]{:S(2)}) collective-permute-start(f32[1,128,128]{2,1,0:T(8,128)S(1)} %get-tuple-element.37), channel_id=1, source_target_pairs={{0,16},{2,18},{4,20},{6,22},{8,24},{10,26},{12,28},{14,30},{16,0},... | collective-permute-start | bytes 196616 | tf_op jit(solution)/shard_map/ppermute | solution.py:61
  43.0 1.8 %collective-permute-done.15.refs_2_ = f32[1,128,128]{2,1,0:T(8,128)S(1)} collective-permute-done((f32[1,128,128]{2,1,0:T(8,128)S(1)}, f32[1,128,128]{2,1,0:T(8,128)S(1)}, u32[]{:S(2)}, u32[]{:S(2)}) %collective-permute-start.15) | collective-permute-done | bytes 65568 | tf_op jit(solution)/shard_map/ppermute | solution.py:61
  44.8 2.0 %collective-permute-done.10.refs_0_ = f32[1,128,128]{2,1,0:T(8,128)S(1)} collective-permute-done((f32[1,128,128]{2,1,0:T(8,128)S(1)}, f32[1,128,128]{2,1,0:T(8,128)S(1)}, u32[]{:S(2)}, u32[]{:S(2)}) %collective-permute-start.10) | collective-permute-done | bytes 65568 | tf_op jit(solution)/shard_map/ppermute | solution.py:61
  46.8 0.7 %shard_map.73 = f32[256,128]{1,0:T(8,128)} custom-call(f32[1,128,128]{2,1,0:T(8,128)S(1)} %collective-permute-done.10.refs_0_, f32[1,128,128]{2,1,0:T(8,128)S(1)} %get-tuple-element.38.refs_1_, f32[1,128,128]{2,1,0:T(8,128)S(1)} %collective-permute-done.15.refs_2_, f32[1,128,128]{2,1,0:T(8,128)S(1)} %get-tuple-element.44.refs_3_), custom_call_target="tpu_custom_call" | custom-call | flops 32768 | bytes 393216 | tf_op jit(solution)/shard_map/pallas_call | solution.py:434
  (14 shorter events, 0.1 us)
Async XLA Ops:
  0.7 4.8 %collective-permute-start = (s32[4,8]{1,0:T(4,128)S(1)}, s32[4,8]{1,0:T(4,128)S(1)}, u32[]{:S(2)}, u32[]{:S(2)}) collective-permute-start(s32[4,8]{1,0:T(4,128)S(1)} %pad_add_fusion.1), channel_id=1, source_target_pairs={{0,1},{1,0},{2,3},{3,2},{4,5},{5,4},{6,7},{7,6},{8,9},{9,8},{10,11... | collective-permute-start | bytes 392 | tf_op jit(solution)/shard_map/ppermute | solution.py:61
  3.7 1.6 %copy-start = (f32[4096,1,128]{2,1,0:T(1,128)S(1)}, f32[4096,1,128]{2,1,0:T(1,128)}, u32[]{:S(2)}) copy-start(f32[4096,1,128]{2,1,0:T(1,128)} %param.6) | copy-start | bytes 6291460
  5.4 2.5 %copy-start.3 = (s32[2,8]{1,0:T(2,128)S(1)}, s32[2,8]{1,0:T(2,128)}, u32[]{:S(2)}) copy-start(s32[2,8]{1,0:T(2,128)} %refs_0_.1) | copy-start | bytes 196
  5.4 2.6 %copy-start.1 = (f32[2,3,8,4096]{3,2,1,0:T(8,128)S(1)}, f32[2,3,8,4096]{3,2,1,0:T(8,128)}, u32[]{:S(2)}) copy-start(f32[2,3,8,4096]{3,2,1,0:T(8,128)} %param.7) | copy-start | bytes 2359300
  5.4 2.6 %copy-start.2 = (f32[2,3,8,4096]{3,2,1,0:T(8,128)S(1)}, f32[2,3,8,4096]{3,2,1,0:T(8,128)}, u32[]{:S(2)}) copy-start(f32[2,3,8,4096]{3,2,1,0:T(8,128)} %param.8) | copy-start | bytes 2359300
  6.1 6.5 %copy-start.4 = (s32[2,8]{1,0:T(2,128)S(1)}, s32[2,8]{1,0:T(2,128)}, u32[]{:S(2)}) copy-start(s32[2,8]{1,0:T(2,128)} %lengths_ref.1) | copy-start | bytes 196
  6.1 6.4 %copy-start.5 = (s32[2,8,1]{1,2,0:T(1,128)S(1)}, s32[2,8,1]{1,2,0:T(1,128)}, u32[]{:S(2)}) copy-start(s32[2,8,1]{1,2,0:T(1,128)} %param.9) | copy-start | bytes 196
  6.1 6.4 %collective-permute-start.1 = (f32[384,128]{1,0:T(8,128)S(1)}, f32[384,128]{1,0:T(8,128)S(1)}, u32[]{:S(2)}, u32[]{:S(2)}) collective-permute-start(f32[384,128]{1,0:T(8,128)S(1)} %shard_map.65), channel_id=1, source_target_pairs={{0,1},{1,0},{2,3},{3,2},{4,5},{5,4},{6,7},{7,6},{8,9},{9,8},{10,11... | collective-permute-start | bytes 589832 | tf_op jit(solution)/shard_map/ppermute | solution.py:61
  8.0 1.2 %collective-permute-start.2 = (s32[6,8]{1,0:T(8,128)S(1)}, s32[6,8]{1,0:T(8,128)S(1)}, u32[]{:S(2)}, u32[]{:S(2)}) collective-permute-start(s32[6,8]{1,0:T(8,128)S(1)} %pad_add_fusion), channel_id=1, source_target_pairs={{0,2},{2,0},{4,6},{6,4},{8,10},{10,8},{12,14},{14,12},{16,18},{18,... | collective-permute-start | bytes 584 | tf_op jit(solution)/shard_map/ppermute | solution.py:61
  17.1 5.7 %collective-permute-start.3 = (f32[384,128]{1,0:T(8,128)S(1)}, f32[384,128]{1,0:T(8,128)S(1)}, u32[]{:S(2)}, u32[]{:S(2)}) collective-permute-start(f32[384,128]{1,0:T(8,128)S(1)} %get-tuple-element.31), channel_id=1, source_target_pairs={{0,1},{1,0},{2,3},{3,2},{4,5},{5,4},{6,7},{7,6},{8,9},{9,8},{10,11... | collective-permute-start | bytes 589832 | tf_op jit(solution)/shard_map/ppermute | solution.py:61
  18.3 4.6 %collective-permute-start.5 = (f32[16,32,128]{2,1,0:T(8,128)S(1)}, f32[16,32,128]{2,1,0:T(8,128)S(1)}, u32[]{:S(2)}, u32[]{:S(2)}) collective-permute-start(f32[16,32,128]{2,1,0:T(8,128)S(1)} %bitcast.19), channel_id=1, source_target_pairs={{0,2},{2,0},{4,6},{6,4},{8,10},{10,8},{12,14},{14,12},{16,18},{18,... | collective-permute-start | bytes 786440 | tf_op jit(solution)/shard_map/ppermute | solution.py:61
  22.8 1.6 %collective-permute-start.4 = (f32[384,128]{1,0:T(8,128)S(1)}, f32[384,128]{1,0:T(8,128)S(1)}, u32[]{:S(2)}, u32[]{:S(2)}) collective-permute-start(f32[384,128]{1,0:T(8,128)S(1)} %collective-permute-done.3.terms_ref), channel_id=1, source_target_pairs={{0,2},{2,0},{4,6},{6,4},{8,10},{10,8},{12,14},{14,12},{16,18},{18,... | collective-permute-start | bytes 589832 | tf_op jit(solution)/shard_map/ppermute | solution.py:61
  25.2 6.2 %collective-permute-start.13 = (f32[4,64,128]{2,1,0:T(8,128)S(1)}, f32[4,64,128]{2,1,0:T(8,128)S(1)}, u32[]{:S(2)}, u32[]{:S(2)}) collective-permute-start(f32[4,64,128]{2,1,0:T(8,128)S(1)} %get-tuple-element.41), channel_id=1, source_target_pairs={{0,8},{2,10},{4,12},{6,14},{8,0},{10,2},{12,4},{14,6},{16,24},{18,... | collective-permute-start | bytes 393224 | tf_op jit(solution)/shard_map/ppermute | solution.py:61
  26.8 6.4 %collective-permute-start.11 = (f32[4,64,128]{2,1,0:T(8,128)S(1)}, f32[4,64,128]{2,1,0:T(8,128)S(1)}, u32[]{:S(2)}, u32[]{:S(2)}) collective-permute-start(f32[4,64,128]{2,1,0:T(8,128)S(1)} %get-tuple-element.39), channel_id=1, source_target_pairs={{0,4},{2,6},{4,0},{6,2},{8,12},{10,14},{12,8},{14,10},{16,20},{18,... | collective-permute-start | bytes 393224 | tf_op jit(solution)/shard_map/ppermute | solution.py:61
  28.3 6.6 %collective-permute-start.8 = (f32[4,64,128]{2,1,0:T(8,128)S(1)}, f32[4,64,128]{2,1,0:T(8,128)S(1)}, u32[]{:S(2)}, u32[]{:S(2)}) collective-permute-start(f32[4,64,128]{2,1,0:T(8,128)S(1)} %get-tuple-element.35), channel_id=1, source_target_pairs={{0,8},{2,10},{4,12},{6,14},{8,0},{10,2},{12,4},{14,6},{16,24},{18,... | collective-permute-start | bytes 393224 | tf_op jit(solution)/shard_map/ppermute | solution.py:61
  28.8 7.2 %collective-permute-start.6 = (f32[4,64,128]{2,1,0:T(8,128)S(1)}, f32[4,64,128]{2,1,0:T(8,128)S(1)}, u32[]{:S(2)}, u32[]{:S(2)}) collective-permute-start(f32[4,64,128]{2,1,0:T(8,128)S(1)} %get-tuple-element.33), channel_id=1, source_target_pairs={{0,4},{2,6},{4,0},{6,2},{8,12},{10,14},{12,8},{14,10},{16,20},{18,... | collective-permute-start | bytes 393224 | tf_op jit(solution)/shard_map/ppermute | solution.py:61
  31.4 6.0 %collective-permute-start.14 = (f32[2,64,128]{2,1,0:T(8,128)S(1)}, f32[2,64,128]{2,1,0:T(8,128)S(1)}, u32[]{:S(2)}, u32[]{:S(2)}) collective-permute-start(f32[2,64,128]{2,1,0:T(8,128)S(1)} %get-tuple-element.46), channel_id=1, source_target_pairs={{0,4},{2,6},{4,0},{6,2},{8,12},{10,14},{12,8},{14,10},{16,20},{18,... | collective-permute-start | bytes 196616 | tf_op jit(solution)/shard_map/ppermute | solution.py:61
  33.2 4.3 %collective-permute-start.12 = (f32[2,64,128]{2,1,0:T(8,128)S(1)}, f32[2,64,128]{2,1,0:T(8,128)S(1)}, u32[]{:S(2)}, u32[]{:S(2)}) collective-permute-start(f32[2,64,128]{2,1,0:T(8,128)S(1)} %get-tuple-element.48), channel_id=1, source_target_pairs={{0,8},{2,10},{4,12},{6,14},{8,0},{10,2},{12,4},{14,6},{16,24},{18,... | collective-permute-start | bytes 196616 | tf_op jit(solution)/shard_map/ppermute | solution.py:61
  34.9 5.3 %collective-permute-start.9 = (f32[2,64,128]{2,1,0:T(8,128)S(1)}, f32[2,64,128]{2,1,0:T(8,128)S(1)}, u32[]{:S(2)}, u32[]{:S(2)}) collective-permute-start(f32[2,64,128]{2,1,0:T(8,128)S(1)} %get-tuple-element.50), channel_id=1, source_target_pairs={{0,4},{2,6},{4,0},{6,2},{8,12},{10,14},{12,8},{14,10},{16,20},{18,... | collective-permute-start | bytes 196616 | tf_op jit(solution)/shard_map/ppermute | solution.py:61
  36.0 4.9 %collective-permute-start.7 = (f32[2,64,128]{2,1,0:T(8,128)S(1)}, f32[2,64,128]{2,1,0:T(8,128)S(1)}, u32[]{:S(2)}, u32[]{:S(2)}) collective-permute-start(f32[2,64,128]{2,1,0:T(8,128)S(1)} %get-tuple-element.52), channel_id=1, source_target_pairs={{0,8},{2,10},{4,12},{6,14},{8,0},{10,2},{12,4},{14,6},{16,24},{18,... | collective-permute-start | bytes 196616 | tf_op jit(solution)/shard_map/ppermute | solution.py:61
  37.6 7.2 %collective-permute-start.15 = (f32[1,128,128]{2,1,0:T(8,128)S(1)}, f32[1,128,128]{2,1,0:T(8,128)S(1)}, u32[]{:S(2)}, u32[]{:S(2)}) collective-permute-start(f32[1,128,128]{2,1,0:T(8,128)S(1)} %get-tuple-element.43), channel_id=1, source_target_pairs={{0,16},{2,18},{4,20},{6,22},{8,24},{10,26},{12,28},{14,30},{16,0},... | collective-permute-start | bytes 196616 | tf_op jit(solution)/shard_map/ppermute | solution.py:61
  40.9 5.9 %collective-permute-start.10 = (f32[1,128,128]{2,1,0:T(8,128)S(1)}, f32[1,128,128]{2,1,0:T(8,128)S(1)}, u32[]{:S(2)}, u32[]{:S(2)}) collective-permute-start(f32[1,128,128]{2,1,0:T(8,128)S(1)} %get-tuple-element.37), channel_id=1, source_target_pairs={{0,16},{2,18},{4,20},{6,22},{8,24},{10,26},{12,28},{14,30},{16,0},... | collective-permute-start | bytes 196616 | tf_op jit(solution)/shard_map/ppermute | solution.py:61

commit v9 on v8

--- a/solution.py
+++ b/solution.py
@@ -297,6 +297,12 @@
     return [slot | (1 << order[0]) for slot in rest] + rest
 
 
+def slot_of(target, me):
+    far = (target >> 1) ^ (me >> 1)
+    flip = (far ^ (far >> 1)) & (me & 1)
+    return far ^ (flip | (flip << 1))
+
+
 def add_terms(index_ref, terms_ref, total, share, slots, padded):
     me = lax.axis_index("grp")
     packed = len(terms_ref.shape) == 2
@@ -310,7 +316,7 @@
         first = lax.div(start, share)
         target = first + ((first ^ me) & 1)
         where = start - target * share
-        base = ((target >> 1) ^ (me >> 1)) * span + TILE + where
+        base = slot_of(target, me) * span + TILE + where
         base = jnp.where(where > -TILE, base, slots * span)
         if packed:
             place = tile // LZ * EARTH if tile % LZ == 0 else place + length
@@ -359,22 +365,22 @@
     )(index, terms, total)
 
 
-PIECES = 4
-
-
-def last_body(orders, groups, share, count, *refs):
+PIECES = 2
+
+
+def last_body(groups, share, count, *refs):
     total, outs, padded = refs[2 * count + 1], refs[2 * count + 2 : -1], refs[-1]
     span, slots, piece = share + 2 * TILE, groups // 2, share // PIECES
     for i in range(count):
         add_terms(*refs[2 * i : 2 * i + 2], total, share, slots, padded)
     for which in range(PIECES):
-        for place, slot in enumerate(arranged(orders[which % 2])):
+        for place, slot in enumerate(arranged(tuple(range(slots.bit_length() - 1)))):
             out = outs[2 * which + (place * 2 >= slots)]
             begin = slot * span + TILE + which * piece
             out[place % (slots // 2)] = total[begin : begin + piece, :]
 
 
-def last_sums(groups_of, total, rows, orders):
+def last_sums(groups_of, total, rows):
     groups = lax.axis_size("grp")
     share, slots = rows // groups, groups // 2
     out = floats(slots // 2, share // PIECES, LANES)
@@ -382,19 +388,12 @@
     count = len(groups_of)
     terms_rows = max(a.shape[0] for _, a in groups_of)
     outs = call(
-        functools.partial(last_body, orders, groups, share, count),
+        functools.partial(last_body, groups, share, count),
         (floats(*total.shape),) + (out,) * (2 * PIECES), [SMEM, VMEM] * count + [VMEM],
         total.size, 8 * total.size, input_output_aliases={2 * count: 0},
         scratch_shapes=[padded_rows(terms_rows + TILE)],
     )(*flat, total)[1:]
-    return [outs[4 * i : 4 * i + 4] for i in range(PIECES // 2)]
-
-
-def join_body(got_low, low, got_high, high, give_ref, keep_ref):
-    cut, split = low.shape[0] // 2, low.shape[1]
-    for got, held, rows in ((got_low, low, slice(0, split)), (got_high, high, slice(split, None))):
-        give_ref[:, rows] = got[:cut] + held[:cut]
-        keep_ref[:, rows] = got[cut:] + held[cut:]
+    return [outs[2 * i : 2 * i + 2] for i in range(PIECES)]
 
 
 def finish_body(*refs):
@@ -405,31 +404,20 @@
         out_ref[i // 2 * rows : (i // 2 + 1) * rows] = got[0] + held[0]
 
 
-def halve(stages, orders):
-    bit_pairs = list(zip(*orders))
-    state = list(stages)
-    for step, (low_bit, high_bit) in enumerate(bit_pairs[:2]):
-        for i, (low_give, low, high_give, high) in enumerate(state):
-            got_low = swap_over("grp", 2 << low_bit)(low_give)
-            got_high = swap_over("grp", 2 << high_bit)(high_give)
-            cut = low.shape[0] // 2
-            if step == 0:
-                low_give, low = got_low[:cut] + low[:cut], got_low[cut:] + low[cut:]
-                high_give, high = got_high[:cut] + high[:cut], got_high[cut:] + high[cut:]
-                state[i] = low_give, low, high_give, high
+def halve(stages):
+    groups = lax.axis_size("grp")
+    state, bits = list(stages), groups.bit_length() - 2
+    for step in range(bits):
+        other = 1 - step if step < 2 else step
+        ring = [(i, i ^ (2 << (other if i & 1 else step))) for i in range(groups)]
+        for i, (give, keep) in enumerate(state):
+            got = lax.ppermute(give, "grp", ring)
+            cut = keep.shape[0] // 2
+            if step + 1 < bits:
+                state[i] = got[:cut] + keep[:cut], got[cut:] + keep[cut:]
             else:
-                out = floats(cut, low.shape[1] + high.shape[1], LANES)
-                state[i] = call(
-                    join_body, (out, out), [VMEM] * 4, low.size, 24 * low.size
-                )(got_low, low, got_high, high)
-    last = []
-    for give, keep in state:
-        for bit, _ in bit_pairs[2:]:
-            got = swap_over("grp", 2 << bit)(give)
-            cut = keep.shape[0] // 2
-            if cut:
-                give, keep = got[:cut] + keep[:cut], got[cut:] + keep[cut:]
-        last += [got, keep]
+                state[i] = got, keep
+    last = [a for pair in state for a in pair]
     out = floats(sum(a.shape[1] for a in last) // 2, LANES)
     return call(finish_body, out, [VMEM] * len(last), out.size, 12 * out.size)(*last)
 
@@ -448,7 +436,7 @@
 
 
 def per_device(model, source, observed, owner_ids, offsets, lengths):
-    rows, owners_count, groups = model.shape[0], lax.axis_size("mdl"), lax.axis_size("grp")
+    rows, owners_count = model.shape[0], lax.axis_size("mdl")
     tiles = source.shape[0] * LZ
     across, beside = swap_over("mdl", 1), swap_over("grp", 1)
     block = hold(model.reshape(rows, LANES))
@@ -492,10 +480,7 @@
         total = first_sums([(asked, arrived)], block)
         final = [(beside(asked), beside(arrived))]
 
-    bits = tuple(range(groups.bit_length() - 2))
-    orders = (bits, bits[1:2] + bits[0:1] + bits[2:])
-    sums = halve(last_sums(final, total, rows, orders), orders)
-    return sums[:, None, :]
+    return halve(last_sums(final, total, rows))[:, None, :]
 
 
 def solution(mesh):

time: 47.6 us -> 46.9 us (0.985)
  starting transfers between devices: 20.5 us -> 16.7 us
  waiting for transfers between devices: 15.1 us -> 18.1 us
    ppermute x16 -> x6, starting transfers between devices: 20.5 us -> 6.06 us  [swap_over(): return lambda value: lax.ppermute(value, axis, ring)]
    ppermute x0 -> x6, starting transfers between devices: none -> 10.6 us  [halve(): got = lax.ppermute(give, 'grp', ring)]
    ppermute x0 -> x6, waiting for transfers between devices: none -> 9.97 us  [halve(): got = lax.ppermute(give, 'grp', ring)]
    ppermute x16 -> x6, waiting for transfers between devices: 15.1 us -> 8.1 us  [swap_over(): return lambda value: lax.ppermute(value, axis, ring)]
  transfers between devices with their start and end apart: 16 -> 12, of which waited for: 9 -> 8; matrix products, arithmetic and copies ran while one was open for 0% -> 0% of each run, Pallas kernels for 6% -> 6%
where the time goes in v9:
time: 46.9 us; the launch traced here: 46.7 us
  waiting for transfers between devices  18.1 us (39%)
  starting transfers between devices  16.7 us (36%)
  Pallas kernels  9.31 us (20%)
  local copies, waits for them, and re-layouts  1.63 us (3%)
  other arithmetic  0.84 us (2%)
    ppermute x6, starting transfers between devices, halve(): got = lax.ppermute(give, 'grp', ring)  10.6 us
    ppermute x6, waiting for transfers between devices, halve(): got = lax.ppermute(give, 'grp', ring)  9.97 us
    ppermute x6, waiting for transfers between devices, swap_over(): return lambda value: lax.ppermute(value, axis, ring)  8.1 us
    ppermute x6, starting transfers between devices, swap_over(): return lambda value: lax.ppermute(value, axis, ring)  6.06 us
    pallas_call x1, Pallas kernels, soundings_partial(): call(functools.partial(fields_body, packed), (floats(tiles * TILE, LANES)...  4.55 us
    unnamed x12, local copies, waits for them, and re-layouts  1.62 us
    pallas_call x1, Pallas kernels, prepare(): call(prepare_body, (out, out), [VMEM, VMEM], 8 * source.size, 16 * source...  0.94 us
  transfers between devices with their start and end apart: 12, of which 8 were waited for; matrix products, arithmetic and copies ran while one was open for 0% of the time, Pallas kernels for 6%

profile of v9, /device:TPU:0, one launch (start us, length us, event | category | flops | bytes accessed | tf_op | source)
XLA Modules:
  0.0 46.7 jit_solution(10388388014340871896)
XLA Ops:
  0.0 0.7 %pad_add_fusion.1 = s32[4,8]{1,0:T(4,128)S(1)} fusion(s32[2,8]{1,0:T(2,128)} %lengths_ref.1, s32[2,8]{1,0:T(2,128)} %refs_0_.1), kind=kLoop, calls=%fused_computation.9 | loop fusion | flops 32 | bytes 256 | tf_op jit(solution)/shard_map/concatenate | solution.py:445
  0.7 3.0 %collective-permute-start = (s32[4,8]{1,0:T(4,128)S(1)}, s32[4,8]{1,0:T(4,128)S(1)}, u32[]{:S(2)}, u32[]{:S(2)}) collective-permute-start(s32[4,8]{1,0:T(4,128)S(1)} %pad_add_fusion.1), channel_id=1, source_target_pairs={{0,1},{1,0},{2,3},{3,2},{4,5},{5,4},{6,7},{7,6},{8,9},{9,8},{10,11... | collective-permute-start | bytes 392 | tf_op jit(solution)/shard_map/ppermute | solution.py:61
  3.7 0.0 copy-start
  3.7 1.6 %copy-done = f32[4096,1,128]{2,1,0:T(1,128)S(1)} copy-done((f32[4096,1,128]{2,1,0:T(1,128)S(1)}, f32[4096,1,128]{2,1,0:T(1,128)}, u32[]{:S(2)}) %copy-start) | copy-done | bytes 2097176
  5.3 0.1 shard_map.64.block_ref.table_ref.refs_4_
  5.4 0.0 copy-start.3
  5.4 0.0 copy-start.1
  5.4 0.0 copy-start.2
  5.5 0.0 collective-permute-done.index_ref
  5.5 0.6 %shard_map.65 = f32[384,128]{1,0:T(8,128)S(1)} custom-call(s32[4,8]{1,0:T(4,128)S(1)} %collective-permute-done.index_ref, f32[4096,128]{1,0:T(8,128)S(1)} %shard_map.64.block_ref.table_ref.refs_4_), custom_call_target="tpu_custom_call" | custom-call | bytes 393216 | tf_op jit(solution)/shard_map/pallas_call | solution.py:106
  6.1 0.0 copy-start.4
  6.1 0.0 copy-start.5
  6.1 1.9 %collective-permute-start.1 = (f32[384,128]{1,0:T(8,128)S(1)}, f32[384,128]{1,0:T(8,128)S(1)}, u32[]{:S(2)}, u32[]{:S(2)}) collective-permute-start(f32[384,128]{1,0:T(8,128)S(1)} %shard_map.65), channel_id=1, source_target_pairs={{0,1},{1,0},{2,3},{3,2},{4,5},{5,4},{6,7},{7,6},{8,9},{9,8},{10,11... | collective-permute-start | bytes 589832 | tf_op jit(solution)/shard_map/ppermute | solution.py:61
  8.0 0.0 copy-done.3
  8.0 0.1 collective-permute-start.2
  8.0 0.0 copy-done.1
  8.1 0.0 copy-done.2
  8.1 0.9 %shard_map.66 = (f32[3,8,8,8,128]{4,3,2,1,0:T(8,128)S(1)}, f32[3,8,8,8,128]{4,3,2,1,0:T(8,128)S(1)}) custom-call(f32[1536,128]{1,0:T(8,128)S(1)} %bitcast.17, f32[1536,128]{1,0:T(8,128)S(1)} %bitcast.18), custom_call_target="tpu_custom_call" | custom-call | flops 1572864 | bytes 3145728 | tf_op jit(solution)/shard_map/pallas_call | solution.py:146
  9.0 0.2 collective-permute-done.2
  9.2 3.3 %collective-permute-done.1.answer_ref = f32[384,128]{1,0:T(8,128)S(1)} collective-permute-done((f32[384,128]{1,0:T(8,128)S(1)}, f32[384,128]{1,0:T(8,128)S(1)}, u32[]{:S(2)}, u32[]{:S(2)}) %collective-permute-start.1) | collective-permute-done | bytes 196640 | tf_op jit(solution)/shard_map/ppermute | solution.py:61
  12.5 0.0 copy-done.4
  12.5 0.0 copy-done.5
  12.5 4.6 %shard_map.67 = (f32[512,128]{1,0:T(8,128)S(1)}, f32[384,128]{1,0:T(8,128)S(1)}) custom-call(s32[2,8]{1,0:T(2,128)S(1)} %copy-done.3, s32[2,8]{1,0:T(2,128)S(1)} %bitcast.21, s32[2,8]{1,0:T(2,128)S(1)} %copy-done.4, f32[4096,128]{1,0:T(8,128)S(1)} %shard_map.64.block_ref.table_ref.refs_4_, f32[384,128]{1,0:T(8,128)S(1)} %collective-permute-done.1.answer_ref, ...), custom_call_target="tpu_custom_call" | custom-call | flops 32768000 | bytes 2621440 | tf_op jit(solution)/shard_map/pallas_call | solution.py:283
  17.1 1.2 %collective-permute-start.3 = (f32[384,128]{1,0:T(8,128)S(1)}, f32[384,128]{1,0:T(8,128)S(1)}, u32[]{:S(2)}, u32[]{:S(2)}) collective-permute-start(f32[384,128]{1,0:T(8,128)S(1)} %get-tuple-element.23), channel_id=1, source_target_pairs={{0,1},{1,0},{2,3},{3,2},{4,5},{5,4},{6,7},{7,6},{8,9},{9,8},{10,11... | collective-permute-start | bytes 589832 | tf_op jit(solution)/shard_map/ppermute | solution.py:61
  18.3 0.0 collective-permute-start.5
  18.3 4.6 %collective-permute-done.3.terms_ref = f32[384,128]{1,0:T(8,128)S(1)} collective-permute-done((f32[384,128]{1,0:T(8,128)S(1)}, f32[384,128]{1,0:T(8,128)S(1)}, u32[]{:S(2)}, u32[]{:S(2)}) %collective-permute-start.3) | collective-permute-done | bytes 196640 | tf_op jit(solution)/shard_map/ppermute | solution.py:61
  22.8 0.0 collective-permute-start.4
  22.8 0.0 collective-permute-done.5.refs_3_
  22.8 0.9 %shard_map.68.given_total = f32[2592,128]{1,0:T(8,128)S(1)} custom-call(s32[2,8]{1,0:T(2,128)S(1)} %copy-done.3, f32[16,32,128]{2,1,0:T(8,128)S(1)} %bitcast.20, s32[2,8]{1,0:T(2,128)S(1)} %slice.55.refs_2_, f32[16,32,128]{2,1,0:T(8,128)S(1)} %collective-permute-done.5.refs_3_, f32[4096,128]{1,0:T(8,128)S(1)} %shard_map.64.block_ref.table_ref.refs_4_), custom_call_target="tpu_custom_call" | custom-call | flops 331776 | bytes 2654208 | tf_op jit(solution)/shard_map/pallas_call | solution.py:349
  23.8 0.7 %shard_map.69.refs_2_ = f32[2592,128]{1,0:T(8,128)S(1)} custom-call(s32[4,8]{1,0:T(4,128)S(1)} %collective-permute-done.index_ref, f32[384,128]{1,0:T(8,128)S(1)} %collective-permute-done.3.terms_ref, f32[2592,128]{1,0:T(8,128)S(1)} %shard_map.68.given_total), custom_call_target="tpu_custom_call", output_to_operand_aliasing={{}: (2, {})} | custom-call | flops 331776 | bytes 2654208 | tf_op jit(solution)/shard_map/pallas_call | solution.py:361
  24.5 0.0 collective-permute-done.4.refs_1_
  24.5 0.8 %shard_map.70 = (f32[2592,128]{1,0:T(8,128)S(1)}, f32[4,128,128]{2,1,0:T(8,128)S(1)}, f32[4,128,128]{2,1,0:T(8,128)S(1)}, f32[4,128,128]{2,1,0:T(8,128)S(1)}, f32[4,128,128]{2,1,0:T(8,128)S(1)}) custom-call(s32[4,8]{1,0:T(4,128)S(1)} %slice.54.refs_0_, f32[384,128]{1,0:T(8,128)S(1)} %collective-permute-done.4.refs_1_, ...), custom_call_target="tpu_custom_call", output_to_operand_aliasing={{0}: (2, {})} | custom-call | flops 331776 | bytes 2654208 | tf_op jit(solution)/shard_map/pallas_call | solution.py:390
  25.3 1.6 %collective-permute-start.9 = (f32[4,128,128]{2,1,0:T(8,128)S(1)}, f32[4,128,128]{2,1,0:T(8,128)S(1)}, u32[]{:S(2)}, u32[]{:S(2)}) collective-permute-start(f32[4,128,128]{2,1,0:T(8,128)S(1)} %get-tuple-element.27), channel_id=1, source_target_pairs={{0,4},{2,10},{4,0},{6,14},{8,12},{10,2},{12,8},{14,6},{16,20},{18,... | collective-permute-start | bytes 786440 | tf_op jit(solution)/shard_map/ppermute | solution.py:414
  26.9 0.5 %collective-permute-start.6 = (f32[4,128,128]{2,1,0:T(8,128)S(1)}, f32[4,128,128]{2,1,0:T(8,128)S(1)}, u32[]{:S(2)}, u32[]{:S(2)}) collective-permute-start(f32[4,128,128]{2,1,0:T(8,128)S(1)} %get-tuple-element.25), channel_id=1, source_target_pairs={{0,4},{2,10},{4,0},{6,14},{8,12},{10,2},{12,8},{14,6},{16,20},{18,... | collective-permute-start | bytes 786440 | tf_op jit(solution)/shard_map/ppermute | solution.py:414
  27.4 4.3 %collective-permute-done.9 = f32[4,128,128]{2,1,0:T(8,128)S(1)} collective-permute-done((f32[4,128,128]{2,1,0:T(8,128)S(1)}, f32[4,128,128]{2,1,0:T(8,128)S(1)}, u32[]{:S(2)}, u32[]{:S(2)}) %collective-permute-start.9) | collective-permute-done | bytes 262176 | tf_op jit(solution)/shard_map/ppermute | solution.py:414
  31.8 1.6 %collective-permute-start.10 = (f32[2,128,128]{2,1,0:T(8,128)S(1)}, f32[2,128,128]{2,1,0:T(8,128)S(1)}, u32[]{:S(2)}, u32[]{:S(2)}) collective-permute-start(f32[2,128,128]{2,1,0:T(8,128)S(1)} %get-tuple-element.29), channel_id=1, source_target_pairs={{0,8},{2,6},{4,12},{6,2},{8,0},{10,14},{12,4},{14,10},{16,24},{18,... | collective-permute-start | bytes 393224 | tf_op jit(solution)/shard_map/ppermute | solution.py:414
  33.4 1.6 %collective-permute-done.6 = f32[4,128,128]{2,1,0:T(8,128)S(1)} collective-permute-done((f32[4,128,128]{2,1,0:T(8,128)S(1)}, f32[4,128,128]{2,1,0:T(8,128)S(1)}, u32[]{:S(2)}, u32[]{:S(2)}) %collective-permute-start.6) | collective-permute-done | bytes 262176 | tf_op jit(solution)/shard_map/ppermute | solution.py:414
  35.0 1.6 %collective-permute-start.7 = (f32[2,128,128]{2,1,0:T(8,128)S(1)}, f32[2,128,128]{2,1,0:T(8,128)S(1)}, u32[]{:S(2)}, u32[]{:S(2)}) collective-permute-start(f32[2,128,128]{2,1,0:T(8,128)S(1)} %get-tuple-element.31), channel_id=1, source_target_pairs={{0,8},{2,6},{4,12},{6,2},{8,0},{10,14},{12,4},{14,10},{16,24},{18,... | collective-permute-start | bytes 393224 | tf_op jit(solution)/shard_map/ppermute | solution.py:414
  36.7 0.1 collective-permute-done.10
  36.8 2.7 %collective-permute-start.11 = (f32[1,128,128]{2,1,0:T(8,128)S(1)}, f32[1,128,128]{2,1,0:T(8,128)S(1)}, u32[]{:S(2)}, u32[]{:S(2)}) collective-permute-start(f32[1,128,128]{2,1,0:T(8,128)S(1)} %get-tuple-element.34), channel_id=1, source_target_pairs={{0,16},{2,18},{4,20},{6,22},{8,24},{10,26},{12,28},{14,30},{16,0},... | collective-permute-start | bytes 196616 | tf_op jit(solution)/shard_map/ppermute | solution.py:414
  39.5 1.3 %collective-permute-done.7 = f32[2,128,128]{2,1,0:T(8,128)S(1)} collective-permute-done((f32[2,128,128]{2,1,0:T(8,128)S(1)}, f32[2,128,128]{2,1,0:T(8,128)S(1)}, u32[]{:S(2)}, u32[]{:S(2)}) %collective-permute-start.7) | collective-permute-done | bytes 131104 | tf_op jit(solution)/shard_map/ppermute | solution.py:414
  40.8 2.6 %collective-permute-start.8 = (f32[1,128,128]{2,1,0:T(8,128)S(1)}, f32[1,128,128]{2,1,0:T(8,128)S(1)}, u32[]{:S(2)}, u32[]{:S(2)}) collective-permute-start(f32[1,128,128]{2,1,0:T(8,128)S(1)} %get-tuple-element.36), channel_id=1, source_target_pairs={{0,16},{2,18},{4,20},{6,22},{8,24},{10,26},{12,28},{14,30},{16,0},... | collective-permute-start | bytes 196616 | tf_op jit(solution)/shard_map/ppermute | solution.py:414
  43.4 0.0 collective-permute-done.11.refs_2_
  43.4 2.6 %collective-permute-done.8.refs_0_ = f32[1,128,128]{2,1,0:T(8,128)S(1)} collective-permute-done((f32[1,128,128]{2,1,0:T(8,128)S(1)}, f32[1,128,128]{2,1,0:T(8,128)S(1)}, u32[]{:S(2)}, u32[]{:S(2)}) %collective-permute-start.8) | collective-permute-done | bytes 65568 | tf_op jit(solution)/shard_map/ppermute | solution.py:414
  46.0 0.7 %shard_map.71 = f32[256,128]{1,0:T(8,128)} custom-call(f32[1,128,128]{2,1,0:T(8,128)S(1)} %collective-permute-done.8.refs_0_, f32[1,128,128]{2,1,0:T(8,128)S(1)} %get-tuple-element.35.refs_1_, f32[1,128,128]{2,1,0:T(8,128)S(1)} %collective-permute-done.11.refs_2_, f32[1,128,128]{2,1,0:T(8,128)S(1)} %get-tuple-element.33.refs_3_), custom_call_target="tpu_custom_call" | custom-call | flops 32768 | bytes 393216 | tf_op jit(solution)/shard_map/pallas_call | solution.py:422
  (7 shorter events, 0.1 us)
Async XLA Ops:
  0.7 4.8 %collective-permute-start = (s32[4,8]{1,0:T(4,128)S(1)}, s32[4,8]{1,0:T(4,128)S(1)}, u32[]{:S(2)}, u32[]{:S(2)}) collective-permute-start(s32[4,8]{1,0:T(4,128)S(1)} %pad_add_fusion.1), channel_id=1, source_target_pairs={{0,1},{1,0},{2,3},{3,2},{4,5},{5,4},{6,7},{7,6},{8,9},{9,8},{10,11... | collective-permute-start | bytes 392 | tf_op jit(solution)/shard_map/ppermute | solution.py:61
  3.7 1.6 %copy-start = (f32[4096,1,128]{2,1,0:T(1,128)S(1)}, f32[4096,1,128]{2,1,0:T(1,128)}, u32[]{:S(2)}) copy-start(f32[4096,1,128]{2,1,0:T(1,128)} %param.6) | copy-start | bytes 6291460
  5.4 2.5 %copy-start.3 = (s32[2,8]{1,0:T(2,128)S(1)}, s32[2,8]{1,0:T(2,128)}, u32[]{:S(2)}) copy-start(s32[2,8]{1,0:T(2,128)} %refs_0_.1) | copy-start | bytes 196
  5.4 2.6 %copy-start.1 = (f32[2,3,8,4096]{3,2,1,0:T(8,128)S(1)}, f32[2,3,8,4096]{3,2,1,0:T(8,128)}, u32[]{:S(2)}) copy-start(f32[2,3,8,4096]{3,2,1,0:T(8,128)} %param.7) | copy-start | bytes 2359300
  5.4 2.6 %copy-start.2 = (f32[2,3,8,4096]{3,2,1,0:T(8,128)S(1)}, f32[2,3,8,4096]{3,2,1,0:T(8,128)}, u32[]{:S(2)}) copy-start(f32[2,3,8,4096]{3,2,1,0:T(8,128)} %param.8) | copy-start | bytes 2359300
  6.1 6.5 %copy-start.4 = (s32[2,8]{1,0:T(2,128)S(1)}, s32[2,8]{1,0:T(2,128)}, u32[]{:S(2)}) copy-start(s32[2,8]{1,0:T(2,128)} %lengths_ref.1) | copy-start | bytes 196
  6.1 6.4 %copy-start.5 = (s32[2,8,1]{1,2,0:T(1,128)S(1)}, s32[2,8,1]{1,2,0:T(1,128)}, u32[]{:S(2)}) copy-start(s32[2,8,1]{1,2,0:T(1,128)} %param.9) | copy-start | bytes 196
  6.1 6.4 %collective-permute-start.1 = (f32[384,128]{1,0:T(8,128)S(1)}, f32[384,128]{1,0:T(8,128)S(1)}, u32[]{:S(2)}, u32[]{:S(2)}) collective-permute-start(f32[384,128]{1,0:T(8,128)S(1)} %shard_map.65), channel_id=1, source_target_pairs={{0,1},{1,0},{2,3},{3,2},{4,5},{5,4},{6,7},{7,6},{8,9},{9,8},{10,11... | collective-permute-start | bytes 589832 | tf_op jit(solution)/shard_map/ppermute | solution.py:61
  8.0 1.2 %collective-permute-start.2 = (s32[6,8]{1,0:T(8,128)S(1)}, s32[6,8]{1,0:T(8,128)S(1)}, u32[]{:S(2)}, u32[]{:S(2)}) collective-permute-start(s32[6,8]{1,0:T(8,128)S(1)} %pad_add_fusion), channel_id=1, source_target_pairs={{0,2},{2,0},{4,6},{6,4},{8,10},{10,8},{12,14},{14,12},{16,18},{18,... | collective-permute-start | bytes 584 | tf_op jit(solution)/shard_map/ppermute | solution.py:61
  17.1 5.7 %collective-permute-start.3 = (f32[384,128]{1,0:T(8,128)S(1)}, f32[384,128]{1,0:T(8,128)S(1)}, u32[]{:S(2)}, u32[]{:S(2)}) collective-permute-start(f32[384,128]{1,0:T(8,128)S(1)} %get-tuple-element.23), channel_id=1, source_target_pairs={{0,1},{1,0},{2,3},{3,2},{4,5},{5,4},{6,7},{7,6},{8,9},{9,8},{10,11... | collective-permute-start | bytes 589832 | tf_op jit(solution)/shard_map/ppermute | solution.py:61
  18.3 4.6 %collective-permute-start.5 = (f32[16,32,128]{2,1,0:T(8,128)S(1)}, f32[16,32,128]{2,1,0:T(8,128)S(1)}, u32[]{:S(2)}, u32[]{:S(2)}) collective-permute-start(f32[16,32,128]{2,1,0:T(8,128)S(1)} %bitcast.19), channel_id=1, source_target_pairs={{0,2},{2,0},{4,6},{6,4},{8,10},{10,8},{12,14},{14,12},{16,18},{18,... | collective-permute-start | bytes 786440 | tf_op jit(solution)/shard_map/ppermute | solution.py:61
  22.8 1.7 %collective-permute-start.4 = (f32[384,128]{1,0:T(8,128)S(1)}, f32[384,128]{1,0:T(8,128)S(1)}, u32[]{:S(2)}, u32[]{:S(2)}) collective-permute-start(f32[384,128]{1,0:T(8,128)S(1)} %collective-permute-done.3.terms_ref), channel_id=1, source_target_pairs={{0,2},{2,0},{4,6},{6,4},{8,10},{10,8},{12,14},{14,12},{16,18},{18,... | collective-permute-start | bytes 589832 | tf_op jit(solution)/shard_map/ppermute | solution.py:61
  25.3 6.4 %collective-permute-start.9 = (f32[4,128,128]{2,1,0:T(8,128)S(1)}, f32[4,128,128]{2,1,0:T(8,128)S(1)}, u32[]{:S(2)}, u32[]{:S(2)}) collective-permute-start(f32[4,128,128]{2,1,0:T(8,128)S(1)} %get-tuple-element.27), channel_id=1, source_target_pairs={{0,4},{2,10},{4,0},{6,14},{8,12},{10,2},{12,8},{14,6},{16,20},{18,... | collective-permute-start | bytes 786440 | tf_op jit(solution)/shard_map/ppermute | solution.py:414
  26.9 8.1 %collective-permute-start.6 = (f32[4,128,128]{2,1,0:T(8,128)S(1)}, f32[4,128,128]{2,1,0:T(8,128)S(1)}, u32[]{:S(2)}, u32[]{:S(2)}) collective-permute-start(f32[4,128,128]{2,1,0:T(8,128)S(1)} %get-tuple-element.25), channel_id=1, source_target_pairs={{0,4},{2,10},{4,0},{6,14},{8,12},{10,2},{12,8},{14,6},{16,20},{18,... | collective-permute-start | bytes 786440 | tf_op jit(solution)/shard_map/ppermute | solution.py:414
  31.8 5.0 %collective-permute-start.10 = (f32[2,128,128]{2,1,0:T(8,128)S(1)}, f32[2,128,128]{2,1,0:T(8,128)S(1)}, u32[]{:S(2)}, u32[]{:S(2)}) collective-permute-start(f32[2,128,128]{2,1,0:T(8,128)S(1)} %get-tuple-element.29), channel_id=1, source_target_pairs={{0,8},{2,6},{4,12},{6,2},{8,0},{10,14},{12,4},{14,10},{16,24},{18,... | collective-permute-start | bytes 393224 | tf_op jit(solution)/shard_map/ppermute | solution.py:414
  35.0 5.7 %collective-permute-start.7 = (f32[2,128,128]{2,1,0:T(8,128)S(1)}, f32[2,128,128]{2,1,0:T(8,128)S(1)}, u32[]{:S(2)}, u32[]{:S(2)}) collective-permute-start(f32[2,128,128]{2,1,0:T(8,128)S(1)} %get-tuple-element.31), channel_id=1, source_target_pairs={{0,8},{2,6},{4,12},{6,2},{8,0},{10,14},{12,4},{14,10},{16,24},{18,... | collective-permute-start | bytes 393224 | tf_op jit(solution)/shard_map/ppermute | solution.py:414
  36.8 6.6 %collective-permute-start.11 = (f32[1,128,128]{2,1,0:T(8,128)S(1)}, f32[1,128,128]{2,1,0:T(8,128)S(1)}, u32[]{:S(2)}, u32[]{:S(2)}) collective-permute-start(f32[1,128,128]{2,1,0:T(8,128)S(1)} %get-tuple-element.34), channel_id=1, source_target_pairs={{0,16},{2,18},{4,20},{6,22},{8,24},{10,26},{12,28},{14,30},{16,0},... | collective-permute-start | bytes 196616 | tf_op jit(solution)/shard_map/ppermute | solution.py:414
  40.8 5.2 %collective-permute-start.8 = (f32[1,128,128]{2,1,0:T(8,128)S(1)}, f32[1,128,128]{2,1,0:T(8,128)S(1)}, u32[]{:S(2)}, u32[]{:S(2)}) collective-permute-start(f32[1,128,128]{2,1,0:T(8,128)S(1)} %get-tuple-element.36), channel_id=1, source_target_pairs={{0,16},{2,18},{4,20},{6,22},{8,24},{10,26},{12,28},{14,30},{16,0},... | collective-permute-start | bytes 196616 | tf_op jit(solution)/shard_map/ppermute | solution.py:414

commit v10 on v8

--- a/solution.py
+++ b/solution.py
@@ -362,28 +362,34 @@
 PIECES = 4
 
 
+def piece_rows(share):
+    few = max(1, share * 7 // 256) * SUB
+    many = share // 2 - few
+    return (many, many, few, few)
+
+
 def last_body(orders, groups, share, count, *refs):
     total, outs, padded = refs[2 * count + 1], refs[2 * count + 2 : -1], refs[-1]
-    span, slots, piece = share + 2 * TILE, groups // 2, share // PIECES
+    span, slots = share + 2 * TILE, groups // 2
     for i in range(count):
         add_terms(*refs[2 * i : 2 * i + 2], total, share, slots, padded)
     for which in range(PIECES):
         for place, slot in enumerate(arranged(orders[which % 2])):
             out = outs[2 * which + (place * 2 >= slots)]
-            begin = slot * span + TILE + which * piece
-            out[place % (slots // 2)] = total[begin : begin + piece, :]
+            begin = slot * span + TILE + sum(piece_rows(share)[:which])
+            out[place % (slots // 2)] = total[begin : begin + out.shape[1], :]
 
 
 def last_sums(groups_of, total, rows, orders):
     groups = lax.axis_size("grp")
     share, slots = rows // groups, groups // 2
-    out = floats(slots // 2, share // PIECES, LANES)
+    out = tuple(floats(slots // 2, r, LANES) for r in piece_rows(share) for _ in range(2))
     flat = [a for pair in groups_of for a in pair]
     count = len(groups_of)
     terms_rows = max(a.shape[0] for _, a in groups_of)
     outs = call(
         functools.partial(last_body, orders, groups, share, count),
-        (floats(*total.shape),) + (out,) * (2 * PIECES), [SMEM, VMEM] * count + [VMEM],
+        (floats(*total.shape),) + out, [SMEM, VMEM] * count + [VMEM],
         total.size, 8 * total.size, input_output_aliases={2 * count: 0},
         scratch_shapes=[padded_rows(terms_rows + TILE)],
     )(*flat, total)[1:]
@@ -398,11 +404,12 @@
 
 
 def finish_body(*refs):
-    out_ref = refs[-1]
+    out_ref, begin = refs[-1], 0
     for i in range(0, len(refs) - 1, 2):
         got, held = refs[i : i + 2]
         rows = got.shape[1]
-        out_ref[i // 2 * rows : (i // 2 + 1) * rows] = got[0] + held[0]
+        out_ref[begin : begin + rows] = got[0] + held[0]
+        begin += rows
 
 
 def halve(stages, orders):

time: 47.6 us -> 49.1 us (1.032)
  waiting for transfers between devices: 15.1 us -> 17.1 us
  starting transfers between devices: 20.5 us -> 20 us
    ppermute x16, waiting for transfers between devices: 15.1 us -> 17.1 us  [swap_over(): return lambda value: lax.ppermute(value, axis, ring)]
  transfers between devices with their start and end apart: 16 -> 16, of which waited for: 9 -> 9; matrix products, arithmetic and copies ran while one was open for 0% -> 0% of each run, Pallas kernels for 6% -> 5%
where the time goes in v10:
time: 49.1 us; the launch traced here: 48.9 us
  starting transfers between devices  20 us (41%)
  waiting for transfers between devices  17.1 us (35%)
  Pallas kernels  9.26 us (19%)
  local copies, waits for them, and re-layouts  1.63 us (3%)
  other arithmetic  0.79 us (2%)
    ppermute x16, starting transfers between devices, swap_over(): return lambda value: lax.ppermute(value, axis, ring)  20 us
    ppermute x16, waiting for transfers between devices, swap_over(): return lambda value: lax.ppermute(value, axis, ring)  17.1 us
    pallas_call x1, Pallas kernels, soundings_partial(): call(functools.partial(fields_body, packed), (floats(tiles * TILE, LANES)...  4.55 us
    unnamed x12, local copies, waits for them, and re-layouts  1.62 us
  transfers between devices with their start and end apart: 16, of which 9 were waited for; matrix products, arithmetic and copies ran while one was open for 0% of the time, Pallas kernels for 5%

profile of v10, /device:TPU:0, one launch (start us, length us, event | category | flops | bytes accessed | tf_op | source)
XLA Modules:
  0.0 48.9 jit_solution(9320423590929980249)
XLA Ops:
  0.0 0.7 %pad_add_fusion.1 = s32[4,8]{1,0:T(4,128)S(1)} fusion(s32[2,8]{1,0:T(2,128)} %lengths_ref.1, s32[2,8]{1,0:T(2,128)} %refs_0_.1), kind=kLoop, calls=%fused_computation.9 | loop fusion | flops 32 | bytes 256 | tf_op jit(solution)/shard_map/concatenate | solution.py:464
  0.7 3.0 %collective-permute-start = (s32[4,8]{1,0:T(4,128)S(1)}, s32[4,8]{1,0:T(4,128)S(1)}, u32[]{:S(2)}, u32[]{:S(2)}) collective-permute-start(s32[4,8]{1,0:T(4,128)S(1)} %pad_add_fusion.1), channel_id=1, source_target_pairs={{0,1},{1,0},{2,3},{3,2},{4,5},{5,4},{6,7},{7,6},{8,9},{9,8},{10,11... | collective-permute-start | bytes 392 | tf_op jit(solution)/shard_map/ppermute | solution.py:61
  3.7 1.6 %copy-done = f32[4096,1,128]{2,1,0:T(1,128)S(1)} copy-done((f32[4096,1,128]{2,1,0:T(1,128)S(1)}, f32[4096,1,128]{2,1,0:T(1,128)}, u32[]{:S(2)}) %copy-start) | copy-done | bytes 2097176
  5.3 0.1 shard_map.64.block_ref.table_ref.refs_4_
  5.4 0.0 copy-start.3
  5.4 0.0 copy-start.1
  5.4 0.0 copy-start.2
  5.5 0.0 collective-permute-done.index_ref
  5.5 0.6 %shard_map.65 = f32[384,128]{1,0:T(8,128)S(1)} custom-call(s32[4,8]{1,0:T(4,128)S(1)} %collective-permute-done.index_ref, f32[4096,128]{1,0:T(8,128)S(1)} %shard_map.64.block_ref.table_ref.refs_4_), custom_call_target="tpu_custom_call" | custom-call | bytes 393216 | tf_op jit(solution)/shard_map/pallas_call | solution.py:106
  6.1 0.0 copy-start.4
  6.1 0.0 copy-start.5
  6.1 1.9 %collective-permute-start.1 = (f32[384,128]{1,0:T(8,128)S(1)}, f32[384,128]{1,0:T(8,128)S(1)}, u32[]{:S(2)}, u32[]{:S(2)}) collective-permute-start(f32[384,128]{1,0:T(8,128)S(1)} %shard_map.65), channel_id=1, source_target_pairs={{0,1},{1,0},{2,3},{3,2},{4,5},{5,4},{6,7},{7,6},{8,9},{9,8},{10,11... | collective-permute-start | bytes 589832 | tf_op jit(solution)/shard_map/ppermute | solution.py:61
  8.0 0.1 collective-permute-start.2
  8.1 0.9 %shard_map.66 = (f32[3,8,8,8,128]{4,3,2,1,0:T(8,128)S(1)}, f32[3,8,8,8,128]{4,3,2,1,0:T(8,128)S(1)}) custom-call(f32[1536,128]{1,0:T(8,128)S(1)} %bitcast.17, f32[1536,128]{1,0:T(8,128)S(1)} %bitcast.18), custom_call_target="tpu_custom_call" | custom-call | flops 1572864 | bytes 3145728 | tf_op jit(solution)/shard_map/pallas_call | solution.py:146
  9.0 0.2 collective-permute-done.2
  9.2 3.3 %collective-permute-done.1.answer_ref = f32[384,128]{1,0:T(8,128)S(1)} collective-permute-done((f32[384,128]{1,0:T(8,128)S(1)}, f32[384,128]{1,0:T(8,128)S(1)}, u32[]{:S(2)}, u32[]{:S(2)}) %collective-permute-start.1) | collective-permute-done | bytes 196640 | tf_op jit(solution)/shard_map/ppermute | solution.py:61
  12.5 0.0 copy-done.4
  12.5 4.6 %shard_map.67 = (f32[512,128]{1,0:T(8,128)S(1)}, f32[384,128]{1,0:T(8,128)S(1)}) custom-call(s32[2,8]{1,0:T(2,128)S(1)} %copy-done.3, s32[2,8]{1,0:T(2,128)S(1)} %bitcast.21, s32[2,8]{1,0:T(2,128)S(1)} %copy-done.4, f32[4096,128]{1,0:T(8,128)S(1)} %shard_map.64.block_ref.table_ref.refs_4_, f32[384,128]{1,0:T(8,128)S(1)} %collective-permute-done.1.answer_ref, ...), custom_call_target="tpu_custom_call" | custom-call | flops 32768000 | bytes 2621440 | tf_op jit(solution)/shard_map/pallas_call | solution.py:283
  17.1 1.2 %collective-permute-start.3 = (f32[384,128]{1,0:T(8,128)S(1)}, f32[384,128]{1,0:T(8,128)S(1)}, u32[]{:S(2)}, u32[]{:S(2)}) collective-permute-start(f32[384,128]{1,0:T(8,128)S(1)} %get-tuple-element.31), channel_id=1, source_target_pairs={{0,1},{1,0},{2,3},{3,2},{4,5},{5,4},{6,7},{7,6},{8,9},{9,8},{10,11... | collective-permute-start | bytes 589832 | tf_op jit(solution)/shard_map/ppermute | solution.py:61
  18.3 0.0 collective-permute-start.5
  18.3 4.6 %collective-permute-done.3.terms_ref = f32[384,128]{1,0:T(8,128)S(1)} collective-permute-done((f32[384,128]{1,0:T(8,128)S(1)}, f32[384,128]{1,0:T(8,128)S(1)}, u32[]{:S(2)}, u32[]{:S(2)}) %collective-permute-start.3) | collective-permute-done | bytes 196640 | tf_op jit(solution)/shard_map/ppermute | solution.py:61
  22.8 0.0 collective-permute-start.4
  22.8 0.0 collective-permute-done.5.refs_3_
  22.8 0.9 %shard_map.68.given_total = f32[2592,128]{1,0:T(8,128)S(1)} custom-call(s32[2,8]{1,0:T(2,128)S(1)} %copy-done.3, f32[16,32,128]{2,1,0:T(8,128)S(1)} %bitcast.20, s32[2,8]{1,0:T(2,128)S(1)} %slice.55.refs_2_, f32[16,32,128]{2,1,0:T(8,128)S(1)} %collective-permute-done.5.refs_3_, f32[4096,128]{1,0:T(8,128)S(1)} %shard_map.64.block_ref.table_ref.refs_4_), custom_call_target="tpu_custom_call" | custom-call | flops 331776 | bytes 2654208 | tf_op jit(solution)/shard_map/pallas_call | solution.py:343
  23.7 0.7 %shard_map.69.refs_2_ = f32[2592,128]{1,0:T(8,128)S(1)} custom-call(s32[4,8]{1,0:T(4,128)S(1)} %collective-permute-done.index_ref, f32[384,128]{1,0:T(8,128)S(1)} %collective-permute-done.3.terms_ref, f32[2592,128]{1,0:T(8,128)S(1)} %shard_map.68.given_total), custom_call_target="tpu_custom_call", output_to_operand_aliasing={{}: (2, {})} | custom-call | flops 331776 | bytes 2654208 | tf_op jit(solution)/shard_map/pallas_call | solution.py:355
  24.4 0.0 collective-permute-done.4.refs_1_
  24.4 0.7 %shard_map.70 = (f32[2592,128]{1,0:T(8,128)S(1)}, f32[4,72,128]{2,1,0:T(8,128)S(1)}, f32[4,72,128]{2,1,0:T(8,128)S(1)}, f32[4,72,128]{2,1,0:T(8,128)S(1)}, f32[4...) custom-call(s32[4,8]{1,0:T(4,128)S(1)} %slice.54.refs_0_, ...), custom_call_target="tpu_custom_call", output_to_operand_aliasing={{0}: (2, {})} | custom-call | flops 331776 | bytes 2654208 | tf_op jit(solution)/shard_map/pallas_call | solution.py:390
  25.2 1.6 %collective-permute-start.13 = (f32[4,56,128]{2,1,0:T(8,128)S(1)}, f32[4,56,128]{2,1,0:T(8,128)S(1)}, u32[]{:S(2)}, u32[]{:S(2)}) collective-permute-start(f32[4,56,128]{2,1,0:T(8,128)S(1)} %get-tuple-element.41), channel_id=1, source_target_pairs={{0,8},{2,10},{4,12},{6,14},{8,0},{10,2},{12,4},{14,6},{16,24},{18,... | collective-permute-start | bytes 344072 | tf_op jit(solution)/shard_map/ppermute | solution.py:61
  26.8 1.5 %collective-permute-start.11 = (f32[4,56,128]{2,1,0:T(8,128)S(1)}, f32[4,56,128]{2,1,0:T(8,128)S(1)}, u32[]{:S(2)}, u32[]{:S(2)}) collective-permute-start(f32[4,56,128]{2,1,0:T(8,128)S(1)} %get-tuple-element.39), channel_id=1, source_target_pairs={{0,4},{2,6},{4,0},{6,2},{8,12},{10,14},{12,8},{14,10},{16,20},{18,... | collective-permute-start | bytes 344072 | tf_op jit(solution)/shard_map/ppermute | solution.py:61
  28.3 0.4 collective-permute-start.8
  28.8 0.5 %collective-permute-start.6 = (f32[4,72,128]{2,1,0:T(8,128)S(1)}, f32[4,72,128]{2,1,0:T(8,128)S(1)}, u32[]{:S(2)}, u32[]{:S(2)}) collective-permute-start(f32[4,72,128]{2,1,0:T(8,128)S(1)} %get-tuple-element.33), channel_id=1, source_target_pairs={{0,4},{2,6},{4,0},{6,2},{8,12},{10,14},{12,8},{14,10},{16,20},{18,... | collective-permute-start | bytes 442376 | tf_op jit(solution)/shard_map/ppermute | solution.py:61
  29.3 1.5 %collective-permute-done.13 = f32[4,56,128]{2,1,0:T(8,128)S(1)} collective-permute-done((f32[4,56,128]{2,1,0:T(8,128)S(1)}, f32[4,56,128]{2,1,0:T(8,128)S(1)}, u32[]{:S(2)}, u32[]{:S(2)}) %collective-permute-start.13) | collective-permute-done | bytes 114720 | tf_op jit(solution)/shard_map/ppermute | solution.py:61
  30.8 2.1 %collective-permute-start.14 = (f32[2,56,128]{2,1,0:T(8,128)S(1)}, f32[2,56,128]{2,1,0:T(8,128)S(1)}, u32[]{:S(2)}, u32[]{:S(2)}) collective-permute-start(f32[2,56,128]{2,1,0:T(8,128)S(1)} %get-tuple-element.50), channel_id=1, source_target_pairs={{0,4},{2,6},{4,0},{6,2},{8,12},{10,14},{12,8},{14,10},{16,20},{18,... | collective-permute-start | bytes 172040 | tf_op jit(solution)/shard_map/ppermute | solution.py:61
  32.9 1.2 %collective-permute-done.8 = f32[4,72,128]{2,1,0:T(8,128)S(1)} collective-permute-done((f32[4,72,128]{2,1,0:T(8,128)S(1)}, f32[4,72,128]{2,1,0:T(8,128)S(1)}, u32[]{:S(2)}, u32[]{:S(2)}) %collective-permute-start.8) | collective-permute-done | bytes 147488 | tf_op jit(solution)/shard_map/ppermute | solution.py:61
  34.1 1.5 %collective-permute-start.9 = (f32[2,72,128]{2,1,0:T(8,128)S(1)}, f32[2,72,128]{2,1,0:T(8,128)S(1)}, u32[]{:S(2)}, u32[]{:S(2)}) collective-permute-start(f32[2,72,128]{2,1,0:T(8,128)S(1)} %get-tuple-element.46), channel_id=1, source_target_pairs={{0,4},{2,6},{4,0},{6,2},{8,12},{10,14},{12,8},{14,10},{16,20},{18,... | collective-permute-start | bytes 221192 | tf_op jit(solution)/shard_map/ppermute | solution.py:61
  35.6 0.3 collective-permute-done.6
  35.9 1.3 %collective-permute-start.7 = (f32[2,72,128]{2,1,0:T(8,128)S(1)}, f32[2,72,128]{2,1,0:T(8,128)S(1)}, u32[]{:S(2)}, u32[]{:S(2)}) collective-permute-start(f32[2,72,128]{2,1,0:T(8,128)S(1)} %get-tuple-element.48), channel_id=1, source_target_pairs={{0,8},{2,10},{4,12},{6,14},{8,0},{10,2},{12,4},{14,6},{16,24},{18,... | collective-permute-start | bytes 221192 | tf_op jit(solution)/shard_map/ppermute | solution.py:61
  37.2 0.0 collective-permute-done.11
  37.3 0.8 %collective-permute-start.12 = (f32[2,56,128]{2,1,0:T(8,128)S(1)}, f32[2,56,128]{2,1,0:T(8,128)S(1)}, u32[]{:S(2)}, u32[]{:S(2)}) collective-permute-start(f32[2,56,128]{2,1,0:T(8,128)S(1)} %get-tuple-element.52), channel_id=1, source_target_pairs={{0,8},{2,10},{4,12},{6,14},{8,0},{10,2},{12,4},{14,6},{16,24},{18,... | collective-permute-start | bytes 172040 | tf_op jit(solution)/shard_map/ppermute | solution.py:61
  38.1 0.4 collective-permute-done.9.got_high
  38.5 1.9 %collective-permute-done.7.got_low = f32[2,72,128]{2,1,0:T(8,128)S(1)} collective-permute-done((f32[2,72,128]{2,1,0:T(8,128)S(1)}, f32[2,72,128]{2,1,0:T(8,128)S(1)}, u32[]{:S(2)}, u32[]{:S(2)}) %collective-permute-start.7) | collective-permute-done | bytes 73760 | tf_op jit(solution)/shard_map/ppermute | solution.py:61
  40.4 2.6 %collective-permute-start.10 = (f32[1,144,128]{2,1,0:T(8,128)S(1)}, f32[1,144,128]{2,1,0:T(8,128)S(1)}, u32[]{:S(2)}, u32[]{:S(2)}) collective-permute-start(f32[1,144,128]{2,1,0:T(8,128)S(1)} %get-tuple-element.37), channel_id=1, source_target_pairs={{0,16},{2,18},{4,20},{6,22},{8,24},{10,26},{12,28},{14,30},{16,0},... | collective-permute-start | bytes 221192 | tf_op jit(solution)/shard_map/ppermute | solution.py:61
  43.1 0.0 collective-permute-done.14.got_high
  43.1 0.0 collective-permute-done.12.got_low
  43.1 1.5 %collective-permute-start.15 = (f32[1,112,128]{2,1,0:T(8,128)S(1)}, f32[1,112,128]{2,1,0:T(8,128)S(1)}, u32[]{:S(2)}, u32[]{:S(2)}) collective-permute-start(f32[1,112,128]{2,1,0:T(8,128)S(1)} %get-tuple-element.43), channel_id=1, source_target_pairs={{0,16},{2,18},{4,20},{6,22},{8,24},{10,26},{12,28},{14,30},{16,0},... | collective-permute-start | bytes 172040 | tf_op jit(solution)/shard_map/ppermute | solution.py:61
  44.6 3.7 %collective-permute-done.15.refs_2_ = f32[1,112,128]{2,1,0:T(8,128)S(1)} collective-permute-done((f32[1,112,128]{2,1,0:T(8,128)S(1)}, f32[1,112,128]{2,1,0:T(8,128)S(1)}, u32[]{:S(2)}, u32[]{:S(2)}) %collective-permute-start.15) | collective-permute-done | bytes 57376 | tf_op jit(solution)/shard_map/ppermute | solution.py:61
  48.2 0.0 collective-permute-done.10.refs_0_
  48.2 0.7 %shard_map.73 = f32[256,128]{1,0:T(8,128)} custom-call(f32[1,144,128]{2,1,0:T(8,128)S(1)} %collective-permute-done.10.refs_0_, f32[1,144,128]{2,1,0:T(8,128)S(1)} %get-tuple-element.38.refs_1_, f32[1,112,128]{2,1,0:T(8,128)S(1)} %collective-permute-done.15.refs_2_, f32[1,112,128]{2,1,0:T(8,128)S(1)} %get-tuple-element.44.refs_3_), custom_call_target="tpu_custom_call" | custom-call | flops 32768 | bytes 393216 | tf_op jit(solution)/shard_map/pallas_call | solution.py:441
  (14 shorter events, 0.1 us)
Async XLA Ops:
  0.7 4.8 %collective-permute-start = (s32[4,8]{1,0:T(4,128)S(1)}, s32[4,8]{1,0:T(4,128)S(1)}, u32[]{:S(2)}, u32[]{:S(2)}) collective-permute-start(s32[4,8]{1,0:T(4,128)S(1)} %pad_add_fusion.1), channel_id=1, source_target_pairs={{0,1},{1,0},{2,3},{3,2},{4,5},{5,4},{6,7},{7,6},{8,9},{9,8},{10,11... | collective-permute-start | bytes 392 | tf_op jit(solution)/shard_map/ppermute | solution.py:61
  3.7 1.6 %copy-start = (f32[4096,1,128]{2,1,0:T(1,128)S(1)}, f32[4096,1,128]{2,1,0:T(1,128)}, u32[]{:S(2)}) copy-start(f32[4096,1,128]{2,1,0:T(1,128)} %param.6) | copy-start | bytes 6291460
  5.4 2.5 %copy-start.3 = (s32[2,8]{1,0:T(2,128)S(1)}, s32[2,8]{1,0:T(2,128)}, u32[]{:S(2)}) copy-start(s32[2,8]{1,0:T(2,128)} %refs_0_.1) | copy-start | bytes 196
  5.4 2.6 %copy-start.1 = (f32[2,3,8,4096]{3,2,1,0:T(8,128)S(1)}, f32[2,3,8,4096]{3,2,1,0:T(8,128)}, u32[]{:S(2)}) copy-start(f32[2,3,8,4096]{3,2,1,0:T(8,128)} %param.7) | copy-start | bytes 2359300
  5.4 2.6 %copy-start.2 = (f32[2,3,8,4096]{3,2,1,0:T(8,128)S(1)}, f32[2,3,8,4096]{3,2,1,0:T(8,128)}, u32[]{:S(2)}) copy-start(f32[2,3,8,4096]{3,2,1,0:T(8,128)} %param.8) | copy-start | bytes 2359300
  6.1 6.5 %copy-start.4 = (s32[2,8]{1,0:T(2,128)S(1)}, s32[2,8]{1,0:T(2,128)}, u32[]{:S(2)}) copy-start(s32[2,8]{1,0:T(2,128)} %lengths_ref.1) | copy-start | bytes 196
  6.1 6.4 %copy-start.5 = (s32[2,8,1]{1,2,0:T(1,128)S(1)}, s32[2,8,1]{1,2,0:T(1,128)}, u32[]{:S(2)}) copy-start(s32[2,8,1]{1,2,0:T(1,128)} %param.9) | copy-start | bytes 196
  6.1 6.4 %collective-permute-start.1 = (f32[384,128]{1,0:T(8,128)S(1)}, f32[384,128]{1,0:T(8,128)S(1)}, u32[]{:S(2)}, u32[]{:S(2)}) collective-permute-start(f32[384,128]{1,0:T(8,128)S(1)} %shard_map.65), channel_id=1, source_target_pairs={{0,1},{1,0},{2,3},{3,2},{4,5},{5,4},{6,7},{7,6},{8,9},{9,8},{10,11... | collective-permute-start | bytes 589832 | tf_op jit(solution)/shard_map/ppermute | solution.py:61
  8.0 1.2 %collective-permute-start.2 = (s32[6,8]{1,0:T(8,128)S(1)}, s32[6,8]{1,0:T(8,128)S(1)}, u32[]{:S(2)}, u32[]{:S(2)}) collective-permute-start(s32[6,8]{1,0:T(8,128)S(1)} %pad_add_fusion), channel_id=1, source_target_pairs={{0,2},{2,0},{4,6},{6,4},{8,10},{10,8},{12,14},{14,12},{16,18},{18,... | collective-permute-start | bytes 584 | tf_op jit(solution)/shard_map/ppermute | solution.py:61
  17.1 5.7 %collective-permute-start.3 = (f32[384,128]{1,0:T(8,128)S(1)}, f32[384,128]{1,0:T(8,128)S(1)}, u32[]{:S(2)}, u32[]{:S(2)}) collective-permute-start(f32[384,128]{1,0:T(8,128)S(1)} %get-tuple-element.31), channel_id=1, source_target_pairs={{0,1},{1,0},{2,3},{3,2},{4,5},{5,4},{6,7},{7,6},{8,9},{9,8},{10,11... | collective-permute-start | bytes 589832 | tf_op jit(solution)/shard_map/ppermute | solution.py:61
  18.3 4.6 %collective-permute-start.5 = (f32[16,32,128]{2,1,0:T(8,128)S(1)}, f32[16,32,128]{2,1,0:T(8,128)S(1)}, u32[]{:S(2)}, u32[]{:S(2)}) collective-permute-start(f32[16,32,128]{2,1,0:T(8,128)S(1)} %bitcast.19), channel_id=1, source_target_pairs={{0,2},{2,0},{4,6},{6,4},{8,10},{10,8},{12,14},{14,12},{16,18},{18,... | collective-permute-start | bytes 786440 | tf_op jit(solution)/shard_map/ppermute | solution.py:61
  22.8 1.6 %collective-permute-start.4 = (f32[384,128]{1,0:T(8,128)S(1)}, f32[384,128]{1,0:T(8,128)S(1)}, u32[]{:S(2)}, u32[]{:S(2)}) collective-permute-start(f32[384,128]{1,0:T(8,128)S(1)} %collective-permute-done.3.terms_ref), channel_id=1, source_target_pairs={{0,2},{2,0},{4,6},{6,4},{8,10},{10,8},{12,14},{14,12},{16,18},{18,... | collective-permute-start | bytes 589832 | tf_op jit(solution)/shard_map/ppermute | solution.py:61
  25.2 5.6 %collective-permute-start.13 = (f32[4,56,128]{2,1,0:T(8,128)S(1)}, f32[4,56,128]{2,1,0:T(8,128)S(1)}, u32[]{:S(2)}, u32[]{:S(2)}) collective-permute-start(f32[4,56,128]{2,1,0:T(8,128)S(1)} %get-tuple-element.41), channel_id=1, source_target_pairs={{0,8},{2,10},{4,12},{6,14},{8,0},{10,2},{12,4},{14,6},{16,24},{18,... | collective-permute-start | bytes 344072 | tf_op jit(solution)/shard_map/ppermute | solution.py:61
  26.8 10.4 %collective-permute-start.11 = (f32[4,56,128]{2,1,0:T(8,128)S(1)}, f32[4,56,128]{2,1,0:T(8,128)S(1)}, u32[]{:S(2)}, u32[]{:S(2)}) collective-permute-start(f32[4,56,128]{2,1,0:T(8,128)S(1)} %get-tuple-element.39), channel_id=1, source_target_pairs={{0,4},{2,6},{4,0},{6,2},{8,12},{10,14},{12,8},{14,10},{16,20},{18,... | collective-permute-start | bytes 344072 | tf_op jit(solution)/shard_map/ppermute | solution.py:61
  28.3 5.7 %collective-permute-start.8 = (f32[4,72,128]{2,1,0:T(8,128)S(1)}, f32[4,72,128]{2,1,0:T(8,128)S(1)}, u32[]{:S(2)}, u32[]{:S(2)}) collective-permute-start(f32[4,72,128]{2,1,0:T(8,128)S(1)} %get-tuple-element.35), channel_id=1, source_target_pairs={{0,8},{2,10},{4,12},{6,14},{8,0},{10,2},{12,4},{14,6},{16,24},{18,... | collective-permute-start | bytes 442376 | tf_op jit(solution)/shard_map/ppermute | solution.py:61
  28.8 7.1 %collective-permute-start.6 = (f32[4,72,128]{2,1,0:T(8,128)S(1)}, f32[4,72,128]{2,1,0:T(8,128)S(1)}, u32[]{:S(2)}, u32[]{:S(2)}) collective-permute-start(f32[4,72,128]{2,1,0:T(8,128)S(1)} %get-tuple-element.33), channel_id=1, source_target_pairs={{0,4},{2,6},{4,0},{6,2},{8,12},{10,14},{12,8},{14,10},{16,20},{18,... | collective-permute-start | bytes 442376 | tf_op jit(solution)/shard_map/ppermute | solution.py:61
  30.8 12.3 %collective-permute-start.14 = (f32[2,56,128]{2,1,0:T(8,128)S(1)}, f32[2,56,128]{2,1,0:T(8,128)S(1)}, u32[]{:S(2)}, u32[]{:S(2)}) collective-permute-start(f32[2,56,128]{2,1,0:T(8,128)S(1)} %get-tuple-element.50), channel_id=1, source_target_pairs={{0,4},{2,6},{4,0},{6,2},{8,12},{10,14},{12,8},{14,10},{16,20},{18,... | collective-permute-start | bytes 172040 | tf_op jit(solution)/shard_map/ppermute | solution.py:61
  34.1 4.4 %collective-permute-start.9 = (f32[2,72,128]{2,1,0:T(8,128)S(1)}, f32[2,72,128]{2,1,0:T(8,128)S(1)}, u32[]{:S(2)}, u32[]{:S(2)}) collective-permute-start(f32[2,72,128]{2,1,0:T(8,128)S(1)} %get-tuple-element.46), channel_id=1, source_target_pairs={{0,4},{2,6},{4,0},{6,2},{8,12},{10,14},{12,8},{14,10},{16,20},{18,... | collective-permute-start | bytes 221192 | tf_op jit(solution)/shard_map/ppermute | solution.py:61
  35.9 4.5 %collective-permute-start.7 = (f32[2,72,128]{2,1,0:T(8,128)S(1)}, f32[2,72,128]{2,1,0:T(8,128)S(1)}, u32[]{:S(2)}, u32[]{:S(2)}) collective-permute-start(f32[2,72,128]{2,1,0:T(8,128)S(1)} %get-tuple-element.48), channel_id=1, source_target_pairs={{0,8},{2,10},{4,12},{6,14},{8,0},{10,2},{12,4},{14,6},{16,24},{18,... | collective-permute-start | bytes 221192 | tf_op jit(solution)/shard_map/ppermute | solution.py:61
  37.3 5.8 %collective-permute-start.12 = (f32[2,56,128]{2,1,0:T(8,128)S(1)}, f32[2,56,128]{2,1,0:T(8,128)S(1)}, u32[]{:S(2)}, u32[]{:S(2)}) collective-permute-start(f32[2,56,128]{2,1,0:T(8,128)S(1)} %get-tuple-element.52), channel_id=1, source_target_pairs={{0,8},{2,10},{4,12},{6,14},{8,0},{10,2},{12,4},{14,6},{16,24},{18,... | collective-permute-start | bytes 172040 | tf_op jit(solution)/shard_map/ppermute | solution.py:61
  40.4 7.8 %collective-permute-start.10 = (f32[1,144,128]{2,1,0:T(8,128)S(1)}, f32[1,144,128]{2,1,0:T(8,128)S(1)}, u32[]{:S(2)}, u32[]{:S(2)}) collective-permute-start(f32[1,144,128]{2,1,0:T(8,128)S(1)} %get-tuple-element.37), channel_id=1, source_target_pairs={{0,16},{2,18},{4,20},{6,22},{8,24},{10,26},{12,28},{14,30},{16,0},... | collective-permute-start | bytes 221192 | tf_op jit(solution)/shard_map/ppermute | solution.py:61
  43.1 5.1 %collective-permute-start.15 = (f32[1,112,128]{2,1,0:T(8,128)S(1)}, f32[1,112,128]{2,1,0:T(8,128)S(1)}, u32[]{:S(2)}, u32[]{:S(2)}) collective-permute-start(f32[1,112,128]{2,1,0:T(8,128)S(1)} %get-tuple-element.43), channel_id=1, source_target_pairs={{0,16},{2,18},{4,20},{6,22},{8,24},{10,26},{12,28},{14,30},{16,0},... | collective-permute-start | bytes 172040 | tf_op jit(solution)/shard_map/ppermute | solution.py:61

commit v11 on v10

--- a/solution.py
+++ b/solution.py
@@ -359,25 +359,24 @@
     )(index, terms, total)
 
 
-PIECES = 4
-
-
 def piece_rows(share):
-    few = max(1, share * 7 // 256) * SUB
-    many = share // 2 - few
-    return (many, many, few, few)
+    return (share // 2, share // 4, share // 4)
 
 
 def last_body(orders, groups, share, count, *refs):
     total, outs, padded = refs[2 * count + 1], refs[2 * count + 2 : -1], refs[-1]
     span, slots = share + 2 * TILE, groups // 2
+    second = lax.axis_index("grp") & 1
     for i in range(count):
         add_terms(*refs[2 * i : 2 * i + 2], total, share, slots, padded)
-    for which in range(PIECES):
-        for place, slot in enumerate(arranged(orders[which % 2])):
+    for which, order in enumerate((orders[0],) + orders):
+        for place, slot in enumerate(arranged(order)):
             out = outs[2 * which + (place * 2 >= slots)]
-            begin = slot * span + TILE + sum(piece_rows(share)[:which])
-            out[place % (slots // 2)] = total[begin : begin + out.shape[1], :]
+            if which == 0:
+                flip = (slot ^ (slot >> 1)) & 1
+                slot = slot ^ (second * (3 * flip))
+            begin = pl.multiple_of(slot * span + TILE + sum(piece_rows(share)[:which]), SUB)
+            out[place % (slots // 2)] = total[pl.ds(begin, out.shape[1]), :]
 
 
 def last_sums(groups_of, total, rows, orders):
@@ -393,7 +392,7 @@
         total.size, 8 * total.size, input_output_aliases={2 * count: 0},
         scratch_shapes=[padded_rows(terms_rows + TILE)],
     )(*flat, total)[1:]
-    return [outs[4 * i : 4 * i + 4] for i in range(PIECES // 2)]
+    return outs[:2], outs[2:]
 
 
 def join_body(got_low, low, got_high, high, give_ref, keep_ref):
@@ -412,33 +411,34 @@
         begin += rows
 
 
-def halve(stages, orders):
-    bit_pairs = list(zip(*orders))
-    state = list(stages)
-    for step, (low_bit, high_bit) in enumerate(bit_pairs[:2]):
-        for i, (low_give, low, high_give, high) in enumerate(state):
+def halve(whole, split, orders):
+    groups = lax.axis_size("grp")
+    give, keep = whole
+    low_give, low, high_give, high = split
+    for step, (low_bit, high_bit) in enumerate(zip(*orders)):
+        if step < 2:
             got_low = swap_over("grp", 2 << low_bit)(low_give)
             got_high = swap_over("grp", 2 << high_bit)(high_give)
-            cut = low.shape[0] // 2
-            if step == 0:
-                low_give, low = got_low[:cut] + low[:cut], got_low[cut:] + low[cut:]
-                high_give, high = got_high[:cut] + high[:cut], got_high[cut:] + high[cut:]
-                state[i] = low_give, low, high_give, high
-            else:
-                out = floats(cut, low.shape[1] + high.shape[1], LANES)
-                state[i] = call(
-                    join_body, (out, out), [VMEM] * 4, low.size, 24 * low.size
-                )(got_low, low, got_high, high)
-    last = []
-    for give, keep in state:
-        for bit, _ in bit_pairs[2:]:
-            got = swap_over("grp", 2 << bit)(give)
-            cut = keep.shape[0] // 2
-            if cut:
-                give, keep = got[:cut] + keep[:cut], got[cut:] + keep[cut:]
-        last += [got, keep]
-    out = floats(sum(a.shape[1] for a in last) // 2, LANES)
-    return call(finish_body, out, [VMEM] * len(last), out.size, 12 * out.size)(*last)
+        else:
+            got_both = swap_over("grp", 2 << low_bit)(both_give)
+        ring = [(i, i ^ (2 << (high_bit if i & 1 else low_bit))) for i in range(groups)]
+        got = lax.ppermute(give, "grp", ring)
+        cut = keep.shape[0] // 2
+        if step == 0:
+            low_give, low = got_low[:cut] + low[:cut], got_low[cut:] + low[cut:]
+            high_give, high = got_high[:cut] + high[:cut], got_high[cut:] + high[cut:]
+        elif step == 1:
+            out = floats(cut, low.shape[1] + high.shape[1], LANES)
+            both_give, both = call(
+                join_body, (out, out), [VMEM] * 4, low.size, 24 * low.size
+            )(got_low, low, got_high, high)
+        elif cut:
+            both_give, both = got_both[:cut] + both[:cut], got_both[cut:] + both[cut:]
+        if cut:
+            give, keep = got[:cut] + keep[:cut], got[cut:] + keep[cut:]
+    last = (got, keep, got_both, both)
+    out = floats(keep.shape[1] + both.shape[1], LANES)
+    return call(finish_body, out, [VMEM] * 4, out.size, 12 * out.size)(*last)
 
 
 def hold_body(block_ref, out_ref, sem):
@@ -501,7 +501,7 @@
 
     bits = tuple(range(groups.bit_length() - 2))
     orders = (bits, bits[1:2] + bits[0:1] + bits[2:])
-    sums = halve(last_sums(final, total, rows, orders), orders)
+    sums = halve(*last_sums(final, total, rows, orders), orders)
     return sums[:, None, :]
 
 

time: 49.1 us -> 50.5 us (1.029)
  waiting for transfers between devices: 17.1 us -> 22.5 us
  starting transfers between devices: 20 us -> 16 us
    ppermute x16 -> x11, starting transfers between devices: 20 us -> 13.5 us  [swap_over(): return lambda value: lax.ppermute(value, axis, ring)]
    ppermute x0 -> x3, waiting for transfers between devices: none -> 2.75 us  [halve(): got = lax.ppermute(give, 'grp', ring)]
    ppermute x16 -> x11, waiting for transfers between devices: 17.1 us -> 19.8 us  [swap_over(): return lambda value: lax.ppermute(value, axis, ring)]
    ppermute x0 -> x3, starting transfers between devices: none -> 2.46 us  [halve(): got = lax.ppermute(give, 'grp', ring)]
  transfers between devices with their start and end apart: 16 -> 14, of which waited for: 9 -> 9; matrix products, arithmetic and copies ran while one was open for 0% -> 0% of each run, Pallas kernels for 5% -> 5%
where the time goes in v11:
time: 50.5 us; the launch traced here: 50.3 us
  waiting for transfers between devices  22.5 us (45%)
  starting transfers between devices  16 us (32%)
  Pallas kernels  9.23 us (18%)
  local copies, waits for them, and re-layouts  1.63 us (3%)
  other arithmetic  0.8 us (2%)
    ppermute x11, waiting for transfers between devices, swap_over(): return lambda value: lax.ppermute(value, axis, ring)  19.8 us
    ppermute x11, starting transfers between devices, swap_over(): return lambda value: lax.ppermute(value, axis, ring)  13.5 us
    pallas_call x1, Pallas kernels, soundings_partial(): call(functools.partial(fields_body, packed), (floats(tiles * TILE, LANES)...  4.55 us
    ppermute x3, waiting for transfers between devices, halve(): got = lax.ppermute(give, 'grp', ring)  2.75 us
    ppermute x3, starting transfers between devices, halve(): got = lax.ppermute(give, 'grp', ring)  2.46 us
    unnamed x12, local copies, waits for them, and re-layouts  1.62 us
  transfers between devices with their start and end apart: 14, of which 9 were waited for; matrix products, arithmetic and copies ran while one was open for 0% of the time, Pallas kernels for 5%

profile of v11, /device:TPU:0, one launch (start us, length us, event | category | flops | bytes accessed | tf_op | source)
XLA Modules:
  0.0 50.3 jit_solution(12205049947152090046)
XLA Ops:
  0.0 0.7 %pad_add_fusion.1 = s32[4,8]{1,0:T(4,128)S(1)} fusion(s32[2,8]{1,0:T(2,128)} %lengths_ref.1, s32[2,8]{1,0:T(2,128)} %refs_0_.1), kind=kLoop, calls=%fused_computation.9 | loop fusion | flops 32 | bytes 256 | tf_op jit(solution)/shard_map/concatenate | solution.py:464
  0.7 3.0 %collective-permute-start = (s32[4,8]{1,0:T(4,128)S(1)}, s32[4,8]{1,0:T(4,128)S(1)}, u32[]{:S(2)}, u32[]{:S(2)}) collective-permute-start(s32[4,8]{1,0:T(4,128)S(1)} %pad_add_fusion.1), channel_id=1, source_target_pairs={{0,1},{1,0},{2,3},{3,2},{4,5},{5,4},{6,7},{7,6},{8,9},{9,8},{10,11... | collective-permute-start | bytes 392 | tf_op jit(solution)/shard_map/ppermute | solution.py:61
  3.7 1.6 %copy-done = f32[4096,1,128]{2,1,0:T(1,128)S(1)} copy-done((f32[4096,1,128]{2,1,0:T(1,128)S(1)}, f32[4096,1,128]{2,1,0:T(1,128)}, u32[]{:S(2)}) %copy-start) | copy-done | bytes 2097176
  5.3 0.1 shard_map.64.block_ref.table_ref.refs_4_
  5.4 0.0 copy-start.3
  5.4 0.0 copy-start.1
  5.4 0.0 copy-start.2
  5.5 0.0 collective-permute-done.index_ref
  5.5 0.6 %shard_map.65 = f32[384,128]{1,0:T(8,128)S(1)} custom-call(s32[4,8]{1,0:T(4,128)S(1)} %collective-permute-done.index_ref, f32[4096,128]{1,0:T(8,128)S(1)} %shard_map.64.block_ref.table_ref.refs_4_), custom_call_target="tpu_custom_call" | custom-call | bytes 393216 | tf_op jit(solution)/shard_map/pallas_call | solution.py:106
  6.1 0.0 copy-start.4
  6.1 0.0 copy-start.5
  6.1 1.9 %collective-permute-start.1 = (f32[384,128]{1,0:T(8,128)S(1)}, f32[384,128]{1,0:T(8,128)S(1)}, u32[]{:S(2)}, u32[]{:S(2)}) collective-permute-start(f32[384,128]{1,0:T(8,128)S(1)} %shard_map.65), channel_id=1, source_target_pairs={{0,1},{1,0},{2,3},{3,2},{4,5},{5,4},{6,7},{7,6},{8,9},{9,8},{10,11... | collective-permute-start | bytes 589832 | tf_op jit(solution)/shard_map/ppermute | solution.py:61
  8.0 0.0 copy-done.3
  8.0 0.1 collective-permute-start.2
  8.0 0.0 copy-done.1
  8.1 0.0 copy-done.2
  8.1 0.9 %shard_map.66 = (f32[3,8,8,8,128]{4,3,2,1,0:T(8,128)S(1)}, f32[3,8,8,8,128]{4,3,2,1,0:T(8,128)S(1)}) custom-call(f32[1536,128]{1,0:T(8,128)S(1)} %bitcast.17, f32[1536,128]{1,0:T(8,128)S(1)} %bitcast.18), custom_call_target="tpu_custom_call" | custom-call | flops 1572864 | bytes 3145728 | tf_op jit(solution)/shard_map/pallas_call | solution.py:146
  9.0 0.2 collective-permute-done.2
  9.2 3.3 %collective-permute-done.1.answer_ref = f32[384,128]{1,0:T(8,128)S(1)} collective-permute-done((f32[384,128]{1,0:T(8,128)S(1)}, f32[384,128]{1,0:T(8,128)S(1)}, u32[]{:S(2)}, u32[]{:S(2)}) %collective-permute-start.1) | collective-permute-done | bytes 196640 | tf_op jit(solution)/shard_map/ppermute | solution.py:61
  12.5 0.0 copy-done.4
  12.5 0.0 copy-done.5
  12.5 4.6 %shard_map.67 = (f32[512,128]{1,0:T(8,128)S(1)}, f32[384,128]{1,0:T(8,128)S(1)}) custom-call(s32[2,8]{1,0:T(2,128)S(1)} %copy-done.3, s32[2,8]{1,0:T(2,128)S(1)} %bitcast.21, s32[2,8]{1,0:T(2,128)S(1)} %copy-done.4, f32[4096,128]{1,0:T(8,128)S(1)} %shard_map.64.block_ref.table_ref.refs_4_, f32[384,128]{1,0:T(8,128)S(1)} %collective-permute-done.1.answer_ref, ...), custom_call_target="tpu_custom_call" | custom-call | flops 32768000 | bytes 2621440 | tf_op jit(solution)/shard_map/pallas_call | solution.py:283
  17.1 1.2 %collective-permute-start.3 = (f32[384,128]{1,0:T(8,128)S(1)}, f32[384,128]{1,0:T(8,128)S(1)}, u32[]{:S(2)}, u32[]{:S(2)}) collective-permute-start(f32[384,128]{1,0:T(8,128)S(1)} %get-tuple-element.27), channel_id=1, source_target_pairs={{0,1},{1,0},{2,3},{3,2},{4,5},{5,4},{6,7},{7,6},{8,9},{9,8},{10,11... | collective-permute-start | bytes 589832 | tf_op jit(solution)/shard_map/ppermute | solution.py:61
  18.3 0.0 collective-permute-start.5
  18.3 4.6 %collective-permute-done.3.terms_ref = f32[384,128]{1,0:T(8,128)S(1)} collective-permute-done((f32[384,128]{1,0:T(8,128)S(1)}, f32[384,128]{1,0:T(8,128)S(1)}, u32[]{:S(2)}, u32[]{:S(2)}) %collective-permute-start.3) | collective-permute-done | bytes 196640 | tf_op jit(solution)/shard_map/ppermute | solution.py:61
  22.8 0.0 collective-permute-start.4
  22.8 0.0 collective-permute-done.5.refs_3_
  22.8 0.9 %shard_map.68.given_total = f32[2592,128]{1,0:T(8,128)S(1)} custom-call(s32[2,8]{1,0:T(2,128)S(1)} %copy-done.3, f32[16,32,128]{2,1,0:T(8,128)S(1)} %bitcast.20, s32[2,8]{1,0:T(2,128)S(1)} %slice.55.refs_2_, f32[16,32,128]{2,1,0:T(8,128)S(1)} %collective-permute-done.5.refs_3_, f32[4096,128]{1,0:T(8,128)S(1)} %shard_map.64.block_ref.table_ref.refs_4_), custom_call_target="tpu_custom_call" | custom-call | flops 331776 | bytes 2654208 | tf_op jit(solution)/shard_map/pallas_call | solution.py:343
  23.7 0.7 %shard_map.69.refs_2_ = f32[2592,128]{1,0:T(8,128)S(1)} custom-call(s32[4,8]{1,0:T(4,128)S(1)} %collective-permute-done.index_ref, f32[384,128]{1,0:T(8,128)S(1)} %collective-permute-done.3.terms_ref, f32[2592,128]{1,0:T(8,128)S(1)} %shard_map.68.given_total), custom_call_target="tpu_custom_call", output_to_operand_aliasing={{}: (2, {})} | custom-call | flops 331776 | bytes 2654208 | tf_op jit(solution)/shard_map/pallas_call | solution.py:355
  24.4 0.0 collective-permute-done.4.refs_1_
  24.4 0.7 %shard_map.70 = (f32[2592,128]{1,0:T(8,128)S(1)}, f32[4,128,128]{2,1,0:T(8,128)S(1)}, f32[4,128,128]{2,1,0:T(8,128)S(1)}, f32[4,64,128]{2,1,0:T(8,128)S(1)}, f32...) custom-call(s32[4,8]{1,0:T(4,128)S(1)} %slice.54.refs_0_, ...), custom_call_target="tpu_custom_call", output_to_operand_aliasing={{0}: (2, {})} | custom-call | flops 331776 | bytes 2654208 | tf_op jit(solution)/shard_map/pallas_call | solution.py:389
  25.2 1.6 %collective-permute-start.11 = (f32[4,64,128]{2,1,0:T(8,128)S(1)}, f32[4,64,128]{2,1,0:T(8,128)S(1)}, u32[]{:S(2)}, u32[]{:S(2)}) collective-permute-start(f32[4,64,128]{2,1,0:T(8,128)S(1)} %get-tuple-element.33), channel_id=1, source_target_pairs={{0,8},{2,10},{4,12},{6,14},{8,0},{10,2},{12,4},{14,6},{16,24},{18,... | collective-permute-start | bytes 393224 | tf_op jit(solution)/shard_map/ppermute | solution.py:61
  26.8 1.5 %collective-permute-start.6 = (f32[4,128,128]{2,1,0:T(8,128)S(1)}, f32[4,128,128]{2,1,0:T(8,128)S(1)}, u32[]{:S(2)}, u32[]{:S(2)}) collective-permute-start(f32[4,128,128]{2,1,0:T(8,128)S(1)} %get-tuple-element.29), channel_id=1, source_target_pairs={{0,4},{2,10},{4,0},{6,14},{8,12},{10,2},{12,8},{14,6},{16,20},{18,... | collective-permute-start | bytes 786440 | tf_op jit(solution)/shard_map/ppermute | solution.py:425
  28.3 0.5 %collective-permute-start.9 = (f32[4,64,128]{2,1,0:T(8,128)S(1)}, f32[4,64,128]{2,1,0:T(8,128)S(1)}, u32[]{:S(2)}, u32[]{:S(2)}) collective-permute-start(f32[4,64,128]{2,1,0:T(8,128)S(1)} %get-tuple-element.31), channel_id=1, source_target_pairs={{0,4},{2,6},{4,0},{6,2},{8,12},{10,14},{12,8},{14,10},{16,20},{18,... | collective-permute-start | bytes 393224 | tf_op jit(solution)/shard_map/ppermute | solution.py:61
  28.8 2.8 %collective-permute-done.11 = f32[4,64,128]{2,1,0:T(8,128)S(1)} collective-permute-done((f32[4,64,128]{2,1,0:T(8,128)S(1)}, f32[4,64,128]{2,1,0:T(8,128)S(1)}, u32[]{:S(2)}, u32[]{:S(2)}) %collective-permute-start.11) | collective-permute-done | bytes 131104 | tf_op jit(solution)/shard_map/ppermute | solution.py:61
  31.6 1.6 %collective-permute-start.12 = (f32[2,64,128]{2,1,0:T(8,128)S(1)}, f32[2,64,128]{2,1,0:T(8,128)S(1)}, u32[]{:S(2)}, u32[]{:S(2)}) collective-permute-start(f32[2,64,128]{2,1,0:T(8,128)S(1)} %get-tuple-element.40), channel_id=1, source_target_pairs={{0,4},{2,6},{4,0},{6,2},{8,12},{10,14},{12,8},{14,10},{16,20},{18,... | collective-permute-start | bytes 196616 | tf_op jit(solution)/shard_map/ppermute | solution.py:61
  33.2 1.3 %collective-permute-done.6 = f32[4,128,128]{2,1,0:T(8,128)S(1)} collective-permute-done((f32[4,128,128]{2,1,0:T(8,128)S(1)}, f32[4,128,128]{2,1,0:T(8,128)S(1)}, u32[]{:S(2)}, u32[]{:S(2)}) %collective-permute-start.6) | collective-permute-done | bytes 262176 | tf_op jit(solution)/shard_map/ppermute | solution.py:425
  34.6 0.5 %collective-permute-start.7 = (f32[2,128,128]{2,1,0:T(8,128)S(1)}, f32[2,128,128]{2,1,0:T(8,128)S(1)}, u32[]{:S(2)}, u32[]{:S(2)}) collective-permute-start(f32[2,128,128]{2,1,0:T(8,128)S(1)} %get-tuple-element.37), channel_id=1, source_target_pairs={{0,8},{2,6},{4,12},{6,2},{8,0},{10,14},{12,4},{14,10},{16,24},{18,... | collective-permute-start | bytes 393224 | tf_op jit(solution)/shard_map/ppermute | solution.py:425
  35.2 1.0 %collective-permute-done.9 = f32[4,64,128]{2,1,0:T(8,128)S(1)} collective-permute-done((f32[4,64,128]{2,1,0:T(8,128)S(1)}, f32[4,64,128]{2,1,0:T(8,128)S(1)}, u32[]{:S(2)}, u32[]{:S(2)}) %collective-permute-start.9) | collective-permute-done | bytes 131104 | tf_op jit(solution)/shard_map/ppermute | solution.py:61
  36.1 1.1 %collective-permute-start.10 = (f32[2,64,128]{2,1,0:T(8,128)S(1)}, f32[2,64,128]{2,1,0:T(8,128)S(1)}, u32[]{:S(2)}, u32[]{:S(2)}) collective-permute-start(f32[2,64,128]{2,1,0:T(8,128)S(1)} %get-tuple-element.42), channel_id=1, source_target_pairs={{0,8},{2,10},{4,12},{6,14},{8,0},{10,2},{12,4},{14,6},{16,24},{18,... | collective-permute-start | bytes 196616 | tf_op jit(solution)/shard_map/ppermute | solution.py:61
  37.2 0.0 collective-permute-done.12.got_high
  37.2 3.7 %collective-permute-done.10.got_low = f32[2,64,128]{2,1,0:T(8,128)S(1)} collective-permute-done((f32[2,64,128]{2,1,0:T(8,128)S(1)}, f32[2,64,128]{2,1,0:T(8,128)S(1)}, u32[]{:S(2)}, u32[]{:S(2)}) %collective-permute-start.10) | collective-permute-done | bytes 65568 | tf_op jit(solution)/shard_map/ppermute | solution.py:61
  40.9 2.7 %collective-permute-start.13 = (f32[1,128,128]{2,1,0:T(8,128)S(1)}, f32[1,128,128]{2,1,0:T(8,128)S(1)}, u32[]{:S(2)}, u32[]{:S(2)}) collective-permute-start(f32[1,128,128]{2,1,0:T(8,128)S(1)} %get-tuple-element.35), channel_id=1, source_target_pairs={{0,16},{2,18},{4,20},{6,22},{8,24},{10,26},{12,28},{14,30},{16,0},... | collective-permute-start | bytes 196616 | tf_op jit(solution)/shard_map/ppermute | solution.py:61
  43.6 0.0 collective-permute-done.7
  43.6 0.4 collective-permute-start.8
  44.0 4.3 %collective-permute-done.13.refs_2_ = f32[1,128,128]{2,1,0:T(8,128)S(1)} collective-permute-done((f32[1,128,128]{2,1,0:T(8,128)S(1)}, f32[1,128,128]{2,1,0:T(8,128)S(1)}, u32[]{:S(2)}, u32[]{:S(2)}) %collective-permute-start.13) | collective-permute-done | bytes 65568 | tf_op jit(solution)/shard_map/ppermute | solution.py:61
  48.3 1.4 %collective-permute-done.8.refs_0_ = f32[1,128,128]{2,1,0:T(8,128)S(1)} collective-permute-done((f32[1,128,128]{2,1,0:T(8,128)S(1)}, f32[1,128,128]{2,1,0:T(8,128)S(1)}, u32[]{:S(2)}, u32[]{:S(2)}) %collective-permute-start.8) | collective-permute-done | bytes 65568 | tf_op jit(solution)/shard_map/ppermute | solution.py:425
  49.7 0.7 %shard_map.72 = f32[256,128]{1,0:T(8,128)} custom-call(f32[1,128,128]{2,1,0:T(8,128)S(1)} %collective-permute-done.8.refs_0_, f32[1,128,128]{2,1,0:T(8,128)S(1)} %get-tuple-element.43.refs_1_, f32[1,128,128]{2,1,0:T(8,128)S(1)} %collective-permute-done.13.refs_2_, f32[1,128,128]{2,1,0:T(8,128)S(1)} %get-tuple-element.36.refs_3_), custom_call_target="tpu_custom_call" | custom-call | flops 32768 | bytes 393216 | tf_op jit(solution)/shard_map/pallas_call | solution.py:441
  (9 shorter events, 0.1 us)
Async XLA Ops:
  0.7 4.8 %collective-permute-start = (s32[4,8]{1,0:T(4,128)S(1)}, s32[4,8]{1,0:T(4,128)S(1)}, u32[]{:S(2)}, u32[]{:S(2)}) collective-permute-start(s32[4,8]{1,0:T(4,128)S(1)} %pad_add_fusion.1), channel_id=1, source_target_pairs={{0,1},{1,0},{2,3},{3,2},{4,5},{5,4},{6,7},{7,6},{8,9},{9,8},{10,11... | collective-permute-start | bytes 392 | tf_op jit(solution)/shard_map/ppermute | solution.py:61
  3.7 1.6 %copy-start = (f32[4096,1,128]{2,1,0:T(1,128)S(1)}, f32[4096,1,128]{2,1,0:T(1,128)}, u32[]{:S(2)}) copy-start(f32[4096,1,128]{2,1,0:T(1,128)} %param.6) | copy-start | bytes 6291460
  5.4 2.5 %copy-start.3 = (s32[2,8]{1,0:T(2,128)S(1)}, s32[2,8]{1,0:T(2,128)}, u32[]{:S(2)}) copy-start(s32[2,8]{1,0:T(2,128)} %refs_0_.1) | copy-start | bytes 196
  5.4 2.6 %copy-start.1 = (f32[2,3,8,4096]{3,2,1,0:T(8,128)S(1)}, f32[2,3,8,4096]{3,2,1,0:T(8,128)}, u32[]{:S(2)}) copy-start(f32[2,3,8,4096]{3,2,1,0:T(8,128)} %param.7) | copy-start | bytes 2359300
  5.4 2.6 %copy-start.2 = (f32[2,3,8,4096]{3,2,1,0:T(8,128)S(1)}, f32[2,3,8,4096]{3,2,1,0:T(8,128)}, u32[]{:S(2)}) copy-start(f32[2,3,8,4096]{3,2,1,0:T(8,128)} %param.8) | copy-start | bytes 2359300
  6.1 6.5 %copy-start.4 = (s32[2,8]{1,0:T(2,128)S(1)}, s32[2,8]{1,0:T(2,128)}, u32[]{:S(2)}) copy-start(s32[2,8]{1,0:T(2,128)} %lengths_ref.1) | copy-start | bytes 196
  6.1 6.4 %copy-start.5 = (s32[2,8,1]{1,2,0:T(1,128)S(1)}, s32[2,8,1]{1,2,0:T(1,128)}, u32[]{:S(2)}) copy-start(s32[2,8,1]{1,2,0:T(1,128)} %param.9) | copy-start | bytes 196
  6.1 6.4 %collective-permute-start.1 = (f32[384,128]{1,0:T(8,128)S(1)}, f32[384,128]{1,0:T(8,128)S(1)}, u32[]{:S(2)}, u32[]{:S(2)}) collective-permute-start(f32[384,128]{1,0:T(8,128)S(1)} %shard_map.65), channel_id=1, source_target_pairs={{0,1},{1,0},{2,3},{3,2},{4,5},{5,4},{6,7},{7,6},{8,9},{9,8},{10,11... | collective-permute-start | bytes 589832 | tf_op jit(solution)/shard_map/ppermute | solution.py:61
  8.0 1.2 %collective-permute-start.2 = (s32[6,8]{1,0:T(8,128)S(1)}, s32[6,8]{1,0:T(8,128)S(1)}, u32[]{:S(2)}, u32[]{:S(2)}) collective-permute-start(s32[6,8]{1,0:T(8,128)S(1)} %pad_add_fusion), channel_id=1, source_target_pairs={{0,2},{2,0},{4,6},{6,4},{8,10},{10,8},{12,14},{14,12},{16,18},{18,... | collective-permute-start | bytes 584 | tf_op jit(solution)/shard_map/ppermute | solution.py:61
  17.1 5.7 %collective-permute-start.3 = (f32[384,128]{1,0:T(8,128)S(1)}, f32[384,128]{1,0:T(8,128)S(1)}, u32[]{:S(2)}, u32[]{:S(2)}) collective-permute-start(f32[384,128]{1,0:T(8,128)S(1)} %get-tuple-element.27), channel_id=1, source_target_pairs={{0,1},{1,0},{2,3},{3,2},{4,5},{5,4},{6,7},{7,6},{8,9},{9,8},{10,11... | collective-permute-start | bytes 589832 | tf_op jit(solution)/shard_map/ppermute | solution.py:61
  18.3 4.6 %collective-permute-start.5 = (f32[16,32,128]{2,1,0:T(8,128)S(1)}, f32[16,32,128]{2,1,0:T(8,128)S(1)}, u32[]{:S(2)}, u32[]{:S(2)}) collective-permute-start(f32[16,32,128]{2,1,0:T(8,128)S(1)} %bitcast.19), channel_id=1, source_target_pairs={{0,2},{2,0},{4,6},{6,4},{8,10},{10,8},{12,14},{14,12},{16,18},{18,... | collective-permute-start | bytes 786440 | tf_op jit(solution)/shard_map/ppermute | solution.py:61
  22.8 1.6 %collective-permute-start.4 = (f32[384,128]{1,0:T(8,128)S(1)}, f32[384,128]{1,0:T(8,128)S(1)}, u32[]{:S(2)}, u32[]{:S(2)}) collective-permute-start(f32[384,128]{1,0:T(8,128)S(1)} %collective-permute-done.3.terms_ref), channel_id=1, source_target_pairs={{0,2},{2,0},{4,6},{6,4},{8,10},{10,8},{12,14},{14,12},{16,18},{18,... | collective-permute-start | bytes 589832 | tf_op jit(solution)/shard_map/ppermute | solution.py:61
  25.2 6.4 %collective-permute-start.11 = (f32[4,64,128]{2,1,0:T(8,128)S(1)}, f32[4,64,128]{2,1,0:T(8,128)S(1)}, u32[]{:S(2)}, u32[]{:S(2)}) collective-permute-start(f32[4,64,128]{2,1,0:T(8,128)S(1)} %get-tuple-element.33), channel_id=1, source_target_pairs={{0,8},{2,10},{4,12},{6,14},{8,0},{10,2},{12,4},{14,6},{16,24},{18,... | collective-permute-start | bytes 393224 | tf_op jit(solution)/shard_map/ppermute | solution.py:61
  26.8 7.7 %collective-permute-start.6 = (f32[4,128,128]{2,1,0:T(8,128)S(1)}, f32[4,128,128]{2,1,0:T(8,128)S(1)}, u32[]{:S(2)}, u32[]{:S(2)}) collective-permute-start(f32[4,128,128]{2,1,0:T(8,128)S(1)} %get-tuple-element.29), channel_id=1, source_target_pairs={{0,4},{2,10},{4,0},{6,14},{8,12},{10,2},{12,8},{14,6},{16,20},{18,... | collective-permute-start | bytes 786440 | tf_op jit(solution)/shard_map/ppermute | solution.py:425
  28.3 7.8 %collective-permute-start.9 = (f32[4,64,128]{2,1,0:T(8,128)S(1)}, f32[4,64,128]{2,1,0:T(8,128)S(1)}, u32[]{:S(2)}, u32[]{:S(2)}) collective-permute-start(f32[4,64,128]{2,1,0:T(8,128)S(1)} %get-tuple-element.31), channel_id=1, source_target_pairs={{0,4},{2,6},{4,0},{6,2},{8,12},{10,14},{12,8},{14,10},{16,20},{18,... | collective-permute-start | bytes 393224 | tf_op jit(solution)/shard_map/ppermute | solution.py:61
  31.6 5.6 %collective-permute-start.12 = (f32[2,64,128]{2,1,0:T(8,128)S(1)}, f32[2,64,128]{2,1,0:T(8,128)S(1)}, u32[]{:S(2)}, u32[]{:S(2)}) collective-permute-start(f32[2,64,128]{2,1,0:T(8,128)S(1)} %get-tuple-element.40), channel_id=1, source_target_pairs={{0,4},{2,6},{4,0},{6,2},{8,12},{10,14},{12,8},{14,10},{16,20},{18,... | collective-permute-start | bytes 196616 | tf_op jit(solution)/shard_map/ppermute | solution.py:61
  34.6 9.0 %collective-permute-start.7 = (f32[2,128,128]{2,1,0:T(8,128)S(1)}, f32[2,128,128]{2,1,0:T(8,128)S(1)}, u32[]{:S(2)}, u32[]{:S(2)}) collective-permute-start(f32[2,128,128]{2,1,0:T(8,128)S(1)} %get-tuple-element.37), channel_id=1, source_target_pairs={{0,8},{2,6},{4,12},{6,2},{8,0},{10,14},{12,4},{14,10},{16,24},{18,... | collective-permute-start | bytes 393224 | tf_op jit(solution)/shard_map/ppermute | solution.py:425
  36.1 4.8 %collective-permute-start.10 = (f32[2,64,128]{2,1,0:T(8,128)S(1)}, f32[2,64,128]{2,1,0:T(8,128)S(1)}, u32[]{:S(2)}, u32[]{:S(2)}) collective-permute-start(f32[2,64,128]{2,1,0:T(8,128)S(1)} %get-tuple-element.42), channel_id=1, source_target_pairs={{0,8},{2,10},{4,12},{6,14},{8,0},{10,2},{12,4},{14,6},{16,24},{18,... | collective-permute-start | bytes 196616 | tf_op jit(solution)/shard_map/ppermute | solution.py:61
  40.9 7.3 %collective-permute-start.13 = (f32[1,128,128]{2,1,0:T(8,128)S(1)}, f32[1,128,128]{2,1,0:T(8,128)S(1)}, u32[]{:S(2)}, u32[]{:S(2)}) collective-permute-start(f32[1,128,128]{2,1,0:T(8,128)S(1)} %get-tuple-element.35), channel_id=1, source_target_pairs={{0,16},{2,18},{4,20},{6,22},{8,24},{10,26},{12,28},{14,30},{16,0},... | collective-permute-start | bytes 196616 | tf_op jit(solution)/shard_map/ppermute | solution.py:61
  43.6 6.1 %collective-permute-start.8 = (f32[1,128,128]{2,1,0:T(8,128)S(1)}, f32[1,128,128]{2,1,0:T(8,128)S(1)}, u32[]{:S(2)}, u32[]{:S(2)}) collective-permute-start(f32[1,128,128]{2,1,0:T(8,128)S(1)} %get-tuple-element.44), channel_id=1, source_target_pairs={{0,16},{2,18},{4,20},{6,22},{8,24},{10,26},{12,28},{14,30},{16,0},... | collective-permute-start | bytes 196616 | tf_op jit(solution)/shard_map/ppermute | solution.py:425
